TPU v7x, 32 devices: a whole 2x2x4 slice. The times are simulated.
32 devices in a mesh: gx: 4 (over z), gy: 2 (over core), gz: 4 (over y, x).
Axes of the slice: x: 2, y: 2, z: 4, core: 2. Of those that a mesh axis runs over, the one named last changes fastest.
Arguments:
- flow_pops: float32 [19, 16, 16, 512], P(None, 'gx', 'gy', 'gz'), may hold values from 0.3 to 0.8
- phase_pops: float32 [7, 16, 16, 512], P(None, 'gx', 'gy', 'gz'), may hold values from -0.15 to 0.15
- pore_mask: int32 [16, 16, 512], P('gx', 'gy', 'gz'), may hold values from 0 to 1, as said below
Outputs:
- flow_next: float32 [19, 16, 16, 512], P(None, 'gx', 'gy', 'gz')
- phase_next: float32 [7, 16, 16, 512], P(None, 'gx', 'gy', 'gz')
Inputs may be any that keep to these rules, and one draw needn't show every extreme that they name: `pore_mask`: 1 marks a pore voxel, 0 a rock voxel. Pores and rock form clusters several voxels wide, and whole aligned blocks of 4 x 8 x 128 voxels may be rock.
All inputs are finite; a program needn't handle non-finite values.
Results may differ from a plain program's by a relative error of at most 0.0003.
Values sent between devices are 32-bit elements; how exact they have to be, the bound alone decides.
No kernel may reach another device: no remote copies, remote signals or barrier semaphores. Data moves between devices by JAX's collectives and lax.ppermute only.
A program may use at most 64 MiB of HBM per device.

v0:
```python
import jax
import jax.numpy as jnp
from jax import lax
from jax.sharding import PartitionSpec as P

STEPS = 2


VEL_F = [
    (0, 0, 0),
    (1, 0, 0),
    (-1, 0, 0),
    (0, 1, 0),
    (0, -1, 0),
    (0, 0, 1),
    (0, 0, -1),
    (1, 1, 0),
    (-1, -1, 0),
    (1, -1, 0),
    (-1, 1, 0),
    (1, 0, 1),
    (-1, 0, -1),
    (1, 0, -1),
    (-1, 0, 1),
    (0, 1, 1),
    (0, -1, -1),
    (0, 1, -1),
    (0, -1, 1),
]
OPP_F = [0, 2, 1, 4, 3, 6, 5, 8, 7, 10, 9, 12, 11, 14, 13, 16, 15, 18, 17]
WT_F = [1.0 / 3.0] + [1.0 / 18.0] * 6 + [1.0 / 36.0] * 12
BT_F = [-2.0 / 9.0] + [1.0 / 54.0] * 6 + [1.0 / 27.0] * 12
WT_G = [0.25] + [0.125] * 6
VEL_ALL = VEL_F + VEL_F[:7]
OPP_ALL = OPP_F + [19 + other for other in OPP_F[:7]]


def with_halo(cells, sides, width):
    for axis, dim in sides:
        count = lax.axis_size(axis)
        ends = count - 1
        head = lax.slice_in_dim(cells, 0, width, axis=dim)
        tail = lax.slice_in_dim(cells, cells.shape[dim] - width, cells.shape[dim], axis=dim)
        cells = jnp.concatenate(
            [
                lax.ppermute(tail, axis, [(i, (i + 1) % count) for i in range(ends)]),
                cells,
                lax.ppermute(head, axis, [((i + 1) % count, i) for i in range(ends)]),
            ],
            axis=dim,
        )
    return cells


def relax(flow_pops, phase_pops, phase, grads, fluid):
    density = sum((flow_pops[member] for member in range(19)))
    flow = [
        sum((VEL_F[member][dim] * flow_pops[member] for member in range(19))) / density
        for dim in range(3)
    ]
    speed_sq = flow[0] * flow[0] + flow[1] * flow[1] + flow[2] * flow[2]
    omega = 1.0 / (0.8 + 0.2 * phase)
    grad_mag = jnp.sqrt(grads[0] * grads[0] + grads[1] * grads[1] + grads[2] * grads[2] + 0.01)
    results = []
    for member in range(19):
        offset = VEL_F[member]
        along = offset[0] * flow[0] + offset[1] * flow[1] + offset[2] * flow[2]
        cross = offset[0] * grads[0] + offset[1] * grads[1] + offset[2] * grads[2]
        balance = (
            WT_F[member] * density * (1.0 + 3.0 * along + 4.5 * along * along - 1.5 * speed_sq)
        )
        perturb = 0.5 * (WT_F[member] * cross * cross / grad_mag - BT_F[member] * grad_mag)
        relaxed = flow_pops[member] - omega * (flow_pops[member] - balance) + perturb
        results.append(jnp.where(fluid, relaxed, flow_pops[member]))
    sharpen_coef = 0.7 * (1.0 - phase * phase) / grad_mag
    for member in range(7):
        offset = VEL_F[member]
        along = offset[0] * flow[0] + offset[1] * flow[1] + offset[2] * flow[2]
        cross = offset[0] * grads[0] + offset[1] * grads[1] + offset[2] * grads[2]
        balance = WT_G[member] * (phase * (1.0 + 4.0 * along) + sharpen_coef * cross)
        relaxed = phase_pops[member] - 1.25 * (phase_pops[member] - balance)
        results.append(jnp.where(fluid, relaxed, phase_pops[member]))
    return jnp.stack(results)


def window(field, flags, offset, sizes):
    starts = [1 - offset[dim] if flags[dim] else 0 for dim in range(3)]
    return field[
        starts[0] : starts[0] + sizes[0],
        starts[1] : starts[1] + sizes[1],
        starts[2] : starts[2] + sizes[2],
    ]


def propagate(post, source, fluid_pad, fluid):
    sizes = post.shape[1:]
    results = []
    for member in range(26):
        offset = VEL_ALL[member]
        field, flags = source(member)
        source_vals = window(field, flags, offset, sizes)
        source_fluid = window(fluid_pad, (1, 1, 1), offset, sizes) == 1
        moved = jnp.where(source_fluid, source_vals, post[OPP_ALL[member]])
        results.append(jnp.where(fluid, moved, post[member]))
    return jnp.stack(results)


def gradient(padded):
    grad_x = 0.5 * (padded[2:, 1:-1, 1:-1] - padded[:-2, 1:-1, 1:-1])
    grad_y = 0.5 * (padded[1:-1, 2:, 1:-1] - padded[1:-1, :-2, 1:-1])
    grad_z = 0.5 * (padded[1:-1, 1:-1, 2:] - padded[1:-1, 1:-1, :-2])
    return (grad_x, grad_y, grad_z)


def movers(dim, sign):
    return [member for member in range(26) if VEL_ALL[member][dim] == sign]


def pack_layers(bases, dim, plus, minus):
    lower = jnp.stack([lax.index_in_dim(bases[member], 0, dim, keepdims=False) for member in minus])
    upper = jnp.stack(
        [
            lax.index_in_dim(bases[member], bases[member].shape[dim] - 1, dim, keepdims=False)
            for member in plus
        ]
    )
    return jnp.stack([lower, upper], axis=dim + 1)


def unpack_layers(bases, got, dim, plus, minus):
    result = {}
    for slot, member in enumerate(plus):
        rim = lax.index_in_dim(got[slot], 0, dim, keepdims=True)
        result[member] = jnp.concatenate([rim, bases[member], jnp.zeros_like(rim)], axis=dim)
    for slot, member in enumerate(minus):
        rim = lax.index_in_dim(got[slot], 3, dim, keepdims=True)
        result[member] = jnp.concatenate([jnp.zeros_like(rim), bases[member], rim], axis=dim)
    return result


def outward_sources(post):
    plus_x, minus_x = (movers(0, 1), movers(0, -1))
    bases_x = {member: post[member] for member in plus_x + minus_x}
    got_x = with_halo(pack_layers(bases_x, 0, plus_x, minus_x), (("gx", 1),), 1)
    ext_x = unpack_layers(bases_x, got_x, 0, plus_x, minus_x)

    def widen_x(member):
        if VEL_ALL[member][0] != 0:
            return ext_x[member]
        return jnp.pad(post[member], ((1, 1), (0, 0), (0, 0)))

    plus_y, minus_y = (movers(1, 1), movers(1, -1))
    bases_y = {member: widen_x(member) for member in plus_y + minus_y}
    got_y = with_halo(pack_layers(bases_y, 1, plus_y, minus_y), (("gy", 2),), 1)
    ext_y = unpack_layers(bases_y, got_y, 1, plus_y, minus_y)

    def widen_y(member):
        if VEL_ALL[member][1] != 0:
            return ext_y[member]
        return jnp.pad(widen_x(member), ((0, 0), (1, 1), (0, 0)))

    plus_z, minus_z = (movers(2, 1), movers(2, -1))
    bases_z = {member: widen_y(member) for member in plus_z + minus_z}
    got_z = with_halo(pack_layers(bases_z, 2, plus_z, minus_z), (("gz", 3),), 1)
    ext_z = unpack_layers(bases_z, got_z, 2, plus_z, minus_z)

    def source(member):
        offset = VEL_ALL[member]
        if offset[2] != 0:
            return (ext_z[member], (1, 1, 1))
        if offset[1] != 0:
            return (ext_y[member], (1, 1, 0))
        if offset[0] != 0:
            return (ext_x[member], (1, 0, 0))
        return (post[member], (0, 0, 0))

    return source


def shards(flow_pops, phase_pops, pore_mask):
    fluid_pad = with_halo(pore_mask, (("gx", 0), ("gy", 1), ("gz", 2)), 1)
    fluid = pore_mask == 1
    for step in range(STEPS):
        phase = jnp.sum(phase_pops, axis=0)
        masked = jnp.where(fluid, phase, jnp.float32(0.0))
        padded = with_halo(masked, (("gx", 0), ("gy", 1), ("gz", 2)), 1)
        post = relax(flow_pops, phase_pops, phase, gradient(padded), fluid)
        source = outward_sources(post)
        moved = propagate(post, source, fluid_pad, fluid)
        flow_pops = moved[:19]
        phase_pops = moved[19:]
    return (flow_pops, phase_pops)


def solution(mesh):
    placed = (P(None, "gx", "gy", "gz"), P(None, "gx", "gy", "gz"), P("gx", "gy", "gz"))
    return jax.shard_map(
        shards,
        mesh=mesh,
        in_specs=placed,
        out_specs=(P(None, "gx", "gy", "gz"), P(None, "gx", "gy", "gz")),
        check_vma=False,
    )
```

profile of v0, /device:TPU:18, one launch (start us, length us, event | category | flops | bytes accessed | tf_op | source)
XLA Modules:
  0.0 118.0 jit_solution(4021139065923795617)
XLA Ops:
  0.6 0.9 reduce_sum.31
  1.6 2.5 %collective-permute-start = (f32[1,8,128]{2,1,0:T(8,128)S(1)}, f32[1,8,128]{2,1,0:T(8,128)S(1)}, u32[]{:S(2)}, u32[]{:S(2)}) collective-permute-start(f32[1,8,128]{2,1,0:T(8,128)S(1)} %get-tuple-element.300), channel_id=1, source_target_pairs={{8,0},{16,8},{24,16},{9,1},{17,9},{25,17},{10,2},{18,10},{26,18},{... | collective-permute-start | bytes 12296 | tf_op jit(solution)/shard_map/ppermute | solution.py:48
  4.1 3.5 %collective-permute-start.1 = (f32[1,8,128]{2,1,0:T(8,128)S(1)}, f32[1,8,128]{2,1,0:T(8,128)S(1)}, u32[]{:S(2)}, u32[]{:S(2)}) collective-permute-start(f32[1,8,128]{2,1,0:T(8,128)S(1)} %get-tuple-element.299), channel_id=1, source_target_pairs={{0,8},{8,16},{16,24},{1,9},{9,17},{17,25},{2,10},{10,18},{18,26},{... | collective-permute-start | bytes 12296 | tf_op jit(solution)/shard_map/ppermute | solution.py:46
  7.6 1.9 %collective-permute-start.6 = (s32[1,8,128]{2,1,0:T(8,128)S(1)}, s32[1,8,128]{2,1,0:T(8,128)S(1)}, u32[]{:S(2)}, u32[]{:S(2)}) collective-permute-start(s32[1,8,128]{2,1,0:T(8,128)S(1)} %get-tuple-element.298), channel_id=1, source_target_pairs={{0,8},{8,16},{16,24},{1,9},{9,17},{17,25},{2,10},{10,18},{18,26},{... | collective-permute-start | bytes 12296 | tf_op jit(solution)/shard_map/ppermute | solution.py:46
  9.5 3.9 %collective-permute-start.8 = (s32[1,8,128]{2,1,0:T(8,128)S(1)}, s32[1,8,128]{2,1,0:T(8,128)S(1)}, u32[]{:S(2)}, u32[]{:S(2)}) collective-permute-start(s32[1,8,128]{2,1,0:T(8,128)S(1)} %get-tuple-element.297), channel_id=1, source_target_pairs={{8,0},{16,8},{24,16},{9,1},{17,9},{25,17},{10,2},{18,10},{26,18},{... | collective-permute-start | bytes 12296 | tf_op jit(solution)/shard_map/ppermute | solution.py:48
  13.5 0.8 slice_bitcast_fusion.4
  14.3 1.3 %collective-permute-start.2 = (f32[6,1,128]{2,1,0:T(1,128)S(1)}, f32[6,1,128]{2,1,0:T(1,128)S(1)}, u32[]{:S(2)}, u32[]{:S(2)}) collective-permute-start(f32[6,1,128]{2,1,0:T(1,128)S(1)} %get-tuple-element.284), channel_id=1, source_target_pairs={{4,0},{5,1},{6,2},{7,3},{12,8},{13,9},{14,10},{15,11},{20,16},{21,... | collective-permute-start | bytes 9224 | tf_op jit(solution)/shard_map/ppermute | solution.py:48
  15.6 3.2 %collective-permute-start.3 = (f32[6,1,128]{2,1,0:T(1,128)S(1)}, f32[6,1,128]{2,1,0:T(1,128)S(1)}, u32[]{:S(2)}, u32[]{:S(2)}) collective-permute-start(f32[6,1,128]{2,1,0:T(1,128)S(1)} %get-tuple-element.283), channel_id=1, source_target_pairs={{0,4},{1,5},{2,6},{3,7},{8,12},{9,13},{10,14},{11,15},{16,20},{17,... | collective-permute-start | bytes 9224 | tf_op jit(solution)/shard_map/ppermute | solution.py:46
  18.8 1.3 %collective-permute-start.10 = (s32[6,1,128]{2,1,0:T(1,128)S(1)}, s32[6,1,128]{2,1,0:T(1,128)S(1)}, u32[]{:S(2)}, u32[]{:S(2)}) collective-permute-start(s32[6,1,128]{2,1,0:T(1,128)S(1)} %get-tuple-element.269), channel_id=1, source_target_pairs={{0,4},{1,5},{2,6},{3,7},{8,12},{9,13},{10,14},{11,15},{16,20},{17,... | collective-permute-start | bytes 9224 | tf_op jit(solution)/shard_map/ppermute | solution.py:46
  20.1 1.3 %collective-permute-start.13 = (s32[6,1,128]{2,1,0:T(1,128)S(1)}, s32[6,1,128]{2,1,0:T(1,128)S(1)}, u32[]{:S(2)}, u32[]{:S(2)}) collective-permute-start(s32[6,1,128]{2,1,0:T(1,128)S(1)} %get-tuple-element.270), channel_id=1, source_target_pairs={{4,0},{5,1},{6,2},{7,3},{12,8},{13,9},{14,10},{15,11},{20,16},{21,... | collective-permute-start | bytes 9224 | tf_op jit(solution)/shard_map/ppermute | solution.py:48
  21.5 2.4 %collective-permute-start.4 = (f32[6,10,1]{2,1,0:T(8,128)S(1)}, f32[6,10,1]{2,1,0:T(8,128)S(1)}, u32[]{:S(2)}, u32[]{:S(2)}) collective-permute-start(f32[6,10,1]{2,1,0:T(8,128)S(1)} %get-tuple-element.221), channel_id=1, source_target_pairs={{1,0},{2,1},{3,2},{5,4},{6,5},{7,6},{9,8},{10,9},{11,10},{13,12},{... | collective-permute-start | bytes 728 | tf_op jit(solution)/shard_map/ppermute | solution.py:48
  24.0 4.3 %collective-permute-start.5 = (f32[6,10,1]{2,1,0:T(8,128)S(1)}, f32[6,10,1]{2,1,0:T(8,128)S(1)}, u32[]{:S(2)}, u32[]{:S(2)}) collective-permute-start(f32[6,10,1]{2,1,0:T(8,128)S(1)} %get-tuple-element.222), channel_id=1, source_target_pairs={{0,1},{1,2},{2,3},{4,5},{5,6},{6,7},{8,9},{9,10},{10,11},{12,13},{... | collective-permute-start | bytes 728 | tf_op jit(solution)/shard_map/ppermute | solution.py:46
  28.4 1.9 %collective-permute-start.17 = (s32[6,10,1]{2,1,0:T(8,128)S(1)}, s32[6,10,1]{2,1,0:T(8,128)S(1)}, u32[]{:S(2)}, u32[]{:S(2)}) collective-permute-start(s32[6,10,1]{2,1,0:T(8,128)S(1)} %get-tuple-element.220), channel_id=1, source_target_pairs={{1,0},{2,1},{3,2},{5,4},{6,5},{7,6},{9,8},{10,9},{11,10},{13,12},{... | collective-permute-start | bytes 728 | tf_op jit(solution)/shard_map/ppermute | solution.py:48
  30.3 4.8 %collective-permute-start.14 = (s32[6,10,1]{2,1,0:T(8,128)S(1)}, s32[6,10,1]{2,1,0:T(8,128)S(1)}, u32[]{:S(2)}, u32[]{:S(2)}) collective-permute-start(s32[6,10,1]{2,1,0:T(8,128)S(1)} %get-tuple-element.219), channel_id=1, source_target_pairs={{0,1},{1,2},{2,3},{4,5},{5,6},{6,7},{8,9},{9,10},{10,11},{12,13},{... | collective-permute-start | bytes 728 | tf_op jit(solution)/shard_map/ppermute | solution.py:46
  35.6 1.9 %collective-permute-start.7 = (f32[6,1,8,128]{3,2,1,0:T(8,128)S(1)}, f32[6,1,8,128]{3,2,1,0:T(8,128)S(1)}, u32[]{:S(2)}, u32[]{:S(2)}) collective-permute-start(f32[6,1,8,128]{3,2,1,0:T(8,128)S(1)} %bitcast.779), channel_id=1, source_target_pairs={{0,8},{8,16},{16,24},{1,9},{9,17},{17,25},{2,10},{10,18},{18,26},{... | collective-permute-start | bytes 73736 | tf_op jit(solution)/shard_map/ppermute | solution.py:46
  37.7 3.6 %collective-permute-done.7 = f32[6,1,8,128]{3,2,1,0:T(8,128)S(1)} collective-permute-done((f32[6,1,8,128]{3,2,1,0:T(8,128)S(1)}, f32[6,1,8,128]{3,2,1,0:T(8,128)S(1)}, u32[]{:S(2)}, u32[]{:S(2)}) %collective-permute-start.7) | collective-permute-done | bytes 24608 | tf_op jit(solution)/shard_map/ppermute | solution.py:46
  41.7 2.4 %collective-permute-start.9 = (f32[6,1,8,128]{3,2,1,0:T(8,128)S(1)}, f32[6,1,8,128]{3,2,1,0:T(8,128)S(1)}, u32[]{:S(2)}, u32[]{:S(2)}) collective-permute-start(f32[6,1,8,128]{3,2,1,0:T(8,128)S(1)} %bitcast.780), channel_id=1, source_target_pairs={{8,0},{16,8},{24,16},{9,1},{17,9},{25,17},{10,2},{18,10},{26,18},{... | collective-permute-start | bytes 73736 | tf_op jit(solution)/shard_map/ppermute | solution.py:48
  44.7 2.8 %collective-permute-done.9 = f32[6,1,8,128]{3,2,1,0:T(8,128)S(1)} collective-permute-done((f32[6,1,8,128]{3,2,1,0:T(8,128)S(1)}, f32[6,1,8,128]{3,2,1,0:T(8,128)S(1)}, u32[]{:S(2)}, u32[]{:S(2)}) %collective-permute-start.9) | collective-permute-done | bytes 24608 | tf_op jit(solution)/shard_map/ppermute | solution.py:48
  47.5 1.3 %collective-permute-start.11 = (f32[6,6,1,128]{3,0,1,2:T(8,128)S(1)}, f32[6,6,1,128]{3,0,1,2:T(8,128)S(1)}, u32[]{:S(2)}, u32[]{:S(2)}) collective-permute-start(f32[6,6,1,128]{3,0,1,2:T(8,128)S(1)} %bitcast.744), channel_id=1, source_target_pairs={{0,4},{1,5},{2,6},{3,7},{8,12},{9,13},{10,14},{11,15},{16,20},{17,... | collective-permute-start | bytes 55304 | tf_op jit(solution)/shard_map/ppermute | solution.py:46
  48.9 1.3 %collective-permute-start.12 = (f32[6,6,1,128]{3,2,1,0:T(1,128)S(1)}, f32[6,6,1,128]{3,2,1,0:T(1,128)S(1)}, u32[]{:S(2)}, u32[]{:S(2)}) collective-permute-start(f32[6,6,1,128]{3,2,1,0:T(1,128)S(1)} %stack.191), channel_id=1, source_target_pairs={{4,0},{5,1},{6,2},{7,3},{12,8},{13,9},{14,10},{15,11},{20,16},{21,... | collective-permute-start | bytes 55304 | tf_op jit(solution)/shard_map/ppermute | solution.py:48
  50.4 0.2 slice_reduce_fusion.6
  51.1 0.9 collective-permute-done.12
  52.1 0.2 fusion.1
  52.4 1.9 %collective-permute-start.15 = (f32[6,6,10,1]{2,0,1,3:T(8,128)S(1)}, f32[6,6,10,1]{2,0,1,3:T(8,128)S(1)}, u32[]{:S(2)}, u32[]{:S(2)}) collective-permute-start(f32[6,6,10,1]{2,0,1,3:T(8,128)S(1)} %bitcast.735), channel_id=1, source_target_pairs={{0,1},{1,2},{2,3},{4,5},{5,6},{6,7},{8,9},{9,10},{10,11},{12,13},{... | collective-permute-start | bytes 4328 | tf_op jit(solution)/shard_map/ppermute | solution.py:46
  54.4 3.9 %collective-permute-start.16 = (f32[6,6,10,1]{2,0,1,3:T(8,128)S(1)}, f32[6,6,10,1]{2,0,1,3:T(8,128)S(1)}, u32[]{:S(2)}, u32[]{:S(2)}) collective-permute-start(f32[6,6,10,1]{2,0,1,3:T(8,128)S(1)} %bitcast.741), channel_id=1, source_target_pairs={{1,0},{2,1},{3,2},{5,4},{6,5},{7,6},{9,8},{10,9},{11,10},{13,12},{... | collective-permute-start | bytes 4328 | tf_op jit(solution)/shard_map/ppermute | solution.py:48
  58.5 2.6 %collective-permute-done.16 = f32[6,6,10,1]{2,0,1,3:T(8,128)S(1)} collective-permute-done((f32[6,6,10,1]{2,0,1,3:T(8,128)S(1)}, f32[6,6,10,1]{2,0,1,3:T(8,128)S(1)}, u32[]{:S(2)}, u32[]{:S(2)}) %collective-permute-start.16) | collective-permute-done | bytes 1472 | tf_op jit(solution)/shard_map/ppermute | solution.py:48
  62.7 2.4 %collective-permute-start.18 = (f32[1,8,128]{2,1,0:T(8,128)S(1)}, f32[1,8,128]{2,1,0:T(8,128)S(1)}, u32[]{:S(2)}, u32[]{:S(2)}) collective-permute-start(f32[1,8,128]{2,1,0:T(8,128)S(1)} %get-tuple-element.296), channel_id=1, source_target_pairs={{8,0},{16,8},{24,16},{9,1},{17,9},{25,17},{10,2},{18,10},{26,18},{... | collective-permute-start | bytes 12296 | tf_op jit(solution)/shard_map/ppermute | solution.py:48
  65.0 3.5 %collective-permute-start.19 = (f32[1,8,128]{2,1,0:T(8,128)S(1)}, f32[1,8,128]{2,1,0:T(8,128)S(1)}, u32[]{:S(2)}, u32[]{:S(2)}) collective-permute-start(f32[1,8,128]{2,1,0:T(8,128)S(1)} %get-tuple-element.295), channel_id=1, source_target_pairs={{0,8},{8,16},{16,24},{1,9},{9,17},{17,25},{2,10},{10,18},{18,26},{... | collective-permute-start | bytes 12296 | tf_op jit(solution)/shard_map/ppermute | solution.py:46
  68.6 1.9 %collective-permute-done.19 = f32[1,8,128]{2,1,0:T(8,128)S(1)} collective-permute-done((f32[1,8,128]{2,1,0:T(8,128)S(1)}, f32[1,8,128]{2,1,0:T(8,128)S(1)}, u32[]{:S(2)}, u32[]{:S(2)}) %collective-permute-start.19) | collective-permute-done | bytes 4128 | tf_op jit(solution)/shard_map/ppermute | solution.py:46
  70.6 1.3 %collective-permute-start.20 = (f32[6,1,128]{2,1,0:T(1,128)S(1)}, f32[6,1,128]{2,1,0:T(1,128)S(1)}, u32[]{:S(2)}, u32[]{:S(2)}) collective-permute-start(f32[6,1,128]{2,1,0:T(1,128)S(1)} %get-tuple-element.268), channel_id=1, source_target_pairs={{4,0},{5,1},{6,2},{7,3},{12,8},{13,9},{14,10},{15,11},{20,16},{21,... | collective-permute-start | bytes 9224 | tf_op jit(solution)/shard_map/ppermute | solution.py:48
  71.8 3.0 %collective-permute-start.21 = (f32[6,1,128]{2,1,0:T(1,128)S(1)}, f32[6,1,128]{2,1,0:T(1,128)S(1)}, u32[]{:S(2)}, u32[]{:S(2)}) collective-permute-start(f32[6,1,128]{2,1,0:T(1,128)S(1)} %get-tuple-element.267), channel_id=1, source_target_pairs={{0,4},{1,5},{2,6},{3,7},{8,12},{9,13},{10,14},{11,15},{16,20},{17,... | collective-permute-start | bytes 9224 | tf_op jit(solution)/shard_map/ppermute | solution.py:46
  75.3 0.4 collective-permute-done.21
  75.8 3.0 %collective-permute-start.22 = (f32[6,10,1]{2,1,0:T(8,128)S(1)}, f32[6,10,1]{2,1,0:T(8,128)S(1)}, u32[]{:S(2)}, u32[]{:S(2)}) collective-permute-start(f32[6,10,1]{2,1,0:T(8,128)S(1)} %get-tuple-element.217), channel_id=1, source_target_pairs={{1,0},{2,1},{3,2},{5,4},{6,5},{7,6},{9,8},{10,9},{11,10},{13,12},{... | collective-permute-start | bytes 728 | tf_op jit(solution)/shard_map/ppermute | solution.py:48
  78.8 3.7 %collective-permute-start.23 = (f32[6,10,1]{2,1,0:T(8,128)S(1)}, f32[6,10,1]{2,1,0:T(8,128)S(1)}, u32[]{:S(2)}, u32[]{:S(2)}) collective-permute-start(f32[6,10,1]{2,1,0:T(8,128)S(1)} %get-tuple-element.218), channel_id=1, source_target_pairs={{0,1},{1,2},{2,3},{4,5},{5,6},{6,7},{8,9},{9,10},{10,11},{12,13},{... | collective-permute-start | bytes 728 | tf_op jit(solution)/shard_map/ppermute | solution.py:46
  82.8 2.0 %collective-permute-done.23 = f32[6,10,1]{2,1,0:T(8,128)S(1)} collective-permute-done((f32[6,10,1]{2,1,0:T(8,128)S(1)}, f32[6,10,1]{2,1,0:T(8,128)S(1)}, u32[]{:S(2)}, u32[]{:S(2)}) %collective-permute-start.23) | collective-permute-done | bytes 272 | tf_op jit(solution)/shard_map/ppermute | solution.py:46
  84.9 0.2 constant_dynamic-update-slice_fusion.70
  85.6 1.9 %collective-permute-start.25 = (f32[6,1,8,128]{3,2,1,0:T(8,128)S(1)}, f32[6,1,8,128]{3,2,1,0:T(8,128)S(1)}, u32[]{:S(2)}, u32[]{:S(2)}) collective-permute-start(f32[6,1,8,128]{3,2,1,0:T(8,128)S(1)} %bitcast.778), channel_id=1, source_target_pairs={{8,0},{16,8},{24,16},{9,1},{17,9},{25,17},{10,2},{18,10},{26,18},{... | collective-permute-start | bytes 73736 | tf_op jit(solution)/shard_map/ppermute | solution.py:48
  87.9 3.5 %collective-permute-done.25 = f32[6,1,8,128]{3,2,1,0:T(8,128)S(1)} collective-permute-done((f32[6,1,8,128]{3,2,1,0:T(8,128)S(1)}, f32[6,1,8,128]{3,2,1,0:T(8,128)S(1)}, u32[]{:S(2)}, u32[]{:S(2)}) %collective-permute-start.25) | collective-permute-done | bytes 24608 | tf_op jit(solution)/shard_map/ppermute | solution.py:48
  91.4 1.9 %collective-permute-start.24 = (f32[6,1,8,128]{3,2,1,0:T(8,128)S(1)}, f32[6,1,8,128]{3,2,1,0:T(8,128)S(1)}, u32[]{:S(2)}, u32[]{:S(2)}) collective-permute-start(f32[6,1,8,128]{3,2,1,0:T(8,128)S(1)} %bitcast.777), channel_id=1, source_target_pairs={{0,8},{8,16},{16,24},{1,9},{9,17},{17,25},{2,10},{10,18},{18,26},{... | collective-permute-start | bytes 73736 | tf_op jit(solution)/shard_map/ppermute | solution.py:46
  94.1 3.1 %collective-permute-done.24 = f32[6,1,8,128]{3,2,1,0:T(8,128)S(1)} collective-permute-done((f32[6,1,8,128]{3,2,1,0:T(8,128)S(1)}, f32[6,1,8,128]{3,2,1,0:T(8,128)S(1)}, u32[]{:S(2)}, u32[]{:S(2)}) %collective-permute-start.24) | collective-permute-done | bytes 24608 | tf_op jit(solution)/shard_map/ppermute | solution.py:46
  97.2 1.3 %collective-permute-start.26 = (f32[6,6,1,128]{3,1,0,2:T(8,128)S(1)}, f32[6,6,1,128]{3,1,0,2:T(8,128)S(1)}, u32[]{:S(2)}, u32[]{:S(2)}) collective-permute-start(f32[6,6,1,128]{3,1,0,2:T(8,128)S(1)} %bitcast.747), channel_id=1, source_target_pairs={{0,4},{1,5},{2,6},{3,7},{8,12},{9,13},{10,14},{11,15},{16,20},{17,... | collective-permute-start | bytes 55304 | tf_op jit(solution)/shard_map/ppermute | solution.py:46
  98.6 1.3 %collective-permute-start.27 = (f32[6,6,1,128]{3,2,1,0:T(1,128)S(1)}, f32[6,6,1,128]{3,2,1,0:T(1,128)S(1)}, u32[]{:S(2)}, u32[]{:S(2)}) collective-permute-start(f32[6,6,1,128]{3,2,1,0:T(1,128)S(1)} %stack.206), channel_id=1, source_target_pairs={{4,0},{5,1},{6,2},{7,3},{12,8},{13,9},{14,10},{15,11},{20,16},{21,... | collective-permute-start | bytes 55304 | tf_op jit(solution)/shard_map/ppermute | solution.py:48
  100.6 1.1 collective-permute-done.27
  102.3 4.6 %collective-permute-start.28 = (f32[6,6,10,1]{2,0,1,3:T(8,128)S(1)}, f32[6,6,10,1]{2,0,1,3:T(8,128)S(1)}, u32[]{:S(2)}, u32[]{:S(2)}) collective-permute-start(f32[6,6,10,1]{2,0,1,3:T(8,128)S(1)} %bitcast.732), channel_id=1, source_target_pairs={{0,1},{1,2},{2,3},{4,5},{5,6},{6,7},{8,9},{9,10},{10,11},{12,13},{... | collective-permute-start | bytes 4328 | tf_op jit(solution)/shard_map/ppermute | solution.py:46
  107.2 1.9 %collective-permute-start.29 = (f32[6,6,10,1]{2,0,1,3:T(8,128)S(1)}, f32[6,6,10,1]{2,0,1,3:T(8,128)S(1)}, u32[]{:S(2)}, u32[]{:S(2)}) collective-permute-start(f32[6,6,10,1]{2,0,1,3:T(8,128)S(1)} %bitcast.738), channel_id=1, source_target_pairs={{1,0},{2,1},{3,2},{5,4},{6,5},{7,6},{9,8},{10,9},{11,10},{13,12},{... | collective-permute-start | bytes 4328 | tf_op jit(solution)/shard_map/ppermute | solution.py:48
  109.2 4.6 %collective-permute-done.29 = f32[6,6,10,1]{2,0,1,3:T(8,128)S(1)} collective-permute-done((f32[6,6,10,1]{2,0,1,3:T(8,128)S(1)}, f32[6,6,10,1]{2,0,1,3:T(8,128)S(1)}, u32[]{:S(2)}, u32[]{:S(2)}) %collective-permute-start.29) | collective-permute-done | bytes 1472 | tf_op jit(solution)/shard_map/ppermute | solution.py:48
  116.1 0.6 copy-done.3
  117.3 0.7 copy-done.4
  (330 shorter events, 10.4 us)
Async XLA Ops:
  0.6 0.9 copy-start.2
  1.6 12.7 %copy-start.1 = (f32[7,4,8,128]{3,2,1,0:T(8,128)S(1)}, f32[7,4,8,128]{3,2,1,0:T(8,128)}, u32[]{:S(2)}) copy-start(f32[7,4,8,128]{3,2,1,0:T(8,128)} %param.4) | copy-start | bytes 344068
  1.6 12.6 %collective-permute-start = (f32[1,8,128]{2,1,0:T(8,128)S(1)}, f32[1,8,128]{2,1,0:T(8,128)S(1)}, u32[]{:S(2)}, u32[]{:S(2)}) collective-permute-start(f32[1,8,128]{2,1,0:T(8,128)S(1)} %get-tuple-element.300), channel_id=1, source_target_pairs={{8,0},{16,8},{24,16},{9,1},{17,9},{25,17},{10,2},{18,10},{26,18},{... | collective-permute-start | bytes 12296 | tf_op jit(solution)/shard_map/ppermute | solution.py:48
  4.1 10.2 %collective-permute-start.1 = (f32[1,8,128]{2,1,0:T(8,128)S(1)}, f32[1,8,128]{2,1,0:T(8,128)S(1)}, u32[]{:S(2)}, u32[]{:S(2)}) collective-permute-start(f32[1,8,128]{2,1,0:T(8,128)S(1)} %get-tuple-element.299), channel_id=1, source_target_pairs={{0,8},{8,16},{16,24},{1,9},{9,17},{17,25},{2,10},{10,18},{18,26},{... | collective-permute-start | bytes 12296 | tf_op jit(solution)/shard_map/ppermute | solution.py:46
  7.6 11.2 %collective-permute-start.6 = (s32[1,8,128]{2,1,0:T(8,128)S(1)}, s32[1,8,128]{2,1,0:T(8,128)S(1)}, u32[]{:S(2)}, u32[]{:S(2)}) collective-permute-start(s32[1,8,128]{2,1,0:T(8,128)S(1)} %get-tuple-element.298), channel_id=1, source_target_pairs={{0,8},{8,16},{16,24},{1,9},{9,17},{17,25},{2,10},{10,18},{18,26},{... | collective-permute-start | bytes 12296 | tf_op jit(solution)/shard_map/ppermute | solution.py:46
  9.5 9.3 %collective-permute-start.8 = (s32[1,8,128]{2,1,0:T(8,128)S(1)}, s32[1,8,128]{2,1,0:T(8,128)S(1)}, u32[]{:S(2)}, u32[]{:S(2)}) collective-permute-start(s32[1,8,128]{2,1,0:T(8,128)S(1)} %get-tuple-element.297), channel_id=1, source_target_pairs={{8,0},{16,8},{24,16},{9,1},{17,9},{25,17},{10,2},{18,10},{26,18},{... | collective-permute-start | bytes 12296 | tf_op jit(solution)/shard_map/ppermute | solution.py:48
  14.3 7.1 %collective-permute-start.2 = (f32[6,1,128]{2,1,0:T(1,128)S(1)}, f32[6,1,128]{2,1,0:T(1,128)S(1)}, u32[]{:S(2)}, u32[]{:S(2)}) collective-permute-start(f32[6,1,128]{2,1,0:T(1,128)S(1)} %get-tuple-element.284), channel_id=1, source_target_pairs={{4,0},{5,1},{6,2},{7,3},{12,8},{13,9},{14,10},{15,11},{20,16},{21,... | collective-permute-start | bytes 9224 | tf_op jit(solution)/shard_map/ppermute | solution.py:48
  15.6 19.6 %copy-start = (f32[19,4,8,128]{3,2,1,0:T(8,128)S(1)}, f32[19,4,8,128]{3,2,1,0:T(8,128)}, u32[]{:S(2)}) copy-start(f32[19,4,8,128]{3,2,1,0:T(8,128)} %param.3) | copy-start | bytes 933892
  15.6 5.8 %collective-permute-start.3 = (f32[6,1,128]{2,1,0:T(1,128)S(1)}, f32[6,1,128]{2,1,0:T(1,128)S(1)}, u32[]{:S(2)}, u32[]{:S(2)}) collective-permute-start(f32[6,1,128]{2,1,0:T(1,128)S(1)} %get-tuple-element.283), channel_id=1, source_target_pairs={{0,4},{1,5},{2,6},{3,7},{8,12},{9,13},{10,14},{11,15},{16,20},{17,... | collective-permute-start | bytes 9224 | tf_op jit(solution)/shard_map/ppermute | solution.py:46
  18.8 9.5 %collective-permute-start.10 = (s32[6,1,128]{2,1,0:T(1,128)S(1)}, s32[6,1,128]{2,1,0:T(1,128)S(1)}, u32[]{:S(2)}, u32[]{:S(2)}) collective-permute-start(s32[6,1,128]{2,1,0:T(1,128)S(1)} %get-tuple-element.269), channel_id=1, source_target_pairs={{0,4},{1,5},{2,6},{3,7},{8,12},{9,13},{10,14},{11,15},{16,20},{17,... | collective-permute-start | bytes 9224 | tf_op jit(solution)/shard_map/ppermute | solution.py:46
  20.1 8.2 %collective-permute-start.13 = (s32[6,1,128]{2,1,0:T(1,128)S(1)}, s32[6,1,128]{2,1,0:T(1,128)S(1)}, u32[]{:S(2)}, u32[]{:S(2)}) collective-permute-start(s32[6,1,128]{2,1,0:T(1,128)S(1)} %get-tuple-element.270), channel_id=1, source_target_pairs={{4,0},{5,1},{6,2},{7,3},{12,8},{13,9},{14,10},{15,11},{20,16},{21,... | collective-permute-start | bytes 9224 | tf_op jit(solution)/shard_map/ppermute | solution.py:48
  21.5 13.6 %collective-permute-start.4 = (f32[6,10,1]{2,1,0:T(8,128)S(1)}, f32[6,10,1]{2,1,0:T(8,128)S(1)}, u32[]{:S(2)}, u32[]{:S(2)}) collective-permute-start(f32[6,10,1]{2,1,0:T(8,128)S(1)} %get-tuple-element.221), channel_id=1, source_target_pairs={{1,0},{2,1},{3,2},{5,4},{6,5},{7,6},{9,8},{10,9},{11,10},{13,12},{... | collective-permute-start | bytes 728 | tf_op jit(solution)/shard_map/ppermute | solution.py:48
  24.0 11.2 %collective-permute-start.5 = (f32[6,10,1]{2,1,0:T(8,128)S(1)}, f32[6,10,1]{2,1,0:T(8,128)S(1)}, u32[]{:S(2)}, u32[]{:S(2)}) collective-permute-start(f32[6,10,1]{2,1,0:T(8,128)S(1)} %get-tuple-element.222), channel_id=1, source_target_pairs={{0,1},{1,2},{2,3},{4,5},{5,6},{6,7},{8,9},{9,10},{10,11},{12,13},{... | collective-permute-start | bytes 728 | tf_op jit(solution)/shard_map/ppermute | solution.py:46
  28.4 9.1 %collective-permute-start.17 = (s32[6,10,1]{2,1,0:T(8,128)S(1)}, s32[6,10,1]{2,1,0:T(8,128)S(1)}, u32[]{:S(2)}, u32[]{:S(2)}) collective-permute-start(s32[6,10,1]{2,1,0:T(8,128)S(1)} %get-tuple-element.220), channel_id=1, source_target_pairs={{1,0},{2,1},{3,2},{5,4},{6,5},{7,6},{9,8},{10,9},{11,10},{13,12},{... | collective-permute-start | bytes 728 | tf_op jit(solution)/shard_map/ppermute | solution.py:48
  30.3 7.2 %collective-permute-start.14 = (s32[6,10,1]{2,1,0:T(8,128)S(1)}, s32[6,10,1]{2,1,0:T(8,128)S(1)}, u32[]{:S(2)}, u32[]{:S(2)}) collective-permute-start(s32[6,10,1]{2,1,0:T(8,128)S(1)} %get-tuple-element.219), channel_id=1, source_target_pairs={{0,1},{1,2},{2,3},{4,5},{5,6},{6,7},{8,9},{9,10},{10,11},{12,13},{... | collective-permute-start | bytes 728 | tf_op jit(solution)/shard_map/ppermute | solution.py:46
  35.6 5.7 %collective-permute-start.7 = (f32[6,1,8,128]{3,2,1,0:T(8,128)S(1)}, f32[6,1,8,128]{3,2,1,0:T(8,128)S(1)}, u32[]{:S(2)}, u32[]{:S(2)}) collective-permute-start(f32[6,1,8,128]{3,2,1,0:T(8,128)S(1)} %bitcast.779), channel_id=1, source_target_pairs={{0,8},{8,16},{16,24},{1,9},{9,17},{17,25},{2,10},{10,18},{18,26},{... | collective-permute-start | bytes 73736 | tf_op jit(solution)/shard_map/ppermute | solution.py:46
  41.7 5.7 %collective-permute-start.9 = (f32[6,1,8,128]{3,2,1,0:T(8,128)S(1)}, f32[6,1,8,128]{3,2,1,0:T(8,128)S(1)}, u32[]{:S(2)}, u32[]{:S(2)}) collective-permute-start(f32[6,1,8,128]{3,2,1,0:T(8,128)S(1)} %bitcast.780), channel_id=1, source_target_pairs={{8,0},{16,8},{24,16},{9,1},{17,9},{25,17},{10,2},{18,10},{26,18},{... | collective-permute-start | bytes 73736 | tf_op jit(solution)/shard_map/ppermute | solution.py:48
  47.5 3.6 %collective-permute-start.11 = (f32[6,6,1,128]{3,0,1,2:T(8,128)S(1)}, f32[6,6,1,128]{3,0,1,2:T(8,128)S(1)}, u32[]{:S(2)}, u32[]{:S(2)}) collective-permute-start(f32[6,6,1,128]{3,0,1,2:T(8,128)S(1)} %bitcast.744), channel_id=1, source_target_pairs={{0,4},{1,5},{2,6},{3,7},{8,12},{9,13},{10,14},{11,15},{16,20},{17,... | collective-permute-start | bytes 55304 | tf_op jit(solution)/shard_map/ppermute | solution.py:46
  48.9 3.1 %collective-permute-start.12 = (f32[6,6,1,128]{3,2,1,0:T(1,128)S(1)}, f32[6,6,1,128]{3,2,1,0:T(1,128)S(1)}, u32[]{:S(2)}, u32[]{:S(2)}) collective-permute-start(f32[6,6,1,128]{3,2,1,0:T(1,128)S(1)} %stack.191), channel_id=1, source_target_pairs={{4,0},{5,1},{6,2},{7,3},{12,8},{13,9},{14,10},{15,11},{20,16},{21,... | collective-permute-start | bytes 55304 | tf_op jit(solution)/shard_map/ppermute | solution.py:48
  52.4 6.0 %collective-permute-start.15 = (f32[6,6,10,1]{2,0,1,3:T(8,128)S(1)}, f32[6,6,10,1]{2,0,1,3:T(8,128)S(1)}, u32[]{:S(2)}, u32[]{:S(2)}) collective-permute-start(f32[6,6,10,1]{2,0,1,3:T(8,128)S(1)} %bitcast.735), channel_id=1, source_target_pairs={{0,1},{1,2},{2,3},{4,5},{5,6},{6,7},{8,9},{9,10},{10,11},{12,13},{... | collective-permute-start | bytes 4328 | tf_op jit(solution)/shard_map/ppermute | solution.py:46
  54.4 6.6 %collective-permute-start.16 = (f32[6,6,10,1]{2,0,1,3:T(8,128)S(1)}, f32[6,6,10,1]{2,0,1,3:T(8,128)S(1)}, u32[]{:S(2)}, u32[]{:S(2)}) collective-permute-start(f32[6,6,10,1]{2,0,1,3:T(8,128)S(1)} %bitcast.741), channel_id=1, source_target_pairs={{1,0},{2,1},{3,2},{5,4},{6,5},{7,6},{9,8},{10,9},{11,10},{13,12},{... | collective-permute-start | bytes 4328 | tf_op jit(solution)/shard_map/ppermute | solution.py:48
  62.7 5.9 %collective-permute-start.18 = (f32[1,8,128]{2,1,0:T(8,128)S(1)}, f32[1,8,128]{2,1,0:T(8,128)S(1)}, u32[]{:S(2)}, u32[]{:S(2)}) collective-permute-start(f32[1,8,128]{2,1,0:T(8,128)S(1)} %get-tuple-element.296), channel_id=1, source_target_pairs={{8,0},{16,8},{24,16},{9,1},{17,9},{25,17},{10,2},{18,10},{26,18},{... | collective-permute-start | bytes 12296 | tf_op jit(solution)/shard_map/ppermute | solution.py:48
  65.0 5.5 %collective-permute-start.19 = (f32[1,8,128]{2,1,0:T(8,128)S(1)}, f32[1,8,128]{2,1,0:T(8,128)S(1)}, u32[]{:S(2)}, u32[]{:S(2)}) collective-permute-start(f32[1,8,128]{2,1,0:T(8,128)S(1)} %get-tuple-element.295), channel_id=1, source_target_pairs={{0,8},{8,16},{16,24},{1,9},{9,17},{17,25},{2,10},{10,18},{18,26},{... | collective-permute-start | bytes 12296 | tf_op jit(solution)/shard_map/ppermute | solution.py:46
  70.6 4.7 %collective-permute-start.20 = (f32[6,1,128]{2,1,0:T(1,128)S(1)}, f32[6,1,128]{2,1,0:T(1,128)S(1)}, u32[]{:S(2)}, u32[]{:S(2)}) collective-permute-start(f32[6,1,128]{2,1,0:T(1,128)S(1)} %get-tuple-element.268), channel_id=1, source_target_pairs={{4,0},{5,1},{6,2},{7,3},{12,8},{13,9},{14,10},{15,11},{20,16},{21,... | collective-permute-start | bytes 9224 | tf_op jit(solution)/shard_map/ppermute | solution.py:48
  71.8 3.8 %collective-permute-start.21 = (f32[6,1,128]{2,1,0:T(1,128)S(1)}, f32[6,1,128]{2,1,0:T(1,128)S(1)}, u32[]{:S(2)}, u32[]{:S(2)}) collective-permute-start(f32[6,1,128]{2,1,0:T(1,128)S(1)} %get-tuple-element.267), channel_id=1, source_target_pairs={{0,4},{1,5},{2,6},{3,7},{8,12},{9,13},{10,14},{11,15},{16,20},{17,... | collective-permute-start | bytes 9224 | tf_op jit(solution)/shard_map/ppermute | solution.py:46
  75.8 7.0 %collective-permute-start.22 = (f32[6,10,1]{2,1,0:T(8,128)S(1)}, f32[6,10,1]{2,1,0:T(8,128)S(1)}, u32[]{:S(2)}, u32[]{:S(2)}) collective-permute-start(f32[6,10,1]{2,1,0:T(8,128)S(1)} %get-tuple-element.217), channel_id=1, source_target_pairs={{1,0},{2,1},{3,2},{5,4},{6,5},{7,6},{9,8},{10,9},{11,10},{13,12},{... | collective-permute-start | bytes 728 | tf_op jit(solution)/shard_map/ppermute | solution.py:48
  78.8 6.0 %collective-permute-start.23 = (f32[6,10,1]{2,1,0:T(8,128)S(1)}, f32[6,10,1]{2,1,0:T(8,128)S(1)}, u32[]{:S(2)}, u32[]{:S(2)}) collective-permute-start(f32[6,10,1]{2,1,0:T(8,128)S(1)} %get-tuple-element.218), channel_id=1, source_target_pairs={{0,1},{1,2},{2,3},{4,5},{5,6},{6,7},{8,9},{9,10},{10,11},{12,13},{... | collective-permute-start | bytes 728 | tf_op jit(solution)/shard_map/ppermute | solution.py:46
  85.6 5.7 %collective-permute-start.25 = (f32[6,1,8,128]{3,2,1,0:T(8,128)S(1)}, f32[6,1,8,128]{3,2,1,0:T(8,128)S(1)}, u32[]{:S(2)}, u32[]{:S(2)}) collective-permute-start(f32[6,1,8,128]{3,2,1,0:T(8,128)S(1)} %bitcast.778), channel_id=1, source_target_pairs={{8,0},{16,8},{24,16},{9,1},{17,9},{25,17},{10,2},{18,10},{26,18},{... | collective-permute-start | bytes 73736 | tf_op jit(solution)/shard_map/ppermute | solution.py:48
  91.4 5.7 %collective-permute-start.24 = (f32[6,1,8,128]{3,2,1,0:T(8,128)S(1)}, f32[6,1,8,128]{3,2,1,0:T(8,128)S(1)}, u32[]{:S(2)}, u32[]{:S(2)}) collective-permute-start(f32[6,1,8,128]{3,2,1,0:T(8,128)S(1)} %bitcast.777), channel_id=1, source_target_pairs={{0,8},{8,16},{16,24},{1,9},{9,17},{17,25},{2,10},{10,18},{18,26},{... | collective-permute-start | bytes 73736 | tf_op jit(solution)/shard_map/ppermute | solution.py:46
  97.2 3.4 %collective-permute-start.26 = (f32[6,6,1,128]{3,1,0,2:T(8,128)S(1)}, f32[6,6,1,128]{3,1,0,2:T(8,128)S(1)}, u32[]{:S(2)}, u32[]{:S(2)}) collective-permute-start(f32[6,6,1,128]{3,1,0,2:T(8,128)S(1)} %bitcast.747), channel_id=1, source_target_pairs={{0,4},{1,5},{2,6},{3,7},{8,12},{9,13},{10,14},{11,15},{16,20},{17,... | collective-permute-start | bytes 55304 | tf_op jit(solution)/shard_map/ppermute | solution.py:46
  98.6 3.1 %collective-permute-start.27 = (f32[6,6,1,128]{3,2,1,0:T(1,128)S(1)}, f32[6,6,1,128]{3,2,1,0:T(1,128)S(1)}, u32[]{:S(2)}, u32[]{:S(2)}) collective-permute-start(f32[6,6,1,128]{3,2,1,0:T(1,128)S(1)} %stack.206), channel_id=1, source_target_pairs={{4,0},{5,1},{6,2},{7,3},{12,8},{13,9},{14,10},{15,11},{20,16},{21,... | collective-permute-start | bytes 55304 | tf_op jit(solution)/shard_map/ppermute | solution.py:48
  102.3 6.9 %collective-permute-start.28 = (f32[6,6,10,1]{2,0,1,3:T(8,128)S(1)}, f32[6,6,10,1]{2,0,1,3:T(8,128)S(1)}, u32[]{:S(2)}, u32[]{:S(2)}) collective-permute-start(f32[6,6,10,1]{2,0,1,3:T(8,128)S(1)} %bitcast.732), channel_id=1, source_target_pairs={{0,1},{1,2},{2,3},{4,5},{5,6},{6,7},{8,9},{9,10},{10,11},{12,13},{... | collective-permute-start | bytes 4328 | tf_op jit(solution)/shard_map/ppermute | solution.py:46
  107.2 6.6 %collective-permute-start.29 = (f32[6,6,10,1]{2,0,1,3:T(8,128)S(1)}, f32[6,6,10,1]{2,0,1,3:T(8,128)S(1)}, u32[]{:S(2)}, u32[]{:S(2)}) collective-permute-start(f32[6,6,10,1]{2,0,1,3:T(8,128)S(1)} %bitcast.738), channel_id=1, source_target_pairs={{1,0},{2,1},{3,2},{5,4},{6,5},{7,6},{9,8},{10,9},{11,10},{13,12},{... | collective-permute-start | bytes 4328 | tf_op jit(solution)/shard_map/ppermute | solution.py:48
  116.0 0.6 copy-start.3
  117.3 0.7 copy-start.4
where the time goes:
time: 119 us; the launch traced here: 118 us
  starting transfers between devices  74.9 us (63%)
  waiting for transfers between devices  26.4 us (22%)
  local copies, waits for them, and re-layouts  9.01 us (8%)
  other arithmetic  4.91 us (4%)
  between operations  2.75 us (2%)
    ppermute x15, starting transfers between devices, with_halo(): lax.ppermute(tail, axis, [(i, (i + 1) % count) for i in range(ends)])  42.2 us
    ppermute x15, starting transfers between devices, with_halo(): lax.ppermute(head, axis, [((i + 1) % count, i) for i in range(ends)])  32.7 us
    ppermute x15, waiting for transfers between devices, with_halo(): lax.ppermute(head, axis, [((i + 1) % count, i) for i in range(ends)])  15.4 us
    ppermute x15, waiting for transfers between devices, with_halo(): lax.ppermute(tail, axis, [(i, (i + 1) % count) for i in range(ends)])  11 us
    unnamed x81, local copies, waits for them, and re-layouts  4.54 us
  transfers between devices with their start and end apart: 30, of which 11 were waited for; matrix products, arithmetic and copies ran while one was open for 5% of the time, Pallas kernels for 0%

commit v1 on v0

v1 whole, which is shorter than its diff:
```python
import jax
import jax.numpy as jnp
from jax import lax
from jax.experimental import pallas as pl
from jax.experimental.pallas import tpu as pltpu
from jax.sharding import PartitionSpec as P

AXES = ("gx", "gy", "gz")

VEL_F = [
    (0, 0, 0),
    (1, 0, 0),
    (-1, 0, 0),
    (0, 1, 0),
    (0, -1, 0),
    (0, 0, 1),
    (0, 0, -1),
    (1, 1, 0),
    (-1, -1, 0),
    (1, -1, 0),
    (-1, 1, 0),
    (1, 0, 1),
    (-1, 0, -1),
    (1, 0, -1),
    (-1, 0, 1),
    (0, 1, 1),
    (0, -1, -1),
    (0, 1, -1),
    (0, -1, 1),
]
OPP_F = [0, 2, 1, 4, 3, 6, 5, 8, 7, 10, 9, 12, 11, 14, 13, 16, 15, 18, 17]
NF = 19
NG = 7
NP = NF + NG
VEL = VEL_F + VEL_F[:NG]
OPP = OPP_F + [NF + other for other in OPP_F[:NG]]

HALO = 4
ROCK = 3.0e38

IN_F = [1, 7, 9, 11, 13]
IN_G = 1
L_G2 = 0
L_F2 = L_G2 + NG
L_RHO2 = L_F2 + len(IN_F)
L_MOM2 = L_RHO2 + 1
L_G3 = L_MOM2 + 3
L_PH3 = L_G3 + 1
L_UX3 = L_PH3 + 1
L_PH4 = L_UX3 + 1
L_MASK = L_PH4 + 1
L_STRIP = L_MASK + 3


def pairing(sizes, axis, first):
    spare = "gy" if axis != "gy" else "gx"
    perm = []
    real = False

    def linear(at):
        return (at["gx"] * sizes["gy"] + at["gy"]) * sizes["gz"] + at["gz"]

    for gx in range(sizes["gx"]):
        for gy in range(sizes["gy"]):
            for gz in range(sizes["gz"]):
                at = {"gx": gx, "gy": gy, "gz": gz}
                other = at[axis] + (1 if at[axis] % 2 == first else -1)
                if 0 <= other < sizes[axis]:
                    real = True
                    perm.append((linear(at), linear({**at, axis: other})))
                elif at[spare] ^ 1 < sizes[spare]:
                    perm.append((linear(at), linear({**at, spare: at[spare] ^ 1})))
    return perm if real else None


def swap(sizes, axis, send_a, send_b):
    perm_a = pairing(sizes, axis, 0)
    perm_b = pairing(sizes, axis, 1)
    got_a = lax.ppermute(send_a, AXES, perm_a) if perm_a else send_a
    got_b = lax.ppermute(send_b, AXES, perm_b) if perm_b else got_a
    return got_a, got_b


def beside(sizes, cells):
    if sizes["gy"] <= 2:
        perm = pairing(sizes, "gy", 0)
        return lax.ppermute(cells, AXES, perm) if perm else cells
    got_a, got_b = swap(sizes, "gy", cells, cells)
    even = lax.axis_index("gy") % 2 == 0
    above = jnp.where(even, got_a, got_b)
    below = jnp.where(even, got_b, got_a)
    row = lax.broadcasted_iota(jnp.int32, cells.shape, cells.ndim - 2)
    return jnp.where(row < HALO, above, below)


def relax(rho, mom, phase, grads, pops):
    inv = 1.0 / rho if rho is not None else None
    vel = [m * inv if inv is not None else m for m in mom]
    square = grads[0] * grads[0] + grads[1] * grads[1] + grads[2] * grads[2] + 0.01
    inv_mag = lax.rsqrt(square)
    mag = square * inv_mag
    out = {}
    if any(member < NF for member in pops):
        omega = 1.0 / (0.8 + 0.2 * phase)
        keep = 1.0 - omega
        scale = omega * rho
        base = scale * (1.0 - 1.5 * (vel[0] * vel[0] + vel[1] * vel[1] + vel[2] * vel[2]))
        quad_v = [4.5 * scale * v for v in vel]
        quad_g = [0.5 * inv_mag * g for g in grads]
        lin = [(3.0 * scale) * v for v in vel]
        diag = [quad_v[d] * vel[d] + quad_g[d] * grads[d] for d in range(3)]
        tail = {
            0: (1.0 / 9.0) * mag,
            1: (-0.5 / 54.0) * mag,
            2: (-0.5 / 27.0) * mag,
        }
        memo = {}

        def once(key, make):
            if key not in memo:
                memo[key] = make()
            return memo[key]

        for member in pops:
            if member >= NF:
                continue
            dims = [d for d in range(3) if VEL[member][d] != 0]
            signs = [VEL[member][d] for d in dims]
            if not dims:
                out[member] = keep * pops[member] + ((1.0 / 3.0) * base + tail[0])
                continue
            if len(dims) == 1:
                d = dims[0]
                even = once(("e", d), lambda: (1.0 / 18.0) * (base + diag[d]) + tail[1])
                odd = once(("o", d), lambda: (1.0 / 18.0) * lin[d])
                flip = signs[0]
            else:
                a, b = dims
                same = signs[0] * signs[1]
                both = once(("s", a, b), lambda: base + diag[a] + diag[b])
                mixed = once(
                    ("m", a, b),
                    lambda: 2.0 * (quad_v[a] * vel[b] + quad_g[a] * grads[b]),
                )
                even = once(
                    ("e", a, b, same),
                    lambda: (1.0 / 36.0) * (both + mixed if same > 0 else both - mixed) + tail[2],
                )
                odd = once(
                    ("o", a, b, same),
                    lambda: (1.0 / 36.0) * (lin[a] + lin[b] if same > 0 else lin[a] - lin[b]),
                )
                flip = signs[0]
            mid = keep * pops[member] + even
            out[member] = mid + odd if flip > 0 else mid - odd
    if any(member >= NF for member in pops):
        sharpen = 0.7 * (1.0 - phase * phase) * inv_mag
        part = 1.25 * 0.125
        for member in pops:
            if member < NF:
                continue
            move = VEL[member]
            if move == (0, 0, 0):
                out[member] = (1.25 * 0.25) * phase - 0.25 * pops[member]
                continue
            d = [i for i in range(3) if move[i] != 0][0]
            drift = part * (4.0 * phase * vel[d] + sharpen * grads[d])
            still = part * phase - 0.25 * pops[member]
            out[member] = still + drift if move[d] > 0 else still - drift
    return out


def moments(pops):
    rho = pops[0]
    for member in range(1, NF):
        rho = rho + pops[member]
    mom = []
    for d in range(3):
        plus = [pops[m] for m in range(NF) if VEL[m][d] > 0]
        minus = [pops[m] for m in range(NF) if VEL[m][d] < 0]
        total = plus[0] - minus[0]
        for p, m in zip(plus[1:], minus[1:]):
            total = total + (p - m)
        mom.append(total)
    return rho, mom


def add_up(values):
    total = values[0]
    for value in values[1:]:
        total = total + value
    return total


def turn(value, shift, dim):
    size = value.shape[dim]
    shift = shift % size
    return pltpu.roll(value, shift, axis=dim) if shift else value


def pack_z_kernel(flow, phase, mask, out_a, out_b):
    cx, cy, cz = mask.shape
    even = lax.axis_index("gz") % 2 == 0
    group = lax.broadcasted_iota(jnp.int32, (cy, cz), 1) // HALO
    per = cz // (cx * HALO)
    for block in range(out_a.shape[0]):
        low = jnp.zeros((cy, cz), jnp.float32)
        high = low
        for field in range(block * per, min((block + 1) * per, NP + 1)):
            for x in range(cx):
                if field < NF:
                    value = flow[field, x]
                elif field < NP:
                    value = phase[field - NF, x]
                else:
                    value = mask[x].astype(jnp.float32)
                slot = (field % per) * cx + x
                here = group == slot
                low = jnp.where(here, turn(value, slot * HALO, 1), low)
                high = jnp.where(here, turn(value, (slot + 1) * HALO, 1), high)
        out_a[block] = jnp.where(even, high, low)
        out_b[block] = jnp.where(even, low, high)


def pack_x_kernel(flow, phase, mask, z_a, z_b, strips, out_a, out_b, *, sizes):
    cx, cy, cz = mask.shape
    at_z = lax.axis_index("gz")
    even_z = at_z % 2 == 0
    even_x = lax.axis_index("gx") % 2 == 0
    group = lax.broadcasted_iota(jnp.int32, (cy, cz), 1) // HALO
    per_in = cz // (cx * HALO)
    per_out = cz // (4 * cx * HALO)
    below = [jnp.where(even_z, z_b[i], z_a[i]) for i in range(z_a.shape[0])]
    above = [jnp.where(even_z, z_a[i], z_b[i]) for i in range(z_a.shape[0])]
    has_below = at_z > 0
    has_above = at_z < sizes["gz"] - 1
    for block in range(strips.shape[0]):
        total = jnp.zeros((cy, cz), jnp.float32)
        for field in range(block * per_out, min((block + 1) * per_out, NP + 1)):
            from_below = below[field // per_in]
            from_above = above[field // per_in]
            if field == NP:
                from_below = jnp.where(has_below, from_below, 0.0)
                from_above = jnp.where(has_above, from_above, 0.0)
            for x in range(cx):
                if field < NF:
                    value = flow[field, x]
                elif field < NP:
                    value = phase[field - NF, x]
                else:
                    value = mask[x].astype(jnp.float32)
                came = (field % per_in) * cx + x
                base = (field % per_out) * 4 * cx
                for piece, origin, slot in (
                    (from_below, came, base + 2 * x),
                    (value, 0, base + 2 * x + 1),
                    (value, cz // HALO - 1, base + 2 * (cx + x)),
                    (from_above, came, base + 2 * (cx + x) + 1),
                ):
                    total = jnp.where(
                        group == slot, turn(piece, (slot - origin) * HALO, 1), total
                    )
        strips[block] = total
        out_a[NP + L_STRIP + block] = total
        out_b[NP + L_STRIP + block] = total

    for out, up in ((out_a, even_x), (out_b, jnp.logical_not(even_x))):
        other = jnp.where(up, 0, 1)
        xs = [jnp.where(up, cx - 1 - d, d) for d in range(HALO)]
        for member in range(NF):
            out[member] = flow[member, xs[0]]
        for member in range(NG):
            out[NF + member] = phase[member, xs[0]]
            out[NP + L_G2 + member] = phase[member, xs[1]]
        for slot, member in enumerate(IN_F):
            out[NP + L_F2 + slot] = flow[member + other, xs[1]]
        rho, mom = moments([flow[member, xs[1]] for member in range(NF)])
        out[NP + L_RHO2] = rho
        for d in range(3):
            out[NP + L_MOM2 + d] = mom[d]
        out[NP + L_G3] = phase[IN_G + other, xs[2]]
        out[NP + L_PH3] = add_up([phase[member, xs[2]] for member in range(NG)])
        rho, mom = moments([flow[member, xs[2]] for member in range(NF)])
        out[NP + L_UX3] = mom[0] / rho
        far = add_up([phase[member, xs[3]] for member in range(NG)])
        out[NP + L_PH4] = jnp.where(mask[xs[3]] == 1, far, 0.0)
        for d in range(3):
            out[NP + L_MASK + d] = mask[xs[d]].astype(jnp.float32)


def steps_kernel(
    flow, phase, mask, strips, x_a, x_b,
    flow_y, phase_y, mask_y, strips_y, x_a_y, x_b_y,
    flow_out, phase_out,
    pops, face, own_mask, own_strips, fluid, potential,
    strip_pops, strip_fluid, strip_phase, moved, stayed, strip_moved, strip_stayed,
    phase_pops, potential1, moved1, stayed1, sem,
    *, sizes,
):
    _, cx, cy, cz = flow_out.shape
    rows = 2 * cy
    at_x = lax.axis_index("gx")
    at_y = lax.axis_index("gy")
    even_x = at_x % 2 == 0
    side_a = jnp.where(even_x, 1, 0)
    side_b = 1 - side_a

    copies = []

    def copy(src, dst):
        one = pltpu.make_async_copy(src, dst, sem.at[len(copies)])
        one.start()
        copies.append(one)

    for at, (f, g, m, s, a, b) in (
        (0, (flow, phase, mask, strips, x_a, x_b)),
        (cy, (flow_y, phase_y, mask_y, strips_y, x_a_y, x_b_y)),
    ):
        part = pl.ds(at, cy)
        copy(f, pops.at[pl.ds(0, NF), pl.ds(1, cx), part])
        copy(g, pops.at[pl.ds(NF, NG), pl.ds(1, cx), part])
        copy(m, own_mask.at[:, part])
        copy(s, own_strips.at[:, part])
        for got, side in ((a, side_a), (b, side_b)):
            copy(got.at[pl.ds(0, NP)], pops.at[:, side * (cx + 1), part])
            copy(got.at[pl.ds(NP, face.shape[1])], face.at[side, :, part])
    for one in copies:
        one.wait()

    lane = lax.broadcasted_iota(jnp.int32, (rows, cz), 1)
    row = lax.broadcasted_iota(jnp.int32, (rows, cz), 0)
    has_left = at_x > 0
    has_right = at_x < sizes["gx"] - 1
    has_low = at_y > 0
    has_high = at_y < sizes["gy"] - 1
    high_row = jnp.where(has_high, cy + HALO, cy)
    low_row = jnp.where(has_low, cy + HALO, rows)
    row_ok = (row < high_row) | (row >= low_row)
    has = (has_left, has_right)
    first, last = HALO, HALO + cx - 1

    def at_depth(side, depth):
        return first - depth if side == 0 else last + depth

    for x in range(cx):
        ok = (own_mask[x] == 1) & row_ok
        fluid[first + x] = ok.astype(jnp.float32)
        total = add_up([pops[NF + member, 1 + x] for member in range(NG)])
        potential[first + x] = jnp.where(ok, total, 0.0)
    for side in range(2):
        side_ok = row_ok & has[side]
        for depth in range(1, HALO + 1):
            if depth == 1:
                total = add_up([pops[NF + m, side * (cx + 1)] for m in range(NG)])
            elif depth == 2:
                total = add_up([face[side, L_G2 + m] for m in range(NG)])
            else:
                total = face[side, L_PH3 if depth == 3 else L_PH4]
            ok = side_ok
            if depth < HALO:
                ok = ok & (face[side, L_MASK + depth - 1] == 1.0)
                fluid[at_depth(side, depth)] = ok.astype(jnp.float32)
            potential[at_depth(side, depth)] = jnp.where(ok, total, 0.0)

    cols = 2 * HALO
    wide = cols * cx
    per = cz // (2 * wide)
    block_ok = row_ok & (
        ((lane < wide) & has_left)
        | ((lane >= wide) & (lane < 2 * wide))
        | ((lane >= 2 * wide) & (lane < 3 * wide) & has_right)
    )
    for side in range(2):
        for field in range(NP + 1):
            block = field // per
            origin = ((field % per) * 2 + side) * wide
            left = turn(face[0, L_STRIP + block], -origin, 1)
            mine = turn(own_strips[block], wide - origin, 1)
            right = turn(face[1, L_STRIP + block], 2 * wide - origin, 1)
            value = jnp.where(lane < wide, left, jnp.where(lane < 2 * wide, mine, right))
            if field < NP:
                strip_pops[side, field] = value
            else:
                strip_fluid[side] = jnp.where(block_ok, value, 0.0)

    def strip_grads(values):
        return (
            0.5 * (turn(values, -cols, 1) - turn(values, cols, 1)),
            0.5 * (turn(values, -1, 0) - turn(values, 1, 0)),
            0.5 * (turn(values, -1, 1) - turn(values, 1, 1)),
        )

    def push_strip(member, value, ok):
        move = VEL[member]
        value = jnp.where(ok, value, ROCK)
        value = turn(value, move[0] * cols + move[2], 1)
        return turn(value, move[1], 0)

    def strip_to_lane(side, values, at):
        if side == 0:
            return pltpu.roll(values, (2 * cz - (at * cols + HALO)) % cz, axis=1)
        return pltpu.roll(values, (cz - HALO - at * cols) % cz, axis=1)

    def main_grads(source, strip_source, at):
        here = source[at]
        down = jnp.where(lane == 0, strip_to_lane(0, strip_source[0], at), turn(here, 1, 1))
        up = jnp.where(
            lane == cz - 1, strip_to_lane(1, strip_source[1], at), turn(here, -1, 1)
        )
        return (
            0.5 * (source[at + 1] - source[at - 1]),
            0.5 * (turn(here, -1, 0) - turn(here, 1, 0)),
            0.5 * (up - down),
        )

    def push_main(member, value, ok, strip_source, at):
        move = VEL[member]
        value = jnp.where(ok, value, ROCK)
        value = turn(value, move[1], 0)
        if move[2] > 0:
            value = jnp.where(
                lane == 0, strip_to_lane(0, strip_source[0, member], at + move[0]), turn(value, 1, 1)
            )
        elif move[2] < 0:
            value = jnp.where(
                lane == cz - 1,
                strip_to_lane(1, strip_source[1, member], at + move[0]),
                turn(value, -1, 1),
            )
        return value

    for side in range(2):
        ok = strip_fluid[side] == 1.0
        values = [strip_pops[side, member] for member in range(NP)]
        total = jnp.where(ok, add_up(values[NF:]), 0.0)
        strip_phase[side] = turn(total, 1 if side == 0 else -1, 1)
        rho, mom = moments(values)
        done = relax(rho, mom, total, strip_grads(total), dict(enumerate(values)))
        for member in range(NP):
            strip_stayed[side, member] = done[member]
            strip_moved[side, member] = push_strip(member, done[member], ok)

    def collide(j, carry):
        at = first - 1 + j
        values = [pops[member, j] for member in range(NP)]
        ok = fluid[at] == 1.0
        rho, mom = moments(values)
        done = relax(
            rho, mom, potential[at], main_grads(potential, strip_phase, at),
            dict(enumerate(values)),
        )
        for member in range(NP):
            stayed[member, at] = done[member]
            moved[member, at] = push_main(member, done[member], ok, strip_moved, at)
        return carry

    lax.fori_loop(0, cx + 2, collide, 0)
    for side in range(2):
        at = at_depth(side, 2)
        members = {m + side: face[side, L_F2 + slot] for slot, m in enumerate(IN_F)}
        members.update({NF + m: face[side, L_G2 + m] for m in range(NG)})
        done = relax(
            face[side, L_RHO2], [face[side, L_MOM2 + d] for d in range(3)],
            potential[at], main_grads(potential, strip_phase, at), members,
        )
        ok = fluid[at] == 1.0
        for member in done:
            stayed[member, at] = done[member]
            moved[member, at] = push_main(member, done[member], ok, strip_moved, at)
        at = at_depth(side, 3)
        member = NF + IN_G + side
        done = relax(
            None, [face[side, L_UX3]] * 3, potential[at],
            main_grads(potential, strip_phase, at), {member: face[side, L_G3]},
        )
        ok = fluid[at] == 1.0
        moved[member, at] = push_main(member, done[member], ok, strip_moved, at)

    def pull(source, kept, member, at):
        if VEL[member] == (0, 0, 0):
            return kept[member, at]
        value = source[member, at - VEL[member][0]]
        return jnp.where(value == ROCK, kept[OPP[member], at], value)

    def stream(j, carry):
        at = first - 2 + j
        values = [pull(moved, stayed, NF + member, at) for member in range(NG)]
        for member in range(NG):
            phase_pops[member, at] = values[member]
        potential1[at] = jnp.where(fluid[at] == 1.0, add_up(values), 0.0)
        return carry

    lax.fori_loop(0, cx + 4, stream, 0)

    for side in range(2):
        ok = strip_fluid[side] == 1.0
        values = []
        for member in range(NP):
            value = strip_moved[side, member]
            back = strip_stayed[side, OPP[member]]
            values.append(jnp.where(value == ROCK, back, value))
        total = jnp.where(ok, add_up(values[NF:]), 0.0)
        rho, mom = moments(values)
        sign = 1 if side == 0 else -1
        wanted = {m: values[m] for m in range(NP) if VEL[m][2] == sign}
        done = relax(rho, mom, total, strip_grads(total), wanted)
        for member in wanted:
            strip_pops[side, member] = push_strip(member, done[member], ok)
        strip_phase[side] = turn(total, sign, 1)

    def collide1(j, carry):
        at = first - 1 + j
        values = [pull(moved, stayed, member, at) for member in range(NF)]
        values += [phase_pops[member, at] for member in range(NG)]
        ok = fluid[at] == 1.0
        rho, mom = moments(values)
        done = relax(
            rho, mom, potential1[at], main_grads(potential1, strip_phase, at),
            dict(enumerate(values)),
        )
        for member in range(NP):
            stayed1[member, at] = done[member]
            moved1[member, at] = push_main(member, done[member], ok, strip_pops, at)
        return carry

    lax.fori_loop(0, cx + 2, collide1, 0)

    def finish(x, carry):
        at = first + x
        own = pl.ds(0, cy)
        ok = fluid[at, own] == 1.0
        for member in range(NP):
            if VEL[member] == (0, 0, 0):
                value = stayed1[member, at, own]
            else:
                value = moved1[member, at - VEL[member][0], own]
                value = jnp.where(value == ROCK, stayed1[OPP[member], at, own], value)
            value = jnp.where(ok, value, pops[member, 1 + x, own])
            if member < NF:
                flow_out[member, x] = value
            else:
                phase_out[member - NF, x] = value
        return carry

    lax.fori_loop(0, cx, finish, 0)


def shards(sizes, flow_pops, phase_pops, pore_mask):
    cx, cy, cz = pore_mask.shape
    rows = 2 * cy
    assert cx >= HALO and cy == 2 * HALO and 6 * cx * HALO <= cz
    f32 = jnp.float32
    vmem = pl.BlockSpec(memory_space=pltpu.VMEM)
    anywhere = pl.BlockSpec(memory_space=pl.ANY)

    flow_y = beside(sizes, flow_pops)
    phase_y = beside(sizes, phase_pops)
    mask_y = beside(sizes, pore_mask)

    z_blocks = pl.cdiv(NP + 1, cz // (cx * HALO))
    z_shape = jax.ShapeDtypeStruct((z_blocks, cy, cz), f32)
    z_a, z_b = pl.pallas_call(
        pack_z_kernel,
        out_shape=(z_shape, z_shape),
        in_specs=[vmem] * 3,
        out_specs=(vmem, vmem),
        name="pack_z",
    )(flow_pops, phase_pops, pore_mask)
    z_a, z_b = swap(sizes, "gz", z_a, z_b)

    strip_blocks = pl.cdiv(NP + 1, cz // (4 * cx * HALO))
    strip_shape = jax.ShapeDtypeStruct((strip_blocks, cy, cz), f32)
    x_layers = NP + L_STRIP + strip_blocks
    x_shape = jax.ShapeDtypeStruct((x_layers, cy, cz), f32)
    strips, x_a, x_b = pl.pallas_call(
        lambda *refs: pack_x_kernel(*refs, sizes=sizes),
        out_shape=(strip_shape, x_shape, x_shape),
        in_specs=[vmem] * 5,
        out_specs=(vmem,) * 3,
        name="pack_x",
    )(flow_pops, phase_pops, pore_mask, z_a, z_b)
    strips_y = beside(sizes, strips)
    x_a, x_b = swap(sizes, "gx", x_a, x_b)
    x_a_y = beside(sizes, x_a)
    x_b_y = beside(sizes, x_b)

    deep = cx + 2 * HALO

    def block(*lead):
        return pltpu.VMEM((*lead, rows, cz), f32)

    return pl.pallas_call(
        lambda *refs: steps_kernel(*refs, sizes=sizes),
        out_shape=(
            jax.ShapeDtypeStruct(flow_pops.shape, f32),
            jax.ShapeDtypeStruct(phase_pops.shape, f32),
        ),
        in_specs=[anywhere] * 12,
        out_specs=(vmem, vmem),
        scratch_shapes=[
            block(NP, cx + 2),
            block(2, L_STRIP + strip_blocks),
            pltpu.VMEM((cx, rows, cz), jnp.int32),
            block(strip_blocks),
            block(deep),
            block(deep),
            block(2, NP),
            block(2),
            block(2),
            block(NP, deep),
            block(NP, deep),
            block(2, NP),
            block(2, NP),
            block(NG, deep),
            block(deep),
            block(NP, deep),
            block(NP, deep),
            pltpu.SemaphoreType.DMA((16,)),
        ],
        name="two_steps",
    )(
        flow_pops, phase_pops, pore_mask, strips, x_a, x_b,
        flow_y, phase_y, mask_y, strips_y, x_a_y, x_b_y,
    )


def solution(mesh):
    sizes = dict(mesh.shape)
    placed = (P(None, "gx", "gy", "gz"), P(None, "gx", "gy", "gz"), P("gx", "gy", "gz"))
    return jax.shard_map(
        lambda *args: shards(sizes, *args),
        mesh=mesh,
        in_specs=placed,
        out_specs=(P(None, "gx", "gy", "gz"), P(None, "gx", "gy", "gz")),
        check_vma=False,
    )
```

time: 119 us -> 31.5 us (0.26)
  the two profiles are of different devices: /device:TPU:18 before, /device:TPU:21 now
where the time goes in v1:
time: 31.5 us; the launch traced here: 31.4 us
  Pallas kernels  10.6 us (34%)
  starting transfers between devices  10.3 us (33%)
  waiting for transfers between devices  7.64 us (24%)
  local copies, waits for them, and re-layouts  2.14 us (7%)
  between operations  0.71 us (2%)
    ppermute x6, starting transfers between devices, beside(): return lax.ppermute(cells, AXES, perm) if perm else cells  7.59 us
    pallas_call x1, Pallas kernels, shards(): pl.pallas_call(lambda *refs: steps_kernel(*refs, sizes=sizes), out_shape=...  6.24 us
    ppermute x2, waiting for transfers between devices, swap(): got_a = lax.ppermute(send_a, AXES, perm_a) if perm_a else send_a  3.58 us
    ppermute x2, starting transfers between devices, swap(): got_a = lax.ppermute(send_a, AXES, perm_a) if perm_a else send_a  2.51 us
    pallas_call x1, Pallas kernels, shards(): pl.pallas_call(lambda *refs: pack_x_kernel(*refs, sizes=sizes), out_shape...  2.39 us
    unnamed x26, local copies, waits for them, and re-layouts  2.14 us
    ppermute x2, waiting for transfers between devices, swap(): got_b = lax.ppermute(send_b, AXES, perm_b) if perm_b else got_a  2.11 us
    ppermute x6, waiting for transfers between devices, beside(): return lax.ppermute(cells, AXES, perm) if perm else cells  1.95 us
  transfers between devices with their start and end apart: 10, of which 5 were waited for; matrix products, arithmetic and copies ran while one was open for 0% of the time, Pallas kernels for 0%

profile of v1, /device:TPU:21, one launch (start us, length us, event | category | flops | bytes accessed | tf_op | source)
XLA Modules:
  0.0 31.4 jit_solution(10267467065255648540)
XLA Ops:
  0.6 1.9 %pack_z.1 = (f32[4,8,128]{2,1,0:T(8,128)}, f32[4,8,128]{2,1,0:T(8,128)}) custom-call(f32[19,4,8,128]{3,2,1,0:T(8,128)} %refs_0_.3, f32[7,4,8,128]{3,2,1,0:T(8,128)} %refs_1_.3, s32[4,8,128]{2,1,0:T(8,128)} %refs_2_.3), custom_call_target="tpu_custom_call" | custom-call | tf_op jit(solution)/shard_map/pack_z/pallas_call | solution.py:562
  2.6 0.0 copy-start
  2.6 1.2 %collective-permute-start = (f32[4,8,128]{2,1,0:T(8,128)}, f32[4,8,128]{2,1,0:T(8,128)S(1)}, u32[]{:S(2)}, u32[]{:S(2)}) collective-permute-start(f32[4,8,128]{2,1,0:T(8,128)} %get-tuple-element.7), channel_id=1, source_target_pairs={{0,1},{1,0},{2,3},{3,2},{4,5},{5,4},{6,7},{7,6},{8,9},{9,8},{10,11... | collective-permute-start | bytes 49160 | tf_op jit(solution)/shard_map/ppermute | solution.py:79
  3.8 0.0 copy-start.1
  3.8 0.0 copy-start.7
  3.8 0.2 collective-permute-start.1
  4.0 1.4 %collective-permute-done.refs_3_ = f32[4,8,128]{2,1,0:T(8,128)S(1)} collective-permute-done((f32[4,8,128]{2,1,0:T(8,128)}, f32[4,8,128]{2,1,0:T(8,128)S(1)}, u32[]{:S(2)}, u32[]{:S(2)}) %collective-permute-start) | collective-permute-done | bytes 16416 | tf_op jit(solution)/shard_map/ppermute | solution.py:79
  5.4 0.0 copy-start.11
  5.4 2.1 %collective-permute-done.1.refs_4_ = f32[4,8,128]{2,1,0:T(8,128)S(1)} collective-permute-done((f32[4,8,128]{2,1,0:T(8,128)}, f32[4,8,128]{2,1,0:T(8,128)S(1)}, u32[]{:S(2)}, u32[]{:S(2)}) %collective-permute-start.1) | collective-permute-done | bytes 16416 | tf_op jit(solution)/shard_map/ppermute | solution.py:80
  7.5 0.0 copy-done.11
  7.5 0.0 copy-start.12
  7.5 0.6 %copy-done.12 = f32[4,8,128]{2,1,0:T(8,128)} copy-done((f32[4,8,128]{2,1,0:T(8,128)}, f32[4,8,128]{2,1,0:T(8,128)S(1)}, u32[]{:S(2)}) %copy-start.12) | copy-done | bytes 16408
  8.1 2.4 %pack_x.1 = (f32[14,8,128]{2,1,0:T(8,128)}, f32[63,8,128]{2,1,0:T(8,128)}, f32[63,8,128]{2,1,0:T(8,128)}) custom-call(f32[19,4,8,128]{3,2,1,0:T(8,128)} %refs_0_.3, f32[7,4,8,128]{3,2,1,0:T(8,128)} %refs_1_.3, s32[4,8,128]{2,1,0:T(8,128)} %refs_2_.3, f32[4,8,128]{2,1,0:T(8,128)} %copy-done.11, f32[4,8,128]{2,1,0:T(8,128)} %copy-done.12), custom_call_target="tpu_custom_call" | custom-call | tf_op jit(solution)/shard_map/pack_x/pallas_call | solution.py:575
  10.5 1.3 %collective-permute-start.2 = (f32[63,8,128]{2,1,0:T(8,128)}, f32[63,8,128]{2,1,0:T(8,128)S(1)}, u32[]{:S(2)}, u32[]{:S(2)}) collective-permute-start(f32[63,8,128]{2,1,0:T(8,128)} %get-tuple-element.10), channel_id=1, source_target_pairs={{0,8},{1,9},{2,10},{3,11},{4,12},{5,13},{6,14},{7,15},{8,0},{9,1},... | collective-permute-start | bytes 774152 | tf_op jit(solution)/shard_map/ppermute | solution.py:79
  11.8 0.0 collective-permute-start.3
  11.8 0.0 copy-done
  11.8 2.4 %collective-permute-start.4 = (f32[19,4,8,128]{3,2,1,0:T(8,128)S(1)}, f32[19,4,8,128]{3,2,1,0:T(8,128)S(1)}, u32[]{:S(2)}, u32[]{:S(2)}) collective-permute-start(f32[19,4,8,128]{3,2,1,0:T(8,128)S(1)} %copy-done), channel_id=1, source_target_pairs={{0,4},{1,5},{2,6},{3,7},{4,0},{5,1},{6,2},{7,3},{8,12},{9,13},{10,... | collective-permute-start | bytes 933896 | tf_op jit(solution)/shard_map/ppermute | solution.py:87
  14.2 2.2 %collective-permute-done.2.refs_4_ = f32[63,8,128]{2,1,0:T(8,128)S(1)} collective-permute-done((f32[63,8,128]{2,1,0:T(8,128)}, f32[63,8,128]{2,1,0:T(8,128)S(1)}, u32[]{:S(2)}, u32[]{:S(2)}) %collective-permute-start.2) | collective-permute-done | bytes 258080 | tf_op jit(solution)/shard_map/ppermute | solution.py:79
  16.4 0.0 copy-start.3
  16.4 3.0 %collective-permute-start.8 = (f32[63,8,128]{2,1,0:T(8,128)S(1)}, f32[63,8,128]{2,1,0:T(8,128)S(1)}, u32[]{:S(2)}, u32[]{:S(2)}) collective-permute-start(f32[63,8,128]{2,1,0:T(8,128)S(1)} %collective-permute-done.2.refs_4_), channel_id=1, source_target_pairs={{0,4},{1,5},{2,6},{3,7},{4,0},{5,1},{6,2},{7,3},{8,12},{9,13},{10,... | collective-permute-start | bytes 774152 | tf_op jit(solution)/shard_map/ppermute | solution.py:87
  19.3 0.0 collective-permute-done.3.refs_5_
  19.3 0.0 copy-start.4
  19.3 1.4 %collective-permute-start.9 = (f32[63,8,128]{2,1,0:T(8,128)S(1)}, f32[63,8,128]{2,1,0:T(8,128)S(1)}, u32[]{:S(2)}, u32[]{:S(2)}) collective-permute-start(f32[63,8,128]{2,1,0:T(8,128)S(1)} %collective-permute-done.3.refs_5_), channel_id=1, source_target_pairs={{0,4},{1,5},{2,6},{3,7},{4,0},{5,1},{6,2},{7,3},{8,12},{9,13},{10,... | collective-permute-start | bytes 774152 | tf_op jit(solution)/shard_map/ppermute | solution.py:87
  20.7 0.0 copy-done.1
  20.7 0.1 collective-permute-start.5
  20.8 0.0 copy-done.7
  20.8 0.4 %collective-permute-start.6 = (s32[4,8,128]{2,1,0:T(8,128)S(1)}, s32[4,8,128]{2,1,0:T(8,128)S(1)}, u32[]{:S(2)}, u32[]{:S(2)}) collective-permute-start(s32[4,8,128]{2,1,0:T(8,128)S(1)} %copy-done.7), channel_id=1, source_target_pairs={{0,4},{1,5},{2,6},{3,7},{4,0},{5,1},{6,2},{7,3},{8,12},{9,13},{10,... | collective-permute-start | bytes 49160 | tf_op jit(solution)/shard_map/ppermute | solution.py:87
  21.2 0.8 %collective-permute-done.6.refs_8_ = s32[4,8,128]{2,1,0:T(8,128)S(1)} collective-permute-done((s32[4,8,128]{2,1,0:T(8,128)S(1)}, s32[4,8,128]{2,1,0:T(8,128)S(1)}, u32[]{:S(2)}, u32[]{:S(2)}) %collective-permute-start.6) | collective-permute-done | bytes 16416 | tf_op jit(solution)/shard_map/ppermute | solution.py:87
  22.1 0.0 copy-start.10
  22.1 0.4 %collective-permute-start.7 = (f32[14,8,128]{2,1,0:T(8,128)}, f32[14,8,128]{2,1,0:T(8,128)S(1)}, u32[]{:S(2)}, u32[]{:S(2)}) collective-permute-start(f32[14,8,128]{2,1,0:T(8,128)} %get-tuple-element.9.refs_3_), channel_id=1, source_target_pairs={{0,4},{1,5},{2,6},{3,7},{4,0},{5,1},{6,2},{7,3},{8,12},{9,13},{10,... | collective-permute-start | bytes 172040 | tf_op jit(solution)/shard_map/ppermute | solution.py:87
  22.4 1.1 %collective-permute-done.7.refs_9_ = f32[14,8,128]{2,1,0:T(8,128)S(1)} collective-permute-done((f32[14,8,128]{2,1,0:T(8,128)}, f32[14,8,128]{2,1,0:T(8,128)S(1)}, u32[]{:S(2)}, u32[]{:S(2)}) %collective-permute-start.7) | collective-permute-done | bytes 57376 | tf_op jit(solution)/shard_map/ppermute | solution.py:87
  23.5 0.0 copy-start.9
  23.5 0.0 collective-permute-done.5.refs_7_
  23.5 0.0 copy-start.8
  23.5 0.0 collective-permute-done.4.refs_6_
  23.5 0.0 copy-start.2
  23.5 0.0 collective-permute-done.8.refs_10_
  23.6 0.0 copy-start.5
  23.6 0.0 collective-permute-done.9.refs_11_
  23.6 0.0 copy-done.3
  23.6 0.0 copy-done.4
  23.6 0.0 copy-done.10
  23.6 0.5 %copy-done.9 = f32[14,8,128]{2,1,0:T(8,128)} copy-done((f32[14,8,128]{2,1,0:T(8,128)}, f32[14,8,128]{2,1,0:T(8,128)S(1)}, u32[]{:S(2)}) %copy-start.9) | copy-done | bytes 57368
  24.2 0.0 copy-done.8
  24.2 0.1 copy-done.2
  24.3 0.1 copy-done.5
  24.4 0.7 %copy-done.6 = f32[63,8,128]{2,1,0:T(8,128)} copy-done((f32[63,8,128]{2,1,0:T(8,128)}, f32[63,8,128]{2,1,0:T(8,128)S(1)}, u32[]{:S(2)}) %copy-start.6) | copy-done | bytes 258072
  25.1 6.2 %two_steps.1 = (f32[19,4,8,128]{3,2,1,0:T(8,128)}, f32[7,4,8,128]{3,2,1,0:T(8,128)}) custom-call(f32[19,4,8,128]{3,2,1,0:T(8,128)} %refs_0_.3, f32[7,4,8,128]{3,2,1,0:T(8,128)} %refs_1_.3, s32[4,8,128]{2,1,0:T(8,128)} %refs_2_.3, f32[14,8,128]{2,1,0:T(8,128)} %get-tuple-element.9.refs_3_, f32[63,8,128]{2,1,0:T(8,128)} %copy-done.3, f32[63,8,128]{2,1,0:T(8,128)} %copy-done.4, ...), custom_call_target="tpu_custom_call" | custom-call | tf_op jit(solution)/shard_map/two_steps/pallas_call | solution.py:592
  (1 shorter events, 0.0 us)
Async XLA Ops:
  2.6 9.2 %copy-start = (f32[19,4,8,128]{3,2,1,0:T(8,128)S(1)}, f32[19,4,8,128]{3,2,1,0:T(8,128)}, u32[]{:S(2)}) copy-start(f32[19,4,8,128]{3,2,1,0:T(8,128)} %refs_0_.3) | copy-start | bytes 933892
  2.6 2.8 %collective-permute-start = (f32[4,8,128]{2,1,0:T(8,128)}, f32[4,8,128]{2,1,0:T(8,128)S(1)}, u32[]{:S(2)}, u32[]{:S(2)}) collective-permute-start(f32[4,8,128]{2,1,0:T(8,128)} %get-tuple-element.7), channel_id=1, source_target_pairs={{0,1},{1,0},{2,3},{3,2},{4,5},{5,4},{6,7},{7,6},{8,9},{9,8},{10,11... | collective-permute-start | bytes 49160 | tf_op jit(solution)/shard_map/ppermute | solution.py:79
  3.8 16.9 %copy-start.1 = (f32[7,4,8,128]{3,2,1,0:T(8,128)S(1)}, f32[7,4,8,128]{3,2,1,0:T(8,128)}, u32[]{:S(2)}) copy-start(f32[7,4,8,128]{3,2,1,0:T(8,128)} %refs_1_.3) | copy-start | bytes 344068
  3.8 17.0 %copy-start.7 = (s32[4,8,128]{2,1,0:T(8,128)S(1)}, s32[4,8,128]{2,1,0:T(8,128)}, u32[]{:S(2)}) copy-start(s32[4,8,128]{2,1,0:T(8,128)} %refs_2_.3) | copy-start | bytes 49156
  3.8 3.7 %collective-permute-start.1 = (f32[4,8,128]{2,1,0:T(8,128)}, f32[4,8,128]{2,1,0:T(8,128)S(1)}, u32[]{:S(2)}, u32[]{:S(2)}) collective-permute-start(f32[4,8,128]{2,1,0:T(8,128)} %get-tuple-element.8), channel_id=1, source_target_pairs={{0,4},{1,2},{2,1},{3,7},{4,0},{5,6},{6,5},{7,3},{8,12},{9,10},{10,... | collective-permute-start | bytes 49160 | tf_op jit(solution)/shard_map/ppermute | solution.py:80
  5.4 2.1 %copy-start.11 = (f32[4,8,128]{2,1,0:T(8,128)}, f32[4,8,128]{2,1,0:T(8,128)S(1)}, u32[]{:S(2)}) copy-start(f32[4,8,128]{2,1,0:T(8,128)S(1)} %collective-permute-done.refs_3_) | copy-start | bytes 49156
  7.5 0.6 %copy-start.12 = (f32[4,8,128]{2,1,0:T(8,128)}, f32[4,8,128]{2,1,0:T(8,128)S(1)}, u32[]{:S(2)}) copy-start(f32[4,8,128]{2,1,0:T(8,128)S(1)} %collective-permute-done.1.refs_4_) | copy-start | bytes 49156
  10.5 5.9 %collective-permute-start.2 = (f32[63,8,128]{2,1,0:T(8,128)}, f32[63,8,128]{2,1,0:T(8,128)S(1)}, u32[]{:S(2)}, u32[]{:S(2)}) collective-permute-start(f32[63,8,128]{2,1,0:T(8,128)} %get-tuple-element.10), channel_id=1, source_target_pairs={{0,8},{1,9},{2,10},{3,11},{4,12},{5,13},{6,14},{7,15},{8,0},{9,1},... | collective-permute-start | bytes 774152 | tf_op jit(solution)/shard_map/ppermute | solution.py:79
  11.8 7.6 %collective-permute-start.3 = (f32[63,8,128]{2,1,0:T(8,128)}, f32[63,8,128]{2,1,0:T(8,128)S(1)}, u32[]{:S(2)}, u32[]{:S(2)}) collective-permute-start(f32[63,8,128]{2,1,0:T(8,128)} %get-tuple-element.11), channel_id=1, source_target_pairs={{0,4},{1,5},{2,6},{3,7},{4,0},{5,1},{6,2},{7,3},{8,16},{9,17},{10,... | collective-permute-start | bytes 774152 | tf_op jit(solution)/shard_map/ppermute | solution.py:80
  11.8 11.8 %collective-permute-start.4 = (f32[19,4,8,128]{3,2,1,0:T(8,128)S(1)}, f32[19,4,8,128]{3,2,1,0:T(8,128)S(1)}, u32[]{:S(2)}, u32[]{:S(2)}) collective-permute-start(f32[19,4,8,128]{3,2,1,0:T(8,128)S(1)} %copy-done), channel_id=1, source_target_pairs={{0,4},{1,5},{2,6},{3,7},{4,0},{5,1},{6,2},{7,3},{8,12},{9,13},{10,... | collective-permute-start | bytes 933896 | tf_op jit(solution)/shard_map/ppermute | solution.py:87
  16.4 7.2 %copy-start.3 = (f32[63,8,128]{2,1,0:T(8,128)}, f32[63,8,128]{2,1,0:T(8,128)S(1)}, u32[]{:S(2)}) copy-start(f32[63,8,128]{2,1,0:T(8,128)S(1)} %collective-permute-done.2.refs_4_) | copy-start | bytes 774148
  16.4 7.2 %collective-permute-start.8 = (f32[63,8,128]{2,1,0:T(8,128)S(1)}, f32[63,8,128]{2,1,0:T(8,128)S(1)}, u32[]{:S(2)}, u32[]{:S(2)}) collective-permute-start(f32[63,8,128]{2,1,0:T(8,128)S(1)} %collective-permute-done.2.refs_4_), channel_id=1, source_target_pairs={{0,4},{1,5},{2,6},{3,7},{4,0},{5,1},{6,2},{7,3},{8,12},{9,13},{10,... | collective-permute-start | bytes 774152 | tf_op jit(solution)/shard_map/ppermute | solution.py:87
  19.3 4.3 %copy-start.4 = (f32[63,8,128]{2,1,0:T(8,128)}, f32[63,8,128]{2,1,0:T(8,128)S(1)}, u32[]{:S(2)}) copy-start(f32[63,8,128]{2,1,0:T(8,128)S(1)} %collective-permute-done.3.refs_5_) | copy-start | bytes 774148
  19.3 4.2 %collective-permute-start.9 = (f32[63,8,128]{2,1,0:T(8,128)S(1)}, f32[63,8,128]{2,1,0:T(8,128)S(1)}, u32[]{:S(2)}, u32[]{:S(2)}) collective-permute-start(f32[63,8,128]{2,1,0:T(8,128)S(1)} %collective-permute-done.3.refs_5_), channel_id=1, source_target_pairs={{0,4},{1,5},{2,6},{3,7},{4,0},{5,1},{6,2},{7,3},{8,12},{9,13},{10,... | collective-permute-start | bytes 774152 | tf_op jit(solution)/shard_map/ppermute | solution.py:87
  20.7 2.8 %collective-permute-start.5 = (f32[7,4,8,128]{3,2,1,0:T(8,128)S(1)}, f32[7,4,8,128]{3,2,1,0:T(8,128)S(1)}, u32[]{:S(2)}, u32[]{:S(2)}) collective-permute-start(f32[7,4,8,128]{3,2,1,0:T(8,128)S(1)} %copy-done.1), channel_id=1, source_target_pairs={{0,4},{1,5},{2,6},{3,7},{4,0},{5,1},{6,2},{7,3},{8,12},{9,13},{10,... | collective-permute-start | bytes 344072 | tf_op jit(solution)/shard_map/ppermute | solution.py:87
  20.8 1.3 %collective-permute-start.6 = (s32[4,8,128]{2,1,0:T(8,128)S(1)}, s32[4,8,128]{2,1,0:T(8,128)S(1)}, u32[]{:S(2)}, u32[]{:S(2)}) collective-permute-start(s32[4,8,128]{2,1,0:T(8,128)S(1)} %copy-done.7), channel_id=1, source_target_pairs={{0,4},{1,5},{2,6},{3,7},{4,0},{5,1},{6,2},{7,3},{8,12},{9,13},{10,... | collective-permute-start | bytes 49160 | tf_op jit(solution)/shard_map/ppermute | solution.py:87
  22.1 1.5 %copy-start.10 = (s32[4,8,128]{2,1,0:T(8,128)}, s32[4,8,128]{2,1,0:T(8,128)S(1)}, u32[]{:S(2)}) copy-start(s32[4,8,128]{2,1,0:T(8,128)S(1)} %collective-permute-done.6.refs_8_) | copy-start | bytes 49156
  22.1 1.5 %collective-permute-start.7 = (f32[14,8,128]{2,1,0:T(8,128)}, f32[14,8,128]{2,1,0:T(8,128)S(1)}, u32[]{:S(2)}, u32[]{:S(2)}) collective-permute-start(f32[14,8,128]{2,1,0:T(8,128)} %get-tuple-element.9.refs_3_), channel_id=1, source_target_pairs={{0,4},{1,5},{2,6},{3,7},{4,0},{5,1},{6,2},{7,3},{8,12},{9,13},{10,... | collective-permute-start | bytes 172040 | tf_op jit(solution)/shard_map/ppermute | solution.py:87
  23.5 0.6 %copy-start.9 = (f32[14,8,128]{2,1,0:T(8,128)}, f32[14,8,128]{2,1,0:T(8,128)S(1)}, u32[]{:S(2)}) copy-start(f32[14,8,128]{2,1,0:T(8,128)S(1)} %collective-permute-done.7.refs_9_) | copy-start | bytes 172036
  23.5 0.7 %copy-start.8 = (f32[7,4,8,128]{3,2,1,0:T(8,128)}, f32[7,4,8,128]{3,2,1,0:T(8,128)S(1)}, u32[]{:S(2)}) copy-start(f32[7,4,8,128]{3,2,1,0:T(8,128)S(1)} %collective-permute-done.5.refs_7_) | copy-start | bytes 344068
  23.5 0.8 %copy-start.2 = (f32[19,4,8,128]{3,2,1,0:T(8,128)}, f32[19,4,8,128]{3,2,1,0:T(8,128)S(1)}, u32[]{:S(2)}) copy-start(f32[19,4,8,128]{3,2,1,0:T(8,128)S(1)} %collective-permute-done.4.refs_6_) | copy-start | bytes 933892
  23.6 0.9 %copy-start.5 = (f32[63,8,128]{2,1,0:T(8,128)}, f32[63,8,128]{2,1,0:T(8,128)S(1)}, u32[]{:S(2)}) copy-start(f32[63,8,128]{2,1,0:T(8,128)S(1)} %collective-permute-done.8.refs_10_) | copy-start | bytes 774148
  24.4 0.7 %copy-start.6 = (f32[63,8,128]{2,1,0:T(8,128)}, f32[63,8,128]{2,1,0:T(8,128)S(1)}, u32[]{:S(2)}) copy-start(f32[63,8,128]{2,1,0:T(8,128)S(1)} %collective-permute-done.9.refs_11_) | copy-start | bytes 774148

commit v2 on v1

--- a/solution.py
+++ b/solution.py
@@ -553,32 +553,35 @@
     vmem = pl.BlockSpec(memory_space=pltpu.VMEM)
     anywhere = pl.BlockSpec(memory_space=pl.ANY)
 
+    def near(*arrays):
+        return [pltpu.with_memory_space_constraint(a, pltpu.VMEM) for a in arrays]
+
     flow_y = beside(sizes, flow_pops)
     phase_y = beside(sizes, phase_pops)
     mask_y = beside(sizes, pore_mask)
 
     z_blocks = pl.cdiv(NP + 1, cz // (cx * HALO))
-    z_shape = jax.ShapeDtypeStruct((z_blocks, cy, cz), f32)
+    z_shape = pltpu.VMEM((z_blocks, cy, cz), f32)
     z_a, z_b = pl.pallas_call(
         pack_z_kernel,
         out_shape=(z_shape, z_shape),
         in_specs=[vmem] * 3,
         out_specs=(vmem, vmem),
         name="pack_z",
-    )(flow_pops, phase_pops, pore_mask)
+    )(*near(flow_pops, phase_pops, pore_mask))
     z_a, z_b = swap(sizes, "gz", z_a, z_b)
 
     strip_blocks = pl.cdiv(NP + 1, cz // (4 * cx * HALO))
-    strip_shape = jax.ShapeDtypeStruct((strip_blocks, cy, cz), f32)
+    strip_shape = pltpu.VMEM((strip_blocks, cy, cz), f32)
     x_layers = NP + L_STRIP + strip_blocks
-    x_shape = jax.ShapeDtypeStruct((x_layers, cy, cz), f32)
+    x_shape = pltpu.VMEM((x_layers, cy, cz), f32)
     strips, x_a, x_b = pl.pallas_call(
         lambda *refs: pack_x_kernel(*refs, sizes=sizes),
         out_shape=(strip_shape, x_shape, x_shape),
         in_specs=[vmem] * 5,
         out_specs=(vmem,) * 3,
         name="pack_x",
-    )(flow_pops, phase_pops, pore_mask, z_a, z_b)
+    )(*near(flow_pops, phase_pops, pore_mask, z_a, z_b))
     strips_y = beside(sizes, strips)
     x_a, x_b = swap(sizes, "gx", x_a, x_b)
     x_a_y = beside(sizes, x_a)
@@ -619,8 +622,10 @@
         ],
         name="two_steps",
     )(
-        flow_pops, phase_pops, pore_mask, strips, x_a, x_b,
-        flow_y, phase_y, mask_y, strips_y, x_a_y, x_b_y,
+        *near(
+            flow_pops, phase_pops, pore_mask, strips, x_a, x_b,
+            flow_y, phase_y, mask_y, strips_y, x_a_y, x_b_y,
+        )
     )
 
 

time: 31.5 us -> 26.7 us (0.85)
  Pallas kernels: 10.6 us -> 5.77 us
  waiting for transfers between devices: 7.64 us -> 7.02 us
  local copies, waits for them, and re-layouts: 2.14 us -> 2.58 us
    pallas_call x1, Pallas kernels: 2.39 us -> 0.55 us  [shards(): pl.pallas_call(lambda *refs: pack_x_kernel(*refs, sizes=sizes), out_shape...]
    pallas_call x1, Pallas kernels: 1.93 us -> 0.28 us  [shards(): pl.pallas_call(pack_z_kernel, out_shape=(z_shape, z_shape), in_specs=[vme...]
    pallas_call x1, Pallas kernels: 6.24 us -> 4.94 us  [shards(): pl.pallas_call(lambda *refs: steps_kernel(*refs, sizes=sizes), out_shape=...]
    unnamed x26 -> x6, local copies, waits for them, and re-layouts: 2.14 us -> 2.58 us
    ppermute x2, waiting for transfers between devices: 3.58 us -> 3.17 us  [swap(): got_a = lax.ppermute(send_a, AXES, perm_a) if perm_a else send_a]
where the time goes in v2:
time: 26.7 us; the launch traced here: 26.5 us
  starting transfers between devices  10.4 us (39%)
  waiting for transfers between devices  7.02 us (26%)
  Pallas kernels  5.77 us (22%)
  local copies, waits for them, and re-layouts  2.58 us (10%)
  between operations  0.67 us (3%)
    ppermute x6, starting transfers between devices, beside(): return lax.ppermute(cells, AXES, perm) if perm else cells  7.6 us
    pallas_call x1, Pallas kernels, shards(): pl.pallas_call(lambda *refs: steps_kernel(*refs, sizes=sizes), out_shape=...  4.94 us
    ppermute x2, waiting for transfers between devices, swap(): got_a = lax.ppermute(send_a, AXES, perm_a) if perm_a else send_a  3.17 us
    ppermute x2, starting transfers between devices, swap(): got_a = lax.ppermute(send_a, AXES, perm_a) if perm_a else send_a  2.64 us
    unnamed x6, local copies, waits for them, and re-layouts  2.58 us
    ppermute x2, waiting for transfers between devices, swap(): got_b = lax.ppermute(send_b, AXES, perm_b) if perm_b else got_a  2.11 us
    ppermute x6, waiting for transfers between devices, beside(): return lax.ppermute(cells, AXES, perm) if perm else cells  1.74 us
    pallas_call x1, Pallas kernels, shards(): pl.pallas_call(lambda *refs: pack_x_kernel(*refs, sizes=sizes), out_shape...  0.55 us
  transfers between devices with their start and end apart: 10, of which 5 were waited for; matrix products, arithmetic and copies ran while one was open for 0% of the time, Pallas kernels for 0%

profile of v2, /device:TPU:21, one launch (start us, length us, event | category | flops | bytes accessed | tf_op | source)
XLA Modules:
  0.0 26.5 jit_solution(7729356374844705325)
XLA Ops:
  0.6 0.0 copy-start
  0.6 1.0 %copy-done = f32[19,4,8,128]{3,2,1,0:T(8,128)S(1)} copy-done((f32[19,4,8,128]{3,2,1,0:T(8,128)S(1)}, f32[19,4,8,128]{3,2,1,0:T(8,128)}, u32[]{:S(2)}) %copy-start) | copy-done | bytes 311320
  1.6 0.0 copy-start.1
  1.6 0.9 %copy-done.1 = f32[7,4,8,128]{3,2,1,0:T(8,128)S(1)} copy-done((f32[7,4,8,128]{3,2,1,0:T(8,128)S(1)}, f32[7,4,8,128]{3,2,1,0:T(8,128)}, u32[]{:S(2)}) %copy-start.1) | copy-done | bytes 114712
  2.5 0.0 copy-start.2
  2.5 0.7 %copy-done.2 = s32[4,8,128]{2,1,0:T(8,128)S(1)} copy-done((s32[4,8,128]{2,1,0:T(8,128)S(1)}, s32[4,8,128]{2,1,0:T(8,128)}, u32[]{:S(2)}) %copy-start.2) | copy-done | bytes 16408
  3.2 0.3 %pack_z.1 = (f32[4,8,128]{2,1,0:T(8,128)S(1)}, f32[4,8,128]{2,1,0:T(8,128)S(1)}) custom-call(f32[19,4,8,128]{3,2,1,0:T(8,128)S(1)} %copy-done, f32[7,4,8,128]{3,2,1,0:T(8,128)S(1)} %copy-done.1, s32[4,8,128]{2,1,0:T(8,128)S(1)} %copy-done.2), custom_call_target="tpu_custom_call" | custom-call | tf_op jit(solution)/shard_map/pack_z/pallas_call | solution.py:565
  3.5 1.3 %collective-permute-start = (f32[4,8,128]{2,1,0:T(8,128)S(1)}, f32[4,8,128]{2,1,0:T(8,128)S(1)}, u32[]{:S(2)}, u32[]{:S(2)}) collective-permute-start(f32[4,8,128]{2,1,0:T(8,128)S(1)} %get-tuple-element.7), channel_id=1, source_target_pairs={{0,1},{1,0},{2,3},{3,2},{4,5},{5,4},{6,7},{7,6},{8,9},{9,8},{10,11... | collective-permute-start | bytes 49160 | tf_op jit(solution)/shard_map/ppermute | solution.py:79
  4.8 0.2 collective-permute-start.1
  5.0 1.2 %collective-permute-done.refs_3_ = f32[4,8,128]{2,1,0:T(8,128)S(1)} collective-permute-done((f32[4,8,128]{2,1,0:T(8,128)S(1)}, f32[4,8,128]{2,1,0:T(8,128)S(1)}, u32[]{:S(2)}, u32[]{:S(2)}) %collective-permute-start) | collective-permute-done | bytes 16416 | tf_op jit(solution)/shard_map/ppermute | solution.py:79
  6.2 2.1 %collective-permute-done.1.refs_4_ = f32[4,8,128]{2,1,0:T(8,128)S(1)} collective-permute-done((f32[4,8,128]{2,1,0:T(8,128)S(1)}, f32[4,8,128]{2,1,0:T(8,128)S(1)}, u32[]{:S(2)}, u32[]{:S(2)}) %collective-permute-start.1) | collective-permute-done | bytes 16416 | tf_op jit(solution)/shard_map/ppermute | solution.py:80
  8.3 0.5 %pack_x.1 = (f32[14,8,128]{2,1,0:T(8,128)S(1)}, f32[63,8,128]{2,1,0:T(8,128)S(1)}, f32[63,8,128]{2,1,0:T(8,128)S(1)}) custom-call(f32[19,4,8,128]{3,2,1,0:T(8,128)S(1)} %copy-done, f32[7,4,8,128]{3,2,1,0:T(8,128)S(1)} %copy-done.1, s32[4,8,128]{2,1,0:T(8,128)S(1)} %copy-done.2, f32[4,8,128]{2,1,0:T(8,128)S(1)} %collective-permute-done.refs_3_, ...), custom_call_target="tpu_custom_call" | custom-call | tf_op jit(solution)/shard_map/pack_x/pallas_call | solution.py:578
  8.8 1.4 %collective-permute-start.2 = (f32[63,8,128]{2,1,0:T(8,128)S(1)}, f32[63,8,128]{2,1,0:T(8,128)S(1)}, u32[]{:S(2)}, u32[]{:S(2)}) collective-permute-start(f32[63,8,128]{2,1,0:T(8,128)S(1)} %get-tuple-element.10), channel_id=1, source_target_pairs={{0,8},{1,9},{2,10},{3,11},{4,12},{5,13},{6,14},{7,15},{8,0},{9,1},... | collective-permute-start | bytes 774152 | tf_op jit(solution)/shard_map/ppermute | solution.py:79
  10.2 0.0 collective-permute-start.3
  10.2 2.4 %collective-permute-start.4 = (f32[19,4,8,128]{3,2,1,0:T(8,128)S(1)}, f32[19,4,8,128]{3,2,1,0:T(8,128)S(1)}, u32[]{:S(2)}, u32[]{:S(2)}) collective-permute-start(f32[19,4,8,128]{3,2,1,0:T(8,128)S(1)} %copy-done), channel_id=1, source_target_pairs={{0,4},{1,5},{2,6},{3,7},{4,0},{5,1},{6,2},{7,3},{8,12},{9,13},{10,... | collective-permute-start | bytes 933896 | tf_op jit(solution)/shard_map/ppermute | solution.py:87
  12.6 2.0 %collective-permute-done.2.refs_4_ = f32[63,8,128]{2,1,0:T(8,128)S(1)} collective-permute-done((f32[63,8,128]{2,1,0:T(8,128)S(1)}, f32[63,8,128]{2,1,0:T(8,128)S(1)}, u32[]{:S(2)}, u32[]{:S(2)}) %collective-permute-start.2) | collective-permute-done | bytes 258080 | tf_op jit(solution)/shard_map/ppermute | solution.py:79
  14.6 3.0 %collective-permute-start.8 = (f32[63,8,128]{2,1,0:T(8,128)S(1)}, f32[63,8,128]{2,1,0:T(8,128)S(1)}, u32[]{:S(2)}, u32[]{:S(2)}) collective-permute-start(f32[63,8,128]{2,1,0:T(8,128)S(1)} %collective-permute-done.2.refs_4_), channel_id=1, source_target_pairs={{0,4},{1,5},{2,6},{3,7},{4,0},{5,1},{6,2},{7,3},{8,12},{9,13},{10,... | collective-permute-start | bytes 774152 | tf_op jit(solution)/shard_map/ppermute | solution.py:87
  17.5 0.0 collective-permute-done.3.refs_5_
  17.5 1.4 %collective-permute-start.9 = (f32[63,8,128]{2,1,0:T(8,128)S(1)}, f32[63,8,128]{2,1,0:T(8,128)S(1)}, u32[]{:S(2)}, u32[]{:S(2)}) collective-permute-start(f32[63,8,128]{2,1,0:T(8,128)S(1)} %collective-permute-done.3.refs_5_), channel_id=1, source_target_pairs={{0,4},{1,5},{2,6},{3,7},{4,0},{5,1},{6,2},{7,3},{8,12},{9,13},{10,... | collective-permute-start | bytes 774152 | tf_op jit(solution)/shard_map/ppermute | solution.py:87
  18.9 0.0 collective-permute-start.5
  18.9 0.5 %collective-permute-start.6 = (s32[4,8,128]{2,1,0:T(8,128)S(1)}, s32[4,8,128]{2,1,0:T(8,128)S(1)}, u32[]{:S(2)}, u32[]{:S(2)}) collective-permute-start(s32[4,8,128]{2,1,0:T(8,128)S(1)} %copy-done.2), channel_id=1, source_target_pairs={{0,4},{1,5},{2,6},{3,7},{4,0},{5,1},{6,2},{7,3},{8,12},{9,13},{10,... | collective-permute-start | bytes 49160 | tf_op jit(solution)/shard_map/ppermute | solution.py:87
  19.4 0.8 %collective-permute-done.6.refs_8_ = s32[4,8,128]{2,1,0:T(8,128)S(1)} collective-permute-done((s32[4,8,128]{2,1,0:T(8,128)S(1)}, s32[4,8,128]{2,1,0:T(8,128)S(1)}, u32[]{:S(2)}, u32[]{:S(2)}) %collective-permute-start.6) | collective-permute-done | bytes 16416 | tf_op jit(solution)/shard_map/ppermute | solution.py:87
  20.2 0.4 %collective-permute-start.7 = (f32[14,8,128]{2,1,0:T(8,128)S(1)}, f32[14,8,128]{2,1,0:T(8,128)S(1)}, u32[]{:S(2)}, u32[]{:S(2)}) collective-permute-start(f32[14,8,128]{2,1,0:T(8,128)S(1)} %get-tuple-element.9.refs_3_), channel_id=1, source_target_pairs={{0,4},{1,5},{2,6},{3,7},{4,0},{5,1},{6,2},{7,3},{8,12},{9,13},{10,... | collective-permute-start | bytes 172040 | tf_op jit(solution)/shard_map/ppermute | solution.py:87
  20.6 0.9 %collective-permute-done.7.refs_9_ = f32[14,8,128]{2,1,0:T(8,128)S(1)} collective-permute-done((f32[14,8,128]{2,1,0:T(8,128)S(1)}, f32[14,8,128]{2,1,0:T(8,128)S(1)}, u32[]{:S(2)}, u32[]{:S(2)}) %collective-permute-start.7) | collective-permute-done | bytes 57376 | tf_op jit(solution)/shard_map/ppermute | solution.py:87
  21.5 0.0 collective-permute-done.5.refs_7_
  21.5 0.0 collective-permute-done.4.refs_6_
  21.5 0.0 collective-permute-done.8.refs_10_
  21.5 0.0 collective-permute-done.9.refs_11_
  21.5 4.9 %two_steps.1 = (f32[19,4,8,128]{3,2,1,0:T(8,128)}, f32[7,4,8,128]{3,2,1,0:T(8,128)}) custom-call(f32[19,4,8,128]{3,2,1,0:T(8,128)S(1)} %copy-done, f32[7,4,8,128]{3,2,1,0:T(8,128)S(1)} %copy-done.1, s32[4,8,128]{2,1,0:T(8,128)S(1)} %copy-done.2, f32[14,8,128]{2,1,0:T(8,128)S(1)} %get-tuple-element.9.refs_3_, ...), custom_call_target="tpu_custom_call" | custom-call | tf_op jit(solution)/shard_map/two_steps/pallas_call | solution.py:595
Async XLA Ops:
  0.6 1.0 %copy-start = (f32[19,4,8,128]{3,2,1,0:T(8,128)S(1)}, f32[19,4,8,128]{3,2,1,0:T(8,128)}, u32[]{:S(2)}) copy-start(f32[19,4,8,128]{3,2,1,0:T(8,128)} %refs_0_.3) | copy-start | bytes 933892
  1.6 0.9 %copy-start.1 = (f32[7,4,8,128]{3,2,1,0:T(8,128)S(1)}, f32[7,4,8,128]{3,2,1,0:T(8,128)}, u32[]{:S(2)}) copy-start(f32[7,4,8,128]{3,2,1,0:T(8,128)} %refs_1_.3) | copy-start | bytes 344068
  2.5 0.7 %copy-start.2 = (s32[4,8,128]{2,1,0:T(8,128)S(1)}, s32[4,8,128]{2,1,0:T(8,128)}, u32[]{:S(2)}) copy-start(s32[4,8,128]{2,1,0:T(8,128)} %refs_2_.3) | copy-start | bytes 49156
  3.5 2.7 %collective-permute-start = (f32[4,8,128]{2,1,0:T(8,128)S(1)}, f32[4,8,128]{2,1,0:T(8,128)S(1)}, u32[]{:S(2)}, u32[]{:S(2)}) collective-permute-start(f32[4,8,128]{2,1,0:T(8,128)S(1)} %get-tuple-element.7), channel_id=1, source_target_pairs={{0,1},{1,0},{2,3},{3,2},{4,5},{5,4},{6,7},{7,6},{8,9},{9,8},{10,11... | collective-permute-start | bytes 49160 | tf_op jit(solution)/shard_map/ppermute | solution.py:79
  4.8 3.5 %collective-permute-start.1 = (f32[4,8,128]{2,1,0:T(8,128)S(1)}, f32[4,8,128]{2,1,0:T(8,128)S(1)}, u32[]{:S(2)}, u32[]{:S(2)}) collective-permute-start(f32[4,8,128]{2,1,0:T(8,128)S(1)} %get-tuple-element.8), channel_id=1, source_target_pairs={{0,4},{1,2},{2,1},{3,7},{4,0},{5,6},{6,5},{7,3},{8,12},{9,10},{10,... | collective-permute-start | bytes 49160 | tf_op jit(solution)/shard_map/ppermute | solution.py:80
  8.8 5.7 %collective-permute-start.2 = (f32[63,8,128]{2,1,0:T(8,128)S(1)}, f32[63,8,128]{2,1,0:T(8,128)S(1)}, u32[]{:S(2)}, u32[]{:S(2)}) collective-permute-start(f32[63,8,128]{2,1,0:T(8,128)S(1)} %get-tuple-element.10), channel_id=1, source_target_pairs={{0,8},{1,9},{2,10},{3,11},{4,12},{5,13},{6,14},{7,15},{8,0},{9,1},... | collective-permute-start | bytes 774152 | tf_op jit(solution)/shard_map/ppermute | solution.py:79
  10.2 7.3 %collective-permute-start.3 = (f32[63,8,128]{2,1,0:T(8,128)S(1)}, f32[63,8,128]{2,1,0:T(8,128)S(1)}, u32[]{:S(2)}, u32[]{:S(2)}) collective-permute-start(f32[63,8,128]{2,1,0:T(8,128)S(1)} %get-tuple-element.11), channel_id=1, source_target_pairs={{0,4},{1,5},{2,6},{3,7},{4,0},{5,1},{6,2},{7,3},{8,16},{9,17},{10,... | collective-permute-start | bytes 774152 | tf_op jit(solution)/shard_map/ppermute | solution.py:80
  10.2 11.3 %collective-permute-start.4 = (f32[19,4,8,128]{3,2,1,0:T(8,128)S(1)}, f32[19,4,8,128]{3,2,1,0:T(8,128)S(1)}, u32[]{:S(2)}, u32[]{:S(2)}) collective-permute-start(f32[19,4,8,128]{3,2,1,0:T(8,128)S(1)} %copy-done), channel_id=1, source_target_pairs={{0,4},{1,5},{2,6},{3,7},{4,0},{5,1},{6,2},{7,3},{8,12},{9,13},{10,... | collective-permute-start | bytes 933896 | tf_op jit(solution)/shard_map/ppermute | solution.py:87
  14.6 7.0 %collective-permute-start.8 = (f32[63,8,128]{2,1,0:T(8,128)S(1)}, f32[63,8,128]{2,1,0:T(8,128)S(1)}, u32[]{:S(2)}, u32[]{:S(2)}) collective-permute-start(f32[63,8,128]{2,1,0:T(8,128)S(1)} %collective-permute-done.2.refs_4_), channel_id=1, source_target_pairs={{0,4},{1,5},{2,6},{3,7},{4,0},{5,1},{6,2},{7,3},{8,12},{9,13},{10,... | collective-permute-start | bytes 774152 | tf_op jit(solution)/shard_map/ppermute | solution.py:87
  17.5 4.0 %collective-permute-start.9 = (f32[63,8,128]{2,1,0:T(8,128)S(1)}, f32[63,8,128]{2,1,0:T(8,128)S(1)}, u32[]{:S(2)}, u32[]{:S(2)}) collective-permute-start(f32[63,8,128]{2,1,0:T(8,128)S(1)} %collective-permute-done.3.refs_5_), channel_id=1, source_target_pairs={{0,4},{1,5},{2,6},{3,7},{4,0},{5,1},{6,2},{7,3},{8,12},{9,13},{10,... | collective-permute-start | bytes 774152 | tf_op jit(solution)/shard_map/ppermute | solution.py:87
  18.9 2.6 %collective-permute-start.5 = (f32[7,4,8,128]{3,2,1,0:T(8,128)S(1)}, f32[7,4,8,128]{3,2,1,0:T(8,128)S(1)}, u32[]{:S(2)}, u32[]{:S(2)}) collective-permute-start(f32[7,4,8,128]{3,2,1,0:T(8,128)S(1)} %copy-done.1), channel_id=1, source_target_pairs={{0,4},{1,5},{2,6},{3,7},{4,0},{5,1},{6,2},{7,3},{8,12},{9,13},{10,... | collective-permute-start | bytes 344072 | tf_op jit(solution)/shard_map/ppermute | solution.py:87
  18.9 1.3 %collective-permute-start.6 = (s32[4,8,128]{2,1,0:T(8,128)S(1)}, s32[4,8,128]{2,1,0:T(8,128)S(1)}, u32[]{:S(2)}, u32[]{:S(2)}) collective-permute-start(s32[4,8,128]{2,1,0:T(8,128)S(1)} %copy-done.2), channel_id=1, source_target_pairs={{0,4},{1,5},{2,6},{3,7},{4,0},{5,1},{6,2},{7,3},{8,12},{9,13},{10,... | collective-permute-start | bytes 49160 | tf_op jit(solution)/shard_map/ppermute | solution.py:87
  20.2 1.3 %collective-permute-start.7 = (f32[14,8,128]{2,1,0:T(8,128)S(1)}, f32[14,8,128]{2,1,0:T(8,128)S(1)}, u32[]{:S(2)}, u32[]{:S(2)}) collective-permute-start(f32[14,8,128]{2,1,0:T(8,128)S(1)} %get-tuple-element.9.refs_3_), channel_id=1, source_target_pairs={{0,4},{1,5},{2,6},{3,7},{4,0},{5,1},{6,2},{7,3},{8,12},{9,13},{10,... | collective-permute-start | bytes 172040 | tf_op jit(solution)/shard_map/ppermute | solution.py:87

commit v3 on v2

--- a/solution.py
+++ b/solution.py
@@ -4,6 +4,7 @@
 from jax.experimental import pallas as pl
 from jax.experimental.pallas import tpu as pltpu
 from jax.sharding import PartitionSpec as P
+
 
 AXES = ("gx", "gy", "gz")
 
@@ -40,6 +41,7 @@
 
 IN_F = [1, 7, 9, 11, 13]
 IN_G = 1
+NV = NP + 1
 L_G2 = 0
 L_F2 = L_G2 + NG
 L_RHO2 = L_F2 + len(IN_F)
@@ -49,7 +51,7 @@
 L_UX3 = L_PH3 + 1
 L_PH4 = L_UX3 + 1
 L_MASK = L_PH4 + 1
-L_STRIP = L_MASK + 3
+N_FACE = L_MASK + 2
 
 
 def pairing(sizes, axis, first):
@@ -198,22 +200,27 @@
     return pltpu.roll(value, shift, axis=dim) if shift else value
 
 
-def pack_z_kernel(flow, phase, mask, out_a, out_b):
-    cx, cy, cz = mask.shape
+def load_kernel(flow, phase, mask, own, out_a, out_b, mask_in, sem):
+    _, cx, cy, cz = own.shape
+    copies = [
+        pltpu.make_async_copy(flow, own.at[pl.ds(0, NF)], sem.at[0]),
+        pltpu.make_async_copy(phase, own.at[pl.ds(NF, NG)], sem.at[1]),
+        pltpu.make_async_copy(mask, mask_in, sem.at[2]),
+    ]
+    for one in copies:
+        one.start()
+    for one in copies:
+        one.wait()
+    own[NP] = mask_in[...].astype(jnp.float32)
     even = lax.axis_index("gz") % 2 == 0
     group = lax.broadcasted_iota(jnp.int32, (cy, cz), 1) // HALO
     per = cz // (cx * HALO)
     for block in range(out_a.shape[0]):
         low = jnp.zeros((cy, cz), jnp.float32)
         high = low
-        for field in range(block * per, min((block + 1) * per, NP + 1)):
+        for field in range(block * per, min((block + 1) * per, NV)):
             for x in range(cx):
-                if field < NF:
-                    value = flow[field, x]
-                elif field < NP:
-                    value = phase[field - NF, x]
-                else:
-                    value = mask[x].astype(jnp.float32)
+                value = own[field, x]
                 slot = (field % per) * cx + x
                 here = group == slot
                 low = jnp.where(here, turn(value, slot * HALO, 1), low)
@@ -222,33 +229,53 @@
         out_b[block] = jnp.where(even, low, high)
 
 
-def pack_x_kernel(flow, phase, mask, z_a, z_b, strips, out_a, out_b, *, sizes):
-    cx, cy, cz = mask.shape
+def faces_kernel(own, out_a, out_b):
+    cx = own.shape[1]
+    even = lax.axis_index("gx") % 2 == 0
+    for out, up in ((out_a, even), (out_b, jnp.logical_not(even))):
+        other = jnp.where(up, 0, 1)
+        xs = [jnp.where(up, cx - 1 - d, d) for d in range(HALO)]
+        for field in range(NV):
+            out[field] = own[field, xs[0]]
+        for member in range(NG):
+            out[NV + L_G2 + member] = own[NF + member, xs[1]]
+        for slot, member in enumerate(IN_F):
+            out[NV + L_F2 + slot] = own[member + other, xs[1]]
+        rho, mom = moments([own[member, xs[1]] for member in range(NF)])
+        out[NV + L_RHO2] = rho
+        for d in range(3):
+            out[NV + L_MOM2 + d] = mom[d]
+        out[NV + L_G3] = own[NF + IN_G + other, xs[2]]
+        out[NV + L_PH3] = add_up([own[NF + member, xs[2]] for member in range(NG)])
+        rho, mom = moments([own[member, xs[2]] for member in range(NF)])
+        out[NV + L_UX3] = mom[0] / rho
+        far = add_up([own[NF + member, xs[3]] for member in range(NG)])
+        out[NV + L_PH4] = jnp.where(own[NP, xs[3]] == 1.0, far, 0.0)
+        for d in range(2):
+            out[NV + L_MASK + d] = own[NP, xs[1 + d]]
+
+
+def strips_kernel(own, z_a, z_b, strips, *, sizes):
+    _, cx, cy, cz = own.shape
     at_z = lax.axis_index("gz")
-    even_z = at_z % 2 == 0
-    even_x = lax.axis_index("gx") % 2 == 0
+    even = at_z % 2 == 0
     group = lax.broadcasted_iota(jnp.int32, (cy, cz), 1) // HALO
     per_in = cz // (cx * HALO)
     per_out = cz // (4 * cx * HALO)
-    below = [jnp.where(even_z, z_b[i], z_a[i]) for i in range(z_a.shape[0])]
-    above = [jnp.where(even_z, z_a[i], z_b[i]) for i in range(z_a.shape[0])]
+    below = [jnp.where(even, z_b[i], z_a[i]) for i in range(z_a.shape[0])]
+    above = [jnp.where(even, z_a[i], z_b[i]) for i in range(z_a.shape[0])]
     has_below = at_z > 0
     has_above = at_z < sizes["gz"] - 1
     for block in range(strips.shape[0]):
         total = jnp.zeros((cy, cz), jnp.float32)
-        for field in range(block * per_out, min((block + 1) * per_out, NP + 1)):
+        for field in range(block * per_out, min((block + 1) * per_out, NV)):
             from_below = below[field // per_in]
             from_above = above[field // per_in]
             if field == NP:
                 from_below = jnp.where(has_below, from_below, 0.0)
                 from_above = jnp.where(has_above, from_above, 0.0)
             for x in range(cx):
-                if field < NF:
-                    value = flow[field, x]
-                elif field < NP:
-                    value = phase[field - NF, x]
-                else:
-                    value = mask[x].astype(jnp.float32)
+                value = own[field, x]
                 came = (field % per_in) * cx + x
                 base = (field % per_out) * 4 * cx
                 for piece, origin, slot in (
@@ -261,38 +288,13 @@
                         group == slot, turn(piece, (slot - origin) * HALO, 1), total
                     )
         strips[block] = total
-        out_a[NP + L_STRIP + block] = total
-        out_b[NP + L_STRIP + block] = total
-
-    for out, up in ((out_a, even_x), (out_b, jnp.logical_not(even_x))):
-        other = jnp.where(up, 0, 1)
-        xs = [jnp.where(up, cx - 1 - d, d) for d in range(HALO)]
-        for member in range(NF):
-            out[member] = flow[member, xs[0]]
-        for member in range(NG):
-            out[NF + member] = phase[member, xs[0]]
-            out[NP + L_G2 + member] = phase[member, xs[1]]
-        for slot, member in enumerate(IN_F):
-            out[NP + L_F2 + slot] = flow[member + other, xs[1]]
-        rho, mom = moments([flow[member, xs[1]] for member in range(NF)])
-        out[NP + L_RHO2] = rho
-        for d in range(3):
-            out[NP + L_MOM2 + d] = mom[d]
-        out[NP + L_G3] = phase[IN_G + other, xs[2]]
-        out[NP + L_PH3] = add_up([phase[member, xs[2]] for member in range(NG)])
-        rho, mom = moments([flow[member, xs[2]] for member in range(NF)])
-        out[NP + L_UX3] = mom[0] / rho
-        far = add_up([phase[member, xs[3]] for member in range(NG)])
-        out[NP + L_PH4] = jnp.where(mask[xs[3]] == 1, far, 0.0)
-        for d in range(3):
-            out[NP + L_MASK + d] = mask[xs[d]].astype(jnp.float32)
 
 
 def steps_kernel(
-    flow, phase, mask, strips, x_a, x_b,
-    flow_y, phase_y, mask_y, strips_y, x_a_y, x_b_y,
+    own, x_a, x_b, strips, far_a, far_b,
+    own_y, x_a_y, x_b_y, strips_y, far_a_y, far_b_y,
     flow_out, phase_out,
-    pops, face, own_mask, own_strips, fluid, potential,
+    pops, face, own_strips, far_strips, fluid, potential,
     strip_pops, strip_fluid, strip_phase, moved, stayed, strip_moved, strip_stayed,
     phase_pops, potential1, moved1, stayed1, sem,
     *, sizes,
@@ -312,18 +314,17 @@
         one.start()
         copies.append(one)
 
-    for at, (f, g, m, s, a, b) in (
-        (0, (flow, phase, mask, strips, x_a, x_b)),
-        (cy, (flow_y, phase_y, mask_y, strips_y, x_a_y, x_b_y)),
+    for at, (o, a, b, s, fa, fb) in (
+        (0, (own, x_a, x_b, strips, far_a, far_b)),
+        (cy, (own_y, x_a_y, x_b_y, strips_y, far_a_y, far_b_y)),
     ):
         part = pl.ds(at, cy)
-        copy(f, pops.at[pl.ds(0, NF), pl.ds(1, cx), part])
-        copy(g, pops.at[pl.ds(NF, NG), pl.ds(1, cx), part])
-        copy(m, own_mask.at[:, part])
+        copy(o, pops.at[:, pl.ds(1, cx), part])
         copy(s, own_strips.at[:, part])
-        for got, side in ((a, side_a), (b, side_b)):
-            copy(got.at[pl.ds(0, NP)], pops.at[:, side * (cx + 1), part])
-            copy(got.at[pl.ds(NP, face.shape[1])], face.at[side, :, part])
+        for got, far, side in ((a, fa, side_a), (b, fb, side_b)):
+            copy(got.at[pl.ds(0, NV)], pops.at[:, side * (cx + 1), part])
+            copy(got.at[pl.ds(NV, N_FACE)], face.at[side, :, part])
+            copy(far, far_strips.at[side, :, part])
     for one in copies:
         one.wait()
 
@@ -343,7 +344,7 @@
         return first - depth if side == 0 else last + depth
 
     for x in range(cx):
-        ok = (own_mask[x] == 1) & row_ok
+        ok = (pops[NP, 1 + x] == 1.0) & row_ok
         fluid[first + x] = ok.astype(jnp.float32)
         total = add_up([pops[NF + member, 1 + x] for member in range(NG)])
         potential[first + x] = jnp.where(ok, total, 0.0)
@@ -358,7 +359,11 @@
                 total = face[side, L_PH3 if depth == 3 else L_PH4]
             ok = side_ok
             if depth < HALO:
-                ok = ok & (face[side, L_MASK + depth - 1] == 1.0)
+                if depth == 1:
+                    known = pops[NP, side * (cx + 1)]
+                else:
+                    known = face[side, L_MASK + depth - 2]
+                ok = ok & (known == 1.0)
                 fluid[at_depth(side, depth)] = ok.astype(jnp.float32)
             potential[at_depth(side, depth)] = jnp.where(ok, total, 0.0)
 
@@ -371,12 +376,12 @@
         | ((lane >= 2 * wide) & (lane < 3 * wide) & has_right)
     )
     for side in range(2):
-        for field in range(NP + 1):
+        for field in range(NV):
             block = field // per
             origin = ((field % per) * 2 + side) * wide
-            left = turn(face[0, L_STRIP + block], -origin, 1)
+            left = turn(far_strips[0, block], -origin, 1)
             mine = turn(own_strips[block], wide - origin, 1)
-            right = turn(face[1, L_STRIP + block], 2 * wide - origin, 1)
+            right = turn(far_strips[1, block], 2 * wide - origin, 1)
             value = jnp.where(lane < wide, left, jnp.where(lane < 2 * wide, mine, right))
             if field < NP:
                 strip_pops[side, field] = value
@@ -556,55 +561,62 @@
     def near(*arrays):
         return [pltpu.with_memory_space_constraint(a, pltpu.VMEM) for a in arrays]
 
-    flow_y = beside(sizes, flow_pops)
-    phase_y = beside(sizes, phase_pops)
-    mask_y = beside(sizes, pore_mask)
-
-    z_blocks = pl.cdiv(NP + 1, cz // (cx * HALO))
+    def call(kernel, out_shape, in_specs, args, scratch=()):
+        return pl.pallas_call(
+            kernel,
+            out_shape=out_shape,
+            in_specs=in_specs,
+            out_specs=jax.tree.map(lambda _: vmem, out_shape),
+            scratch_shapes=scratch,
+        )(*args)
+
+    z_blocks = pl.cdiv(NV, cz // (cx * HALO))
     z_shape = pltpu.VMEM((z_blocks, cy, cz), f32)
-    z_a, z_b = pl.pallas_call(
-        pack_z_kernel,
-        out_shape=(z_shape, z_shape),
-        in_specs=[vmem] * 3,
-        out_specs=(vmem, vmem),
-        name="pack_z",
-    )(*near(flow_pops, phase_pops, pore_mask))
+    own, z_a, z_b = call(
+        load_kernel, (pltpu.VMEM((NV, cx, cy, cz), f32), z_shape, z_shape),
+        [anywhere] * 3, (flow_pops, phase_pops, pore_mask),
+        [pltpu.VMEM(pore_mask.shape, jnp.int32), pltpu.SemaphoreType.DMA((3,))],
+    )
     z_a, z_b = swap(sizes, "gz", z_a, z_b)
 
-    strip_blocks = pl.cdiv(NP + 1, cz // (4 * cx * HALO))
-    strip_shape = pltpu.VMEM((strip_blocks, cy, cz), f32)
-    x_layers = NP + L_STRIP + strip_blocks
-    x_shape = pltpu.VMEM((x_layers, cy, cz), f32)
-    strips, x_a, x_b = pl.pallas_call(
-        lambda *refs: pack_x_kernel(*refs, sizes=sizes),
-        out_shape=(strip_shape, x_shape, x_shape),
-        in_specs=[vmem] * 5,
-        out_specs=(vmem,) * 3,
-        name="pack_x",
-    )(*near(flow_pops, phase_pops, pore_mask, z_a, z_b))
-    strips_y = beside(sizes, strips)
+    x_shape = pltpu.VMEM((NV + N_FACE, cy, cz), f32)
+    x_a, x_b = call(faces_kernel, (x_shape, x_shape), [vmem], near(own))
     x_a, x_b = swap(sizes, "gx", x_a, x_b)
+    own_y = beside(sizes, own)
     x_a_y = beside(sizes, x_a)
     x_b_y = beside(sizes, x_b)
 
+    strip_blocks = pl.cdiv(NV, cz // (4 * cx * HALO))
+    strips = call(
+        lambda *refs: strips_kernel(*refs, sizes=sizes),
+        pltpu.VMEM((strip_blocks, cy, cz), f32), [vmem] * 3, near(own, z_a, z_b),
+    )
+    strips_y = beside(sizes, strips)
+    far_a, far_b = swap(sizes, "gx", strips, strips)
+    far_a_y = beside(sizes, far_a)
+    far_b_y = beside(sizes, far_b)
+
     deep = cx + 2 * HALO
 
     def block(*lead):
         return pltpu.VMEM((*lead, rows, cz), f32)
 
-    return pl.pallas_call(
+    return call(
         lambda *refs: steps_kernel(*refs, sizes=sizes),
-        out_shape=(
+        (
             jax.ShapeDtypeStruct(flow_pops.shape, f32),
             jax.ShapeDtypeStruct(phase_pops.shape, f32),
         ),
-        in_specs=[anywhere] * 12,
-        out_specs=(vmem, vmem),
-        scratch_shapes=[
-            block(NP, cx + 2),
-            block(2, L_STRIP + strip_blocks),
-            pltpu.VMEM((cx, rows, cz), jnp.int32),
+        [anywhere] * 12,
+        near(
+            own, x_a, x_b, strips, far_a, far_b,
+            own_y, x_a_y, x_b_y, strips_y, far_a_y, far_b_y,
+        ),
+        [
+            block(NV, cx + 2),
+            block(2, N_FACE),
             block(strip_blocks),
+            block(2, strip_blocks),
             block(deep),
             block(deep),
             block(2, NP),
@@ -620,12 +632,6 @@
             block(NP, deep),
             pltpu.SemaphoreType.DMA((16,)),
         ],
-        name="two_steps",
-    )(
-        *near(
-            flow_pops, phase_pops, pore_mask, strips, x_a, x_b,
-            flow_y, phase_y, mask_y, strips_y, x_a_y, x_b_y,
-        )
     )
 
 

time: 26.7 us -> 30.1 us (1.13); the launches traced: 26.5 us -> 29.5 us
  waiting for transfers between devices: 7.02 us -> 12.4 us
  local copies, waits for them, and re-layouts: 2.58 us -> 0 us
  Pallas kernels: 5.77 us -> 6.83 us
  starting transfers between devices: 10.4 us -> 9.61 us
    ppermute x2 -> x3, waiting for transfers between devices: 3.17 us -> 6.39 us  [swap(): got_a = lax.ppermute(send_a, AXES, perm_a) if perm_a else send_a]
    unnamed x6 -> x0, local copies, waits for them, and re-layouts: 2.58 us -> none
    ppermute x2 -> x3, waiting for transfers between devices: 2.11 us -> 4.22 us  [swap(): got_b = lax.ppermute(send_b, AXES, perm_b) if perm_b else got_a]
    ppermute x6, starting transfers between devices: 7.6 us -> 6.33 us  [beside(): return lax.ppermute(cells, AXES, perm) if perm else cells]
    pallas_call x3 -> x4, Pallas kernels: 5.77 us -> 6.83 us  [call(): pl.pallas_call(kernel, out_shape=out_shape, in_specs=in_specs, out_specs=...]
    ppermute x2 -> x3, starting transfers between devices: 2.64 us -> 3.08 us  [swap(): got_a = lax.ppermute(send_a, AXES, perm_a) if perm_a else send_a]
  transfers between devices with their start and end apart: 10 -> 12, of which waited for: 5 -> 7; matrix products, arithmetic and copies ran while one was open for 0% -> 0% of each run, Pallas kernels for 0% -> 2%
where the time goes in v3:
time: 30.1 us; the launch traced here: 29.5 us
  waiting for transfers between devices  12.4 us (41%)
  starting transfers between devices  9.61 us (32%)
  Pallas kernels  6.83 us (23%)
  between operations  0.66 us (2%)
    pallas_call x4, Pallas kernels, call(): pl.pallas_call(kernel, out_shape=out_shape, in_specs=in_specs, out_specs=...  6.83 us
    ppermute x3, waiting for transfers between devices, swap(): got_a = lax.ppermute(send_a, AXES, perm_a) if perm_a else send_a  6.39 us
    ppermute x6, starting transfers between devices, beside(): return lax.ppermute(cells, AXES, perm) if perm else cells  6.33 us
    ppermute x3, waiting for transfers between devices, swap(): got_b = lax.ppermute(send_b, AXES, perm_b) if perm_b else got_a  4.22 us
    ppermute x3, starting transfers between devices, swap(): got_a = lax.ppermute(send_a, AXES, perm_a) if perm_a else send_a  3.08 us
    ppermute x6, waiting for transfers between devices, beside(): return lax.ppermute(cells, AXES, perm) if perm else cells  1.79 us
  transfers between devices with their start and end apart: 12, of which 7 were waited for; matrix products, arithmetic and copies ran while one was open for 0% of the time, Pallas kernels for 2%

profile of v3, /device:TPU:21, one launch (start us, length us, event | category | flops | bytes accessed | tf_op | source)
XLA Modules:
  0.0 29.5 jit_solution(9554617294130913813)
XLA Ops:
  0.6 1.3 %shard_map.50 = (f32[27,4,8,128]{3,2,1,0:T(8,128)S(1)}, f32[4,8,128]{2,1,0:T(8,128)S(1)}, f32[4,8,128]{2,1,0:T(8,128)S(1)}) custom-call(f32[19,4,8,128]{3,2,1,0:T(8,128)} %flow.1, f32[7,4,8,128]{3,2,1,0:T(8,128)} %phase.1, s32[4,8,128]{2,1,0:T(8,128)} %mask.1), custom_call_target="tpu_custom_call" | custom-call | tf_op jit(solution)/shard_map/pallas_call | solution.py:565
  1.9 0.7 %collective-permute-start.6 = (f32[27,4,8,128]{3,2,1,0:T(8,128)S(1)}, f32[27,4,8,128]{3,2,1,0:T(8,128)S(1)}, u32[]{:S(2)}, u32[]{:S(2)}) collective-permute-start(f32[27,4,8,128]{3,2,1,0:T(8,128)S(1)} %get-tuple-element.7.own.refs_0_), channel_id=1, source_target_pairs={{0,4},{1,5},{2,6},{3,7},{4,0},{5,1},{6,2},{7,3},{8,12},{9,13},{10,... | collective-permute-start | bytes 1327112 | tf_op jit(solution)/shard_map/ppermute | solution.py:89
  2.7 0.1 shard_map.51
  2.8 1.4 %collective-permute-start = (f32[49,8,128]{2,1,0:T(8,128)S(1)}, f32[49,8,128]{2,1,0:T(8,128)S(1)}, u32[]{:S(2)}, u32[]{:S(2)}) collective-permute-start(f32[49,8,128]{2,1,0:T(8,128)S(1)} %get-tuple-element.8), channel_id=1, source_target_pairs={{0,8},{1,9},{2,10},{3,11},{4,12},{5,13},{6,14},{7,15},{8,0},{9,1},... | collective-permute-start | bytes 602120 | tf_op jit(solution)/shard_map/ppermute | solution.py:81
  4.1 0.0 collective-permute-start.1
  4.1 5.2 %collective-permute-done.refs_1_ = f32[49,8,128]{2,1,0:T(8,128)S(1)} collective-permute-done((f32[49,8,128]{2,1,0:T(8,128)S(1)}, f32[49,8,128]{2,1,0:T(8,128)S(1)}, u32[]{:S(2)}, u32[]{:S(2)}) %collective-permute-start) | collective-permute-done | bytes 200736 | tf_op jit(solution)/shard_map/ppermute | solution.py:81
  9.3 0.9 %collective-permute-start.7 = (f32[49,8,128]{2,1,0:T(8,128)S(1)}, f32[49,8,128]{2,1,0:T(8,128)S(1)}, u32[]{:S(2)}, u32[]{:S(2)}) collective-permute-start(f32[49,8,128]{2,1,0:T(8,128)S(1)} %collective-permute-done.refs_1_), channel_id=1, source_target_pairs={{0,4},{1,5},{2,6},{3,7},{4,0},{5,1},{6,2},{7,3},{8,12},{9,13},{10,... | collective-permute-start | bytes 602120 | tf_op jit(solution)/shard_map/ppermute | solution.py:89
  10.2 0.1 collective-permute-done.1.refs_2_
  10.3 1.2 %collective-permute-start.8 = (f32[49,8,128]{2,1,0:T(8,128)S(1)}, f32[49,8,128]{2,1,0:T(8,128)S(1)}, u32[]{:S(2)}, u32[]{:S(2)}) collective-permute-start(f32[49,8,128]{2,1,0:T(8,128)S(1)} %collective-permute-done.1.refs_2_), channel_id=1, source_target_pairs={{0,4},{1,5},{2,6},{3,7},{4,0},{5,1},{6,2},{7,3},{8,12},{9,13},{10,... | collective-permute-start | bytes 602120 | tf_op jit(solution)/shard_map/ppermute | solution.py:89
  11.5 1.2 %collective-permute-start.2 = (f32[4,8,128]{2,1,0:T(8,128)S(1)}, f32[4,8,128]{2,1,0:T(8,128)S(1)}, u32[]{:S(2)}, u32[]{:S(2)}) collective-permute-start(f32[4,8,128]{2,1,0:T(8,128)S(1)} %get-tuple-element.10), channel_id=1, source_target_pairs={{0,1},{1,0},{2,3},{3,2},{4,5},{5,4},{6,7},{7,6},{8,9},{9,8},{10,11... | collective-permute-start | bytes 49160 | tf_op jit(solution)/shard_map/ppermute | solution.py:81
  12.7 0.2 collective-permute-start.3
  12.9 1.2 %collective-permute-done.2.refs_1_ = f32[4,8,128]{2,1,0:T(8,128)S(1)} collective-permute-done((f32[4,8,128]{2,1,0:T(8,128)S(1)}, f32[4,8,128]{2,1,0:T(8,128)S(1)}, u32[]{:S(2)}, u32[]{:S(2)}) %collective-permute-start.2) | collective-permute-done | bytes 16416 | tf_op jit(solution)/shard_map/ppermute | solution.py:81
  14.1 2.1 %collective-permute-done.3.refs_2_ = f32[4,8,128]{2,1,0:T(8,128)S(1)} collective-permute-done((f32[4,8,128]{2,1,0:T(8,128)S(1)}, f32[4,8,128]{2,1,0:T(8,128)S(1)}, u32[]{:S(2)}, u32[]{:S(2)}) %collective-permute-start.3) | collective-permute-done | bytes 16416 | tf_op jit(solution)/shard_map/ppermute | solution.py:82
  16.2 0.5 %shard_map.52.refs_3_ = f32[14,8,128]{2,1,0:T(8,128)S(1)} custom-call(f32[27,4,8,128]{3,2,1,0:T(8,128)S(1)} %get-tuple-element.7.own.refs_0_, f32[4,8,128]{2,1,0:T(8,128)S(1)} %collective-permute-done.2.refs_1_, f32[4,8,128]{2,1,0:T(8,128)S(1)} %collective-permute-done.3.refs_2_), custom_call_target="tpu_custom_call" | custom-call | tf_op jit(solution)/shard_map/pallas_call | solution.py:565
  16.7 1.5 %collective-permute-start.9 = (f32[14,8,128]{2,1,0:T(8,128)S(1)}, f32[14,8,128]{2,1,0:T(8,128)S(1)}, u32[]{:S(2)}, u32[]{:S(2)}) collective-permute-start(f32[14,8,128]{2,1,0:T(8,128)S(1)} %shard_map.52.refs_3_), channel_id=1, source_target_pairs={{0,4},{1,5},{2,6},{3,7},{4,0},{5,1},{6,2},{7,3},{8,12},{9,13},{10,... | collective-permute-start | bytes 172040 | tf_op jit(solution)/shard_map/ppermute | solution.py:89
  18.2 0.0 collective-permute-start.5
  18.2 0.9 %collective-permute-done.9.refs_9_ = f32[14,8,128]{2,1,0:T(8,128)S(1)} collective-permute-done((f32[14,8,128]{2,1,0:T(8,128)S(1)}, f32[14,8,128]{2,1,0:T(8,128)S(1)}, u32[]{:S(2)}, u32[]{:S(2)}) %collective-permute-start.9) | collective-permute-done | bytes 57376 | tf_op jit(solution)/shard_map/ppermute | solution.py:89
  19.1 0.5 %collective-permute-start.4 = (f32[14,8,128]{2,1,0:T(8,128)S(1)}, f32[14,8,128]{2,1,0:T(8,128)S(1)}, u32[]{:S(2)}, u32[]{:S(2)}) collective-permute-start(f32[14,8,128]{2,1,0:T(8,128)S(1)} %shard_map.52.refs_3_), channel_id=1, source_target_pairs={{0,8},{1,9},{2,10},{3,11},{4,12},{5,13},{6,14},{7,15},{8,0},{9,1},... | collective-permute-start | bytes 172040 | tf_op jit(solution)/shard_map/ppermute | solution.py:81
  19.6 2.0 %collective-permute-done.5.refs_5_ = f32[14,8,128]{2,1,0:T(8,128)S(1)} collective-permute-done((f32[14,8,128]{2,1,0:T(8,128)S(1)}, f32[14,8,128]{2,1,0:T(8,128)S(1)}, u32[]{:S(2)}, u32[]{:S(2)}) %collective-permute-start.5) | collective-permute-done | bytes 57376 | tf_op jit(solution)/shard_map/ppermute | solution.py:82
  21.6 0.9 %collective-permute-start.11 = (f32[14,8,128]{2,1,0:T(8,128)S(1)}, f32[14,8,128]{2,1,0:T(8,128)S(1)}, u32[]{:S(2)}, u32[]{:S(2)}) collective-permute-start(f32[14,8,128]{2,1,0:T(8,128)S(1)} %collective-permute-done.5.refs_5_), channel_id=1, source_target_pairs={{0,4},{1,5},{2,6},{3,7},{4,0},{5,1},{6,2},{7,3},{8,12},{9,13},{10,... | collective-permute-start | bytes 172040 | tf_op jit(solution)/shard_map/ppermute | solution.py:89
  22.6 0.0 collective-permute-done.4.refs_4_
  22.6 1.1 %collective-permute-start.10 = (f32[14,8,128]{2,1,0:T(8,128)S(1)}, f32[14,8,128]{2,1,0:T(8,128)S(1)}, u32[]{:S(2)}, u32[]{:S(2)}) collective-permute-start(f32[14,8,128]{2,1,0:T(8,128)S(1)} %collective-permute-done.4.refs_4_), channel_id=1, source_target_pairs={{0,4},{1,5},{2,6},{3,7},{4,0},{5,1},{6,2},{7,3},{8,12},{9,13},{10,... | collective-permute-start | bytes 172040 | tf_op jit(solution)/shard_map/ppermute | solution.py:89
  23.7 0.0 collective-permute-done.11.refs_11_
  23.7 0.9 %collective-permute-done.10.refs_10_ = f32[14,8,128]{2,1,0:T(8,128)S(1)} collective-permute-done((f32[14,8,128]{2,1,0:T(8,128)S(1)}, f32[14,8,128]{2,1,0:T(8,128)S(1)}, u32[]{:S(2)}, u32[]{:S(2)}) %collective-permute-start.10) | collective-permute-done | bytes 57376 | tf_op jit(solution)/shard_map/ppermute | solution.py:89
  24.6 0.0 collective-permute-done.7.refs_7_
  24.6 0.0 collective-permute-done.8.refs_8_
  24.6 0.0 collective-permute-done.6.refs_6_
  24.6 4.9 %shard_map.53 = (f32[19,4,8,128]{3,2,1,0:T(8,128)}, f32[7,4,8,128]{3,2,1,0:T(8,128)}) custom-call(f32[27,4,8,128]{3,2,1,0:T(8,128)S(1)} %get-tuple-element.7.own.refs_0_, f32[49,8,128]{2,1,0:T(8,128)S(1)} %collective-permute-done.refs_1_, f32[49,8,128]{2,1,0:T(8,128)S(1)} %collective-permute-done.1.refs_2_, f32[14,8,128]{2,1,0:T(8,128)S(1)} %shard_map.52.refs_3_, ...), custom_call_target="tpu_custom_call" | custom-call | tf_op jit(solution)/shard_map/pallas_call | solution.py:565
Async XLA Ops:
  1.9 22.6 %collective-permute-start.6 = (f32[27,4,8,128]{3,2,1,0:T(8,128)S(1)}, f32[27,4,8,128]{3,2,1,0:T(8,128)S(1)}, u32[]{:S(2)}, u32[]{:S(2)}) collective-permute-start(f32[27,4,8,128]{3,2,1,0:T(8,128)S(1)} %get-tuple-element.7.own.refs_0_), channel_id=1, source_target_pairs={{0,4},{1,5},{2,6},{3,7},{4,0},{5,1},{6,2},{7,3},{8,12},{9,13},{10,... | collective-permute-start | bytes 1327112 | tf_op jit(solution)/shard_map/ppermute | solution.py:89
  2.8 6.6 %collective-permute-start = (f32[49,8,128]{2,1,0:T(8,128)S(1)}, f32[49,8,128]{2,1,0:T(8,128)S(1)}, u32[]{:S(2)}, u32[]{:S(2)}) collective-permute-start(f32[49,8,128]{2,1,0:T(8,128)S(1)} %get-tuple-element.8), channel_id=1, source_target_pairs={{0,8},{1,9},{2,10},{3,11},{4,12},{5,13},{6,14},{7,15},{8,0},{9,1},... | collective-permute-start | bytes 602120 | tf_op jit(solution)/shard_map/ppermute | solution.py:81
  4.1 6.2 %collective-permute-start.1 = (f32[49,8,128]{2,1,0:T(8,128)S(1)}, f32[49,8,128]{2,1,0:T(8,128)S(1)}, u32[]{:S(2)}, u32[]{:S(2)}) collective-permute-start(f32[49,8,128]{2,1,0:T(8,128)S(1)} %get-tuple-element.9), channel_id=1, source_target_pairs={{0,4},{1,5},{2,6},{3,7},{4,0},{5,1},{6,2},{7,3},{8,16},{9,17},{10,... | collective-permute-start | bytes 602120 | tf_op jit(solution)/shard_map/ppermute | solution.py:82
  9.3 15.2 %collective-permute-start.7 = (f32[49,8,128]{2,1,0:T(8,128)S(1)}, f32[49,8,128]{2,1,0:T(8,128)S(1)}, u32[]{:S(2)}, u32[]{:S(2)}) collective-permute-start(f32[49,8,128]{2,1,0:T(8,128)S(1)} %collective-permute-done.refs_1_), channel_id=1, source_target_pairs={{0,4},{1,5},{2,6},{3,7},{4,0},{5,1},{6,2},{7,3},{8,12},{9,13},{10,... | collective-permute-start | bytes 602120 | tf_op jit(solution)/shard_map/ppermute | solution.py:89
  10.3 14.2 %collective-permute-start.8 = (f32[49,8,128]{2,1,0:T(8,128)S(1)}, f32[49,8,128]{2,1,0:T(8,128)S(1)}, u32[]{:S(2)}, u32[]{:S(2)}) collective-permute-start(f32[49,8,128]{2,1,0:T(8,128)S(1)} %collective-permute-done.1.refs_2_), channel_id=1, source_target_pairs={{0,4},{1,5},{2,6},{3,7},{4,0},{5,1},{6,2},{7,3},{8,12},{9,13},{10,... | collective-permute-start | bytes 602120 | tf_op jit(solution)/shard_map/ppermute | solution.py:89
  11.5 2.6 %collective-permute-start.2 = (f32[4,8,128]{2,1,0:T(8,128)S(1)}, f32[4,8,128]{2,1,0:T(8,128)S(1)}, u32[]{:S(2)}, u32[]{:S(2)}) collective-permute-start(f32[4,8,128]{2,1,0:T(8,128)S(1)} %get-tuple-element.10), channel_id=1, source_target_pairs={{0,1},{1,0},{2,3},{3,2},{4,5},{5,4},{6,7},{7,6},{8,9},{9,8},{10,11... | collective-permute-start | bytes 49160 | tf_op jit(solution)/shard_map/ppermute | solution.py:81
  12.7 3.5 %collective-permute-start.3 = (f32[4,8,128]{2,1,0:T(8,128)S(1)}, f32[4,8,128]{2,1,0:T(8,128)S(1)}, u32[]{:S(2)}, u32[]{:S(2)}) collective-permute-start(f32[4,8,128]{2,1,0:T(8,128)S(1)} %get-tuple-element.11), channel_id=1, source_target_pairs={{0,4},{1,2},{2,1},{3,7},{4,0},{5,6},{6,5},{7,3},{8,12},{9,10},{10,... | collective-permute-start | bytes 49160 | tf_op jit(solution)/shard_map/ppermute | solution.py:82
  16.7 2.4 %collective-permute-start.9 = (f32[14,8,128]{2,1,0:T(8,128)S(1)}, f32[14,8,128]{2,1,0:T(8,128)S(1)}, u32[]{:S(2)}, u32[]{:S(2)}) collective-permute-start(f32[14,8,128]{2,1,0:T(8,128)S(1)} %shard_map.52.refs_3_), channel_id=1, source_target_pairs={{0,4},{1,5},{2,6},{3,7},{4,0},{5,1},{6,2},{7,3},{8,12},{9,13},{10,... | collective-permute-start | bytes 172040 | tf_op jit(solution)/shard_map/ppermute | solution.py:89
  18.2 3.4 %collective-permute-start.5 = (f32[14,8,128]{2,1,0:T(8,128)S(1)}, f32[14,8,128]{2,1,0:T(8,128)S(1)}, u32[]{:S(2)}, u32[]{:S(2)}) collective-permute-start(f32[14,8,128]{2,1,0:T(8,128)S(1)} %shard_map.52.refs_3_), channel_id=1, source_target_pairs={{0,4},{1,5},{2,6},{3,7},{4,0},{5,1},{6,2},{7,3},{8,16},{9,17},{10,... | collective-permute-start | bytes 172040 | tf_op jit(solution)/shard_map/ppermute | solution.py:82
  19.1 3.4 %collective-permute-start.4 = (f32[14,8,128]{2,1,0:T(8,128)S(1)}, f32[14,8,128]{2,1,0:T(8,128)S(1)}, u32[]{:S(2)}, u32[]{:S(2)}) collective-permute-start(f32[14,8,128]{2,1,0:T(8,128)S(1)} %shard_map.52.refs_3_), channel_id=1, source_target_pairs={{0,8},{1,9},{2,10},{3,11},{4,12},{5,13},{6,14},{7,15},{8,0},{9,1},... | collective-permute-start | bytes 172040 | tf_op jit(solution)/shard_map/ppermute | solution.py:81
  21.6 2.0 %collective-permute-start.11 = (f32[14,8,128]{2,1,0:T(8,128)S(1)}, f32[14,8,128]{2,1,0:T(8,128)S(1)}, u32[]{:S(2)}, u32[]{:S(2)}) collective-permute-start(f32[14,8,128]{2,1,0:T(8,128)S(1)} %collective-permute-done.5.refs_5_), channel_id=1, source_target_pairs={{0,4},{1,5},{2,6},{3,7},{4,0},{5,1},{6,2},{7,3},{8,12},{9,13},{10,... | collective-permute-start | bytes 172040 | tf_op jit(solution)/shard_map/ppermute | solution.py:89
  22.6 2.0 %collective-permute-start.10 = (f32[14,8,128]{2,1,0:T(8,128)S(1)}, f32[14,8,128]{2,1,0:T(8,128)S(1)}, u32[]{:S(2)}, u32[]{:S(2)}) collective-permute-start(f32[14,8,128]{2,1,0:T(8,128)S(1)} %collective-permute-done.4.refs_4_), channel_id=1, source_target_pairs={{0,4},{1,5},{2,6},{3,7},{4,0},{5,1},{6,2},{7,3},{8,12},{9,13},{10,... | collective-permute-start | bytes 172040 | tf_op jit(solution)/shard_map/ppermute | solution.py:89

commit v4 on v3

--- a/solution.py
+++ b/solution.py
@@ -294,39 +294,21 @@
     own, x_a, x_b, strips, far_a, far_b,
     own_y, x_a_y, x_b_y, strips_y, far_a_y, far_b_y,
     flow_out, phase_out,
-    pops, face, own_strips, far_strips, fluid, potential,
+    face, fluid, potential,
     strip_pops, strip_fluid, strip_phase, moved, stayed, strip_moved, strip_stayed,
-    phase_pops, potential1, moved1, stayed1, sem,
+    phase_pops, potential1, moved1, stayed1, result, sem,
     *, sizes,
 ):
-    _, cx, cy, cz = flow_out.shape
+    _, cx, cy, cz = own.shape
     rows = 2 * cy
     at_x = lax.axis_index("gx")
     at_y = lax.axis_index("gy")
     even_x = at_x % 2 == 0
-    side_a = jnp.where(even_x, 1, 0)
-    side_b = 1 - side_a
-
-    copies = []
-
-    def copy(src, dst):
-        one = pltpu.make_async_copy(src, dst, sem.at[len(copies)])
-        one.start()
-        copies.append(one)
-
-    for at, (o, a, b, s, fa, fb) in (
-        (0, (own, x_a, x_b, strips, far_a, far_b)),
-        (cy, (own_y, x_a_y, x_b_y, strips_y, far_a_y, far_b_y)),
-    ):
-        part = pl.ds(at, cy)
-        copy(o, pops.at[:, pl.ds(1, cx), part])
-        copy(s, own_strips.at[:, part])
-        for got, far, side in ((a, fa, side_a), (b, fb, side_b)):
-            copy(got.at[pl.ds(0, NV)], pops.at[:, side * (cx + 1), part])
-            copy(got.at[pl.ds(NV, N_FACE)], face.at[side, :, part])
-            copy(far, far_strips.at[side, :, part])
-    for one in copies:
-        one.wait()
+    first, last = HALO, HALO + cx - 1
+    own_rows = pl.ds(0, cy)
+
+    def whole(cells, cells_y, *at):
+        return jnp.concatenate([cells[at], cells_y[at]], axis=0)
 
     lane = lax.broadcasted_iota(jnp.int32, (rows, cz), 1)
     row = lax.broadcasted_iota(jnp.int32, (rows, cz), 0)
@@ -338,34 +320,40 @@
     low_row = jnp.where(has_low, cy + HALO, rows)
     row_ok = (row < high_row) | (row >= low_row)
     has = (has_left, has_right)
-    first, last = HALO, HALO + cx - 1
 
     def at_depth(side, depth):
         return first - depth if side == 0 else last + depth
 
+    side_a = jnp.where(even_x, 1, 0)
+    ends = ((x_a, x_a_y, side_a), (x_b, x_b_y, 1 - side_a))
+
     for x in range(cx):
-        ok = (pops[NP, 1 + x] == 1.0) & row_ok
+        ok = (whole(own, own_y, NP, x) == 1.0) & row_ok
         fluid[first + x] = ok.astype(jnp.float32)
-        total = add_up([pops[NF + member, 1 + x] for member in range(NG)])
+        total = add_up([whole(own, own_y, NF + member, x) for member in range(NG)])
         potential[first + x] = jnp.where(ok, total, 0.0)
+    for got, got_y, side in ends:
+        for layer in range(N_FACE):
+            face[side, layer] = whole(got, got_y, NV + layer)
+        at = jnp.where(side == 0, first - 1, last + 1)
+        side_ok = row_ok & ((side == 0) & has_left | (side == 1) & has_right)
+        ok = side_ok & (whole(got, got_y, NP) == 1.0)
+        total = add_up([whole(got, got_y, NF + member) for member in range(NG)])
+        fluid[at] = ok.astype(jnp.float32)
+        potential[at] = jnp.where(ok, total, 0.0)
     for side in range(2):
         side_ok = row_ok & has[side]
-        for depth in range(1, HALO + 1):
-            if depth == 1:
-                total = add_up([pops[NF + m, side * (cx + 1)] for m in range(NG)])
-            elif depth == 2:
+        for depth in range(2, HALO + 1):
+            at = at_depth(side, depth)
+            ok = side_ok
+            if depth == 2:
                 total = add_up([face[side, L_G2 + m] for m in range(NG)])
             else:
                 total = face[side, L_PH3 if depth == 3 else L_PH4]
-            ok = side_ok
             if depth < HALO:
-                if depth == 1:
-                    known = pops[NP, side * (cx + 1)]
-                else:
-                    known = face[side, L_MASK + depth - 2]
-                ok = ok & (known == 1.0)
-                fluid[at_depth(side, depth)] = ok.astype(jnp.float32)
-            potential[at_depth(side, depth)] = jnp.where(ok, total, 0.0)
+                ok = ok & (face[side, L_MASK + depth - 2] == 1.0)
+                fluid[at] = ok.astype(jnp.float32)
+            potential[at] = jnp.where(ok, total, 0.0)
 
     cols = 2 * HALO
     wide = cols * cx
@@ -375,18 +363,28 @@
         | ((lane >= wide) & (lane < 2 * wide))
         | ((lane >= 2 * wide) & (lane < 3 * wide) & has_right)
     )
-    for side in range(2):
-        for field in range(NV):
-            block = field // per
-            origin = ((field % per) * 2 + side) * wide
-            left = turn(far_strips[0, block], -origin, 1)
-            mine = turn(own_strips[block], wide - origin, 1)
-            right = turn(far_strips[1, block], 2 * wide - origin, 1)
-            value = jnp.where(lane < wide, left, jnp.where(lane < 2 * wide, mine, right))
-            if field < NP:
-                strip_pops[side, field] = value
-            else:
-                strip_fluid[side] = jnp.where(block_ok, value, 0.0)
+    for block in range(strips.shape[0]):
+        mine = whole(strips, strips_y, block)
+        from_a = whole(far_a, far_a_y, block)
+        from_b = whole(far_b, far_b_y, block)
+        left = jnp.where(even_x, from_b, from_a)
+        right = jnp.where(even_x, from_a, from_b)
+        for field in range(block * per, min((block + 1) * per, NV)):
+            for side in range(2):
+                origin = ((field % per) * 2 + side) * wide
+                value = jnp.where(
+                    lane < wide,
+                    turn(left, -origin, 1),
+                    jnp.where(
+                        lane < 2 * wide,
+                        turn(mine, wide - origin, 1),
+                        turn(right, 2 * wide - origin, 1),
+                    ),
+                )
+                if field < NP:
+                    strip_pops[side, field] = value
+                else:
+                    strip_fluid[side] = jnp.where(block_ok, value, 0.0)
 
     def strip_grads(values):
         return (
@@ -418,21 +416,20 @@
             0.5 * (up - down),
         )
 
-    def push_main(member, value, ok, strip_source, at):
+    def push_z(member, value, strip_source, at, part):
         move = VEL[member]
-        value = jnp.where(ok, value, ROCK)
-        value = turn(value, move[1], 0)
+        size = value.shape[0]
         if move[2] > 0:
-            value = jnp.where(
-                lane == 0, strip_to_lane(0, strip_source[0, member], at + move[0]), turn(value, 1, 1)
-            )
-        elif move[2] < 0:
-            value = jnp.where(
-                lane == cz - 1,
-                strip_to_lane(1, strip_source[1, member], at + move[0]),
-                turn(value, -1, 1),
-            )
+            fill = strip_to_lane(0, strip_source[0, member, part], at + move[0])
+            return jnp.where(lane[:size] == 0, fill, turn(value, 1, 1))
+        if move[2] < 0:
+            fill = strip_to_lane(1, strip_source[1, member, part], at + move[0])
+            return jnp.where(lane[:size] == cz - 1, fill, turn(value, -1, 1))
         return value
+
+    def push_main(member, value, ok, at):
+        value = turn(jnp.where(ok, value, ROCK), VEL[member][1], 0)
+        return push_z(member, value, strip_moved, at, pl.ds(0, rows))
 
     for side in range(2):
         ok = strip_fluid[side] == 1.0
@@ -445,21 +442,25 @@
             strip_stayed[side, member] = done[member]
             strip_moved[side, member] = push_strip(member, done[member], ok)
 
-    def collide(j, carry):
-        at = first - 1 + j
-        values = [pops[member, j] for member in range(NP)]
+    def collide(at, values):
         ok = fluid[at] == 1.0
         rho, mom = moments(values)
-        done = relax(
-            rho, mom, potential[at], main_grads(potential, strip_phase, at),
-            dict(enumerate(values)),
-        )
+        grads = main_grads(potential, strip_phase, at)
+        done = relax(rho, mom, potential[at], grads, dict(enumerate(values)))
         for member in range(NP):
             stayed[member, at] = done[member]
-            moved[member, at] = push_main(member, done[member], ok, strip_moved, at)
+            moved[member, at] = push_main(member, done[member], ok, at)
+
+    def collide_own(x, carry):
+        collide(first + x, [whole(own, own_y, member, x) for member in range(NP)])
         return carry
 
-    lax.fori_loop(0, cx + 2, collide, 0)
+    lax.fori_loop(0, cx, collide_own, 0, unroll=True)
+    for got, got_y, side in ends:
+        collide(
+            jnp.where(side == 0, first - 1, last + 1),
+            [whole(got, got_y, member) for member in range(NP)],
+        )
     for side in range(2):
         at = at_depth(side, 2)
         members = {m + side: face[side, L_F2 + slot] for slot, m in enumerate(IN_F)}
@@ -471,7 +472,7 @@
         ok = fluid[at] == 1.0
         for member in done:
             stayed[member, at] = done[member]
-            moved[member, at] = push_main(member, done[member], ok, strip_moved, at)
+            moved[member, at] = push_main(member, done[member], ok, at)
         at = at_depth(side, 3)
         member = NF + IN_G + side
         done = relax(
@@ -479,23 +480,23 @@
             main_grads(potential, strip_phase, at), {member: face[side, L_G3]},
         )
         ok = fluid[at] == 1.0
-        moved[member, at] = push_main(member, done[member], ok, strip_moved, at)
-
-    def pull(source, kept, member, at):
+        moved[member, at] = push_main(member, done[member], ok, at)
+
+    def pull(member, at, part):
         if VEL[member] == (0, 0, 0):
-            return kept[member, at]
-        value = source[member, at - VEL[member][0]]
-        return jnp.where(value == ROCK, kept[OPP[member], at], value)
+            return stayed[member, at, part]
+        value = moved[member, at - VEL[member][0], part]
+        return jnp.where(value == ROCK, stayed[OPP[member], at, part], value)
 
     def stream(j, carry):
         at = first - 2 + j
-        values = [pull(moved, stayed, NF + member, at) for member in range(NG)]
+        values = [pull(NF + member, at, pl.ds(0, rows)) for member in range(NG)]
         for member in range(NG):
             phase_pops[member, at] = values[member]
         potential1[at] = jnp.where(fluid[at] == 1.0, add_up(values), 0.0)
         return carry
 
-    lax.fori_loop(0, cx + 4, stream, 0)
+    lax.fori_loop(0, cx + 4, stream, 0, unroll=True)
 
     for side in range(2):
         ok = strip_fluid[side] == 1.0
@@ -513,41 +514,70 @@
             strip_pops[side, member] = push_strip(member, done[member], ok)
         strip_phase[side] = turn(total, sign, 1)
 
-    def collide1(j, carry):
-        at = first - 1 + j
-        values = [pull(moved, stayed, member, at) for member in range(NF)]
-        values += [phase_pops[member, at] for member in range(NG)]
-        ok = fluid[at] == 1.0
-        rho, mom = moments(values)
-        done = relax(
-            rho, mom, potential1[at], main_grads(potential1, strip_phase, at),
-            dict(enumerate(values)),
+    def collide1(at, wanted, keep):
+        grads = main_grads(potential1, strip_phase, at)
+        halves = []
+        for half in range(2):
+            part = pl.ds(half * cy, cy)
+            values = [pull(member, at, part) for member in range(NF)]
+            values += [phase_pops[member, at, part] for member in range(NG)]
+            rho, mom = moments(values)
+            members = [m for m in wanted if half == 0 or VEL[m][1] != 0]
+            done = relax(
+                rho, mom, potential1[at, part],
+                [g[half * cy : (half + 1) * cy] for g in grads],
+                {m: values[m] for m in members},
+            )
+            halves.append((done, fluid[at, part] == 1.0))
+        (done, ok), (done_y, ok_y) = halves
+        for member in wanted:
+            if keep:
+                stayed1[member, at] = done[member]
+            step_y = VEL[member][1]
+            value = turn(jnp.where(ok, done[member], ROCK), step_y, 0)
+            if step_y:
+                value_y = turn(jnp.where(ok_y, done_y[member], ROCK), step_y, 0)
+                edge = 0 if step_y > 0 else cy - 1
+                value = jnp.where(row[:cy] == edge, value_y, value)
+            moved1[member, at] = push_z(member, value, strip_pops, at, own_rows)
+
+    def collide1_own(x, carry):
+        collide1(first + x, range(NP), True)
+        return carry
+
+    lax.fori_loop(0, cx, collide1_own, 0, unroll=True)
+    for side in range(2):
+        inward = 1 if side == 0 else -1
+        collide1(at_depth(side, 1), [m for m in range(NP) if VEL[m][0] == inward], False)
+
+    def outputs(x):
+        return (
+            pltpu.make_async_copy(
+                result.at[pl.ds(0, NF), x], flow_out.at[:, x], sem.at[0, x]
+            ),
+            pltpu.make_async_copy(
+                result.at[pl.ds(NF, NG), x], phase_out.at[:, x], sem.at[1, x]
+            ),
         )
-        for member in range(NP):
-            stayed1[member, at] = done[member]
-            moved1[member, at] = push_main(member, done[member], ok, strip_pops, at)
-        return carry
-
-    lax.fori_loop(0, cx + 2, collide1, 0)
 
     def finish(x, carry):
         at = first + x
-        own = pl.ds(0, cy)
-        ok = fluid[at, own] == 1.0
+        ok = fluid[at, own_rows] == 1.0
         for member in range(NP):
             if VEL[member] == (0, 0, 0):
-                value = stayed1[member, at, own]
+                value = stayed1[member, at]
             else:
-                value = moved1[member, at - VEL[member][0], own]
-                value = jnp.where(value == ROCK, stayed1[OPP[member], at, own], value)
-            value = jnp.where(ok, value, pops[member, 1 + x, own])
-            if member < NF:
-                flow_out[member, x] = value
-            else:
-                phase_out[member - NF, x] = value
+                value = moved1[member, at - VEL[member][0]]
+                value = jnp.where(value == ROCK, stayed1[OPP[member], at], value)
+            result[member, x] = jnp.where(ok, value, own[member, x])
+        for one in outputs(x):
+            one.start()
         return carry
 
-    lax.fori_loop(0, cx, finish, 0)
+    lax.fori_loop(0, cx, finish, 0, unroll=True)
+    for x in range(cx):
+        for one in outputs(x):
+            one.wait()
 
 
 def shards(sizes, flow_pops, phase_pops, pore_mask):
@@ -561,12 +591,12 @@
     def near(*arrays):
         return [pltpu.with_memory_space_constraint(a, pltpu.VMEM) for a in arrays]
 
-    def call(kernel, out_shape, in_specs, args, scratch=()):
+    def call(kernel, out_shape, in_specs, args, scratch=(), out_specs=None):
         return pl.pallas_call(
             kernel,
             out_shape=out_shape,
             in_specs=in_specs,
-            out_specs=jax.tree.map(lambda _: vmem, out_shape),
+            out_specs=out_specs or jax.tree.map(lambda _: vmem, out_shape),
             scratch_shapes=scratch,
         )(*args)
 
@@ -607,16 +637,13 @@
             jax.ShapeDtypeStruct(flow_pops.shape, f32),
             jax.ShapeDtypeStruct(phase_pops.shape, f32),
         ),
-        [anywhere] * 12,
+        [vmem] * 12,
         near(
             own, x_a, x_b, strips, far_a, far_b,
             own_y, x_a_y, x_b_y, strips_y, far_a_y, far_b_y,
         ),
         [
-            block(NV, cx + 2),
             block(2, N_FACE),
-            block(strip_blocks),
-            block(2, strip_blocks),
             block(deep),
             block(deep),
             block(2, NP),
@@ -628,10 +655,12 @@
             block(2, NP),
             block(NG, deep),
             block(deep),
-            block(NP, deep),
-            block(NP, deep),
-            pltpu.SemaphoreType.DMA((16,)),
+            pltpu.VMEM((NP, deep, cy, cz), f32),
+            pltpu.VMEM((NP, deep, cy, cz), f32),
+            pltpu.VMEM((NP, cx, cy, cz), f32),
+            pltpu.SemaphoreType.DMA((2, cx)),
         ],
+        (anywhere, anywhere),
     )
 
 

time: 30.1 us -> 28.5 us (0.947)
  Pallas kernels: 6.83 us -> 5.23 us
    pallas_call x4, Pallas kernels: 6.83 us -> 5.23 us  [call(): pl.pallas_call(kernel, out_shape=out_shape, in_specs=in_specs, out_specs=...]
where the time goes in v4:
time: 28.5 us; the launch traced here: 27.9 us
  waiting for transfers between devices  12.4 us (44%)
  starting transfers between devices  9.61 us (34%)
  Pallas kernels  5.23 us (18%)
  between operations  0.66 us (2%)
    ppermute x3, waiting for transfers between devices, swap(): got_a = lax.ppermute(send_a, AXES, perm_a) if perm_a else send_a  6.39 us
    ppermute x6, starting transfers between devices, beside(): return lax.ppermute(cells, AXES, perm) if perm else cells  6.33 us
    pallas_call x4, Pallas kernels, call(): pl.pallas_call(kernel, out_shape=out_shape, in_specs=in_specs, out_specs=...  5.23 us
    ppermute x3, waiting for transfers between devices, swap(): got_b = lax.ppermute(send_b, AXES, perm_b) if perm_b else got_a  4.22 us
    ppermute x3, starting transfers between devices, swap(): got_a = lax.ppermute(send_a, AXES, perm_a) if perm_a else send_a  3.08 us
    ppermute x6, waiting for transfers between devices, beside(): return lax.ppermute(cells, AXES, perm) if perm else cells  1.79 us
  transfers between devices with their start and end apart: 12, of which 7 were waited for; matrix products, arithmetic and copies ran while one was open for 0% of the time, Pallas kernels for 2%

profile of v4, /device:TPU:21, one launch (start us, length us, event | category | flops | bytes accessed | tf_op | source)
XLA Modules:
  0.0 27.9 jit_solution(10954892581499278282)
XLA Ops:
  0.6 1.3 %shard_map.50 = (f32[27,4,8,128]{3,2,1,0:T(8,128)S(1)}, f32[4,8,128]{2,1,0:T(8,128)S(1)}, f32[4,8,128]{2,1,0:T(8,128)S(1)}) custom-call(f32[19,4,8,128]{3,2,1,0:T(8,128)} %flow.1, f32[7,4,8,128]{3,2,1,0:T(8,128)} %phase.1, s32[4,8,128]{2,1,0:T(8,128)} %mask.1), custom_call_target="tpu_custom_call" | custom-call | tf_op jit(solution)/shard_map/pallas_call | solution.py:595
  1.9 0.7 %collective-permute-start.6 = (f32[27,4,8,128]{3,2,1,0:T(8,128)S(1)}, f32[27,4,8,128]{3,2,1,0:T(8,128)S(1)}, u32[]{:S(2)}, u32[]{:S(2)}) collective-permute-start(f32[27,4,8,128]{3,2,1,0:T(8,128)S(1)} %get-tuple-element.7.own.refs_0_), channel_id=1, source_target_pairs={{0,4},{1,5},{2,6},{3,7},{4,0},{5,1},{6,2},{7,3},{8,12},{9,13},{10,... | collective-permute-start | bytes 1327112 | tf_op jit(solution)/shard_map/ppermute | solution.py:89
  2.7 0.1 shard_map.51
  2.8 1.4 %collective-permute-start = (f32[49,8,128]{2,1,0:T(8,128)S(1)}, f32[49,8,128]{2,1,0:T(8,128)S(1)}, u32[]{:S(2)}, u32[]{:S(2)}) collective-permute-start(f32[49,8,128]{2,1,0:T(8,128)S(1)} %get-tuple-element.8), channel_id=1, source_target_pairs={{0,8},{1,9},{2,10},{3,11},{4,12},{5,13},{6,14},{7,15},{8,0},{9,1},... | collective-permute-start | bytes 602120 | tf_op jit(solution)/shard_map/ppermute | solution.py:81
  4.1 0.0 collective-permute-start.1
  4.1 5.2 %collective-permute-done.refs_1_ = f32[49,8,128]{2,1,0:T(8,128)S(1)} collective-permute-done((f32[49,8,128]{2,1,0:T(8,128)S(1)}, f32[49,8,128]{2,1,0:T(8,128)S(1)}, u32[]{:S(2)}, u32[]{:S(2)}) %collective-permute-start) | collective-permute-done | bytes 200736 | tf_op jit(solution)/shard_map/ppermute | solution.py:81
  9.3 0.9 %collective-permute-start.7 = (f32[49,8,128]{2,1,0:T(8,128)S(1)}, f32[49,8,128]{2,1,0:T(8,128)S(1)}, u32[]{:S(2)}, u32[]{:S(2)}) collective-permute-start(f32[49,8,128]{2,1,0:T(8,128)S(1)} %collective-permute-done.refs_1_), channel_id=1, source_target_pairs={{0,4},{1,5},{2,6},{3,7},{4,0},{5,1},{6,2},{7,3},{8,12},{9,13},{10,... | collective-permute-start | bytes 602120 | tf_op jit(solution)/shard_map/ppermute | solution.py:89
  10.2 0.1 collective-permute-done.1.refs_2_
  10.3 1.2 %collective-permute-start.8 = (f32[49,8,128]{2,1,0:T(8,128)S(1)}, f32[49,8,128]{2,1,0:T(8,128)S(1)}, u32[]{:S(2)}, u32[]{:S(2)}) collective-permute-start(f32[49,8,128]{2,1,0:T(8,128)S(1)} %collective-permute-done.1.refs_2_), channel_id=1, source_target_pairs={{0,4},{1,5},{2,6},{3,7},{4,0},{5,1},{6,2},{7,3},{8,12},{9,13},{10,... | collective-permute-start | bytes 602120 | tf_op jit(solution)/shard_map/ppermute | solution.py:89
  11.5 1.2 %collective-permute-start.2 = (f32[4,8,128]{2,1,0:T(8,128)S(1)}, f32[4,8,128]{2,1,0:T(8,128)S(1)}, u32[]{:S(2)}, u32[]{:S(2)}) collective-permute-start(f32[4,8,128]{2,1,0:T(8,128)S(1)} %get-tuple-element.10), channel_id=1, source_target_pairs={{0,1},{1,0},{2,3},{3,2},{4,5},{5,4},{6,7},{7,6},{8,9},{9,8},{10,11... | collective-permute-start | bytes 49160 | tf_op jit(solution)/shard_map/ppermute | solution.py:81
  12.7 0.2 collective-permute-start.3
  12.9 1.2 %collective-permute-done.2.refs_1_ = f32[4,8,128]{2,1,0:T(8,128)S(1)} collective-permute-done((f32[4,8,128]{2,1,0:T(8,128)S(1)}, f32[4,8,128]{2,1,0:T(8,128)S(1)}, u32[]{:S(2)}, u32[]{:S(2)}) %collective-permute-start.2) | collective-permute-done | bytes 16416 | tf_op jit(solution)/shard_map/ppermute | solution.py:81
  14.1 2.1 %collective-permute-done.3.refs_2_ = f32[4,8,128]{2,1,0:T(8,128)S(1)} collective-permute-done((f32[4,8,128]{2,1,0:T(8,128)S(1)}, f32[4,8,128]{2,1,0:T(8,128)S(1)}, u32[]{:S(2)}, u32[]{:S(2)}) %collective-permute-start.3) | collective-permute-done | bytes 16416 | tf_op jit(solution)/shard_map/ppermute | solution.py:82
  16.2 0.5 %shard_map.52.refs_3_ = f32[14,8,128]{2,1,0:T(8,128)S(1)} custom-call(f32[27,4,8,128]{3,2,1,0:T(8,128)S(1)} %get-tuple-element.7.own.refs_0_, f32[4,8,128]{2,1,0:T(8,128)S(1)} %collective-permute-done.2.refs_1_, f32[4,8,128]{2,1,0:T(8,128)S(1)} %collective-permute-done.3.refs_2_), custom_call_target="tpu_custom_call" | custom-call | tf_op jit(solution)/shard_map/pallas_call | solution.py:595
  16.7 1.5 %collective-permute-start.9 = (f32[14,8,128]{2,1,0:T(8,128)S(1)}, f32[14,8,128]{2,1,0:T(8,128)S(1)}, u32[]{:S(2)}, u32[]{:S(2)}) collective-permute-start(f32[14,8,128]{2,1,0:T(8,128)S(1)} %shard_map.52.refs_3_), channel_id=1, source_target_pairs={{0,4},{1,5},{2,6},{3,7},{4,0},{5,1},{6,2},{7,3},{8,12},{9,13},{10,... | collective-permute-start | bytes 172040 | tf_op jit(solution)/shard_map/ppermute | solution.py:89
  18.2 0.0 collective-permute-start.5
  18.2 0.9 %collective-permute-done.9.refs_9_ = f32[14,8,128]{2,1,0:T(8,128)S(1)} collective-permute-done((f32[14,8,128]{2,1,0:T(8,128)S(1)}, f32[14,8,128]{2,1,0:T(8,128)S(1)}, u32[]{:S(2)}, u32[]{:S(2)}) %collective-permute-start.9) | collective-permute-done | bytes 57376 | tf_op jit(solution)/shard_map/ppermute | solution.py:89
  19.1 0.5 %collective-permute-start.4 = (f32[14,8,128]{2,1,0:T(8,128)S(1)}, f32[14,8,128]{2,1,0:T(8,128)S(1)}, u32[]{:S(2)}, u32[]{:S(2)}) collective-permute-start(f32[14,8,128]{2,1,0:T(8,128)S(1)} %shard_map.52.refs_3_), channel_id=1, source_target_pairs={{0,8},{1,9},{2,10},{3,11},{4,12},{5,13},{6,14},{7,15},{8,0},{9,1},... | collective-permute-start | bytes 172040 | tf_op jit(solution)/shard_map/ppermute | solution.py:81
  19.6 2.0 %collective-permute-done.5.refs_5_ = f32[14,8,128]{2,1,0:T(8,128)S(1)} collective-permute-done((f32[14,8,128]{2,1,0:T(8,128)S(1)}, f32[14,8,128]{2,1,0:T(8,128)S(1)}, u32[]{:S(2)}, u32[]{:S(2)}) %collective-permute-start.5) | collective-permute-done | bytes 57376 | tf_op jit(solution)/shard_map/ppermute | solution.py:82
  21.6 0.9 %collective-permute-start.11 = (f32[14,8,128]{2,1,0:T(8,128)S(1)}, f32[14,8,128]{2,1,0:T(8,128)S(1)}, u32[]{:S(2)}, u32[]{:S(2)}) collective-permute-start(f32[14,8,128]{2,1,0:T(8,128)S(1)} %collective-permute-done.5.refs_5_), channel_id=1, source_target_pairs={{0,4},{1,5},{2,6},{3,7},{4,0},{5,1},{6,2},{7,3},{8,12},{9,13},{10,... | collective-permute-start | bytes 172040 | tf_op jit(solution)/shard_map/ppermute | solution.py:89
  22.6 0.0 collective-permute-done.4.refs_4_
  22.6 1.1 %collective-permute-start.10 = (f32[14,8,128]{2,1,0:T(8,128)S(1)}, f32[14,8,128]{2,1,0:T(8,128)S(1)}, u32[]{:S(2)}, u32[]{:S(2)}) collective-permute-start(f32[14,8,128]{2,1,0:T(8,128)S(1)} %collective-permute-done.4.refs_4_), channel_id=1, source_target_pairs={{0,4},{1,5},{2,6},{3,7},{4,0},{5,1},{6,2},{7,3},{8,12},{9,13},{10,... | collective-permute-start | bytes 172040 | tf_op jit(solution)/shard_map/ppermute | solution.py:89
  23.7 0.0 collective-permute-done.11.refs_11_
  23.7 0.9 %collective-permute-done.10.refs_10_ = f32[14,8,128]{2,1,0:T(8,128)S(1)} collective-permute-done((f32[14,8,128]{2,1,0:T(8,128)S(1)}, f32[14,8,128]{2,1,0:T(8,128)S(1)}, u32[]{:S(2)}, u32[]{:S(2)}) %collective-permute-start.10) | collective-permute-done | bytes 57376 | tf_op jit(solution)/shard_map/ppermute | solution.py:89
  24.6 0.0 collective-permute-done.7.refs_7_
  24.6 0.0 collective-permute-done.8.refs_8_
  24.6 0.0 collective-permute-done.6.refs_6_
  24.6 3.3 %shard_map.53 = (f32[19,4,8,128]{3,2,1,0:T(8,128)}, f32[7,4,8,128]{3,2,1,0:T(8,128)}) custom-call(f32[27,4,8,128]{3,2,1,0:T(8,128)S(1)} %get-tuple-element.7.own.refs_0_, f32[49,8,128]{2,1,0:T(8,128)S(1)} %collective-permute-done.refs_1_, f32[49,8,128]{2,1,0:T(8,128)S(1)} %collective-permute-done.1.refs_2_, f32[14,8,128]{2,1,0:T(8,128)S(1)} %shard_map.52.refs_3_, ...), custom_call_target="tpu_custom_call" | custom-call | tf_op jit(solution)/shard_map/pallas_call | solution.py:595
Async XLA Ops:
  1.9 22.6 %collective-permute-start.6 = (f32[27,4,8,128]{3,2,1,0:T(8,128)S(1)}, f32[27,4,8,128]{3,2,1,0:T(8,128)S(1)}, u32[]{:S(2)}, u32[]{:S(2)}) collective-permute-start(f32[27,4,8,128]{3,2,1,0:T(8,128)S(1)} %get-tuple-element.7.own.refs_0_), channel_id=1, source_target_pairs={{0,4},{1,5},{2,6},{3,7},{4,0},{5,1},{6,2},{7,3},{8,12},{9,13},{10,... | collective-permute-start | bytes 1327112 | tf_op jit(solution)/shard_map/ppermute | solution.py:89
  2.8 6.6 %collective-permute-start = (f32[49,8,128]{2,1,0:T(8,128)S(1)}, f32[49,8,128]{2,1,0:T(8,128)S(1)}, u32[]{:S(2)}, u32[]{:S(2)}) collective-permute-start(f32[49,8,128]{2,1,0:T(8,128)S(1)} %get-tuple-element.8), channel_id=1, source_target_pairs={{0,8},{1,9},{2,10},{3,11},{4,12},{5,13},{6,14},{7,15},{8,0},{9,1},... | collective-permute-start | bytes 602120 | tf_op jit(solution)/shard_map/ppermute | solution.py:81
  4.1 6.2 %collective-permute-start.1 = (f32[49,8,128]{2,1,0:T(8,128)S(1)}, f32[49,8,128]{2,1,0:T(8,128)S(1)}, u32[]{:S(2)}, u32[]{:S(2)}) collective-permute-start(f32[49,8,128]{2,1,0:T(8,128)S(1)} %get-tuple-element.9), channel_id=1, source_target_pairs={{0,4},{1,5},{2,6},{3,7},{4,0},{5,1},{6,2},{7,3},{8,16},{9,17},{10,... | collective-permute-start | bytes 602120 | tf_op jit(solution)/shard_map/ppermute | solution.py:82
  9.3 15.2 %collective-permute-start.7 = (f32[49,8,128]{2,1,0:T(8,128)S(1)}, f32[49,8,128]{2,1,0:T(8,128)S(1)}, u32[]{:S(2)}, u32[]{:S(2)}) collective-permute-start(f32[49,8,128]{2,1,0:T(8,128)S(1)} %collective-permute-done.refs_1_), channel_id=1, source_target_pairs={{0,4},{1,5},{2,6},{3,7},{4,0},{5,1},{6,2},{7,3},{8,12},{9,13},{10,... | collective-permute-start | bytes 602120 | tf_op jit(solution)/shard_map/ppermute | solution.py:89
  10.3 14.2 %collective-permute-start.8 = (f32[49,8,128]{2,1,0:T(8,128)S(1)}, f32[49,8,128]{2,1,0:T(8,128)S(1)}, u32[]{:S(2)}, u32[]{:S(2)}) collective-permute-start(f32[49,8,128]{2,1,0:T(8,128)S(1)} %collective-permute-done.1.refs_2_), channel_id=1, source_target_pairs={{0,4},{1,5},{2,6},{3,7},{4,0},{5,1},{6,2},{7,3},{8,12},{9,13},{10,... | collective-permute-start | bytes 602120 | tf_op jit(solution)/shard_map/ppermute | solution.py:89
  11.5 2.6 %collective-permute-start.2 = (f32[4,8,128]{2,1,0:T(8,128)S(1)}, f32[4,8,128]{2,1,0:T(8,128)S(1)}, u32[]{:S(2)}, u32[]{:S(2)}) collective-permute-start(f32[4,8,128]{2,1,0:T(8,128)S(1)} %get-tuple-element.10), channel_id=1, source_target_pairs={{0,1},{1,0},{2,3},{3,2},{4,5},{5,4},{6,7},{7,6},{8,9},{9,8},{10,11... | collective-permute-start | bytes 49160 | tf_op jit(solution)/shard_map/ppermute | solution.py:81
  12.7 3.5 %collective-permute-start.3 = (f32[4,8,128]{2,1,0:T(8,128)S(1)}, f32[4,8,128]{2,1,0:T(8,128)S(1)}, u32[]{:S(2)}, u32[]{:S(2)}) collective-permute-start(f32[4,8,128]{2,1,0:T(8,128)S(1)} %get-tuple-element.11), channel_id=1, source_target_pairs={{0,4},{1,2},{2,1},{3,7},{4,0},{5,6},{6,5},{7,3},{8,12},{9,10},{10,... | collective-permute-start | bytes 49160 | tf_op jit(solution)/shard_map/ppermute | solution.py:82
  16.7 2.4 %collective-permute-start.9 = (f32[14,8,128]{2,1,0:T(8,128)S(1)}, f32[14,8,128]{2,1,0:T(8,128)S(1)}, u32[]{:S(2)}, u32[]{:S(2)}) collective-permute-start(f32[14,8,128]{2,1,0:T(8,128)S(1)} %shard_map.52.refs_3_), channel_id=1, source_target_pairs={{0,4},{1,5},{2,6},{3,7},{4,0},{5,1},{6,2},{7,3},{8,12},{9,13},{10,... | collective-permute-start | bytes 172040 | tf_op jit(solution)/shard_map/ppermute | solution.py:89
  18.2 3.4 %collective-permute-start.5 = (f32[14,8,128]{2,1,0:T(8,128)S(1)}, f32[14,8,128]{2,1,0:T(8,128)S(1)}, u32[]{:S(2)}, u32[]{:S(2)}) collective-permute-start(f32[14,8,128]{2,1,0:T(8,128)S(1)} %shard_map.52.refs_3_), channel_id=1, source_target_pairs={{0,4},{1,5},{2,6},{3,7},{4,0},{5,1},{6,2},{7,3},{8,16},{9,17},{10,... | collective-permute-start | bytes 172040 | tf_op jit(solution)/shard_map/ppermute | solution.py:82
  19.1 3.4 %collective-permute-start.4 = (f32[14,8,128]{2,1,0:T(8,128)S(1)}, f32[14,8,128]{2,1,0:T(8,128)S(1)}, u32[]{:S(2)}, u32[]{:S(2)}) collective-permute-start(f32[14,8,128]{2,1,0:T(8,128)S(1)} %shard_map.52.refs_3_), channel_id=1, source_target_pairs={{0,8},{1,9},{2,10},{3,11},{4,12},{5,13},{6,14},{7,15},{8,0},{9,1},... | collective-permute-start | bytes 172040 | tf_op jit(solution)/shard_map/ppermute | solution.py:81
  21.6 2.0 %collective-permute-start.11 = (f32[14,8,128]{2,1,0:T(8,128)S(1)}, f32[14,8,128]{2,1,0:T(8,128)S(1)}, u32[]{:S(2)}, u32[]{:S(2)}) collective-permute-start(f32[14,8,128]{2,1,0:T(8,128)S(1)} %collective-permute-done.5.refs_5_), channel_id=1, source_target_pairs={{0,4},{1,5},{2,6},{3,7},{4,0},{5,1},{6,2},{7,3},{8,12},{9,13},{10,... | collective-permute-start | bytes 172040 | tf_op jit(solution)/shard_map/ppermute | solution.py:89
  22.6 2.0 %collective-permute-start.10 = (f32[14,8,128]{2,1,0:T(8,128)S(1)}, f32[14,8,128]{2,1,0:T(8,128)S(1)}, u32[]{:S(2)}, u32[]{:S(2)}) collective-permute-start(f32[14,8,128]{2,1,0:T(8,128)S(1)} %collective-permute-done.4.refs_4_), channel_id=1, source_target_pairs={{0,4},{1,5},{2,6},{3,7},{4,0},{5,1},{6,2},{7,3},{8,12},{9,13},{10,... | collective-permute-start | bytes 172040 | tf_op jit(solution)/shard_map/ppermute | solution.py:89

commit v5 on v4

v5 whole, which is shorter than its diff:
```python
import jax
import jax.numpy as jnp
from jax import lax
from jax.experimental import pallas as pl
from jax.experimental.pallas import tpu as pltpu
from jax.sharding import PartitionSpec as P


AXES = ("gx", "gy", "gz")

VEL_F = [
    (0, 0, 0),
    (1, 0, 0),
    (-1, 0, 0),
    (0, 1, 0),
    (0, -1, 0),
    (0, 0, 1),
    (0, 0, -1),
    (1, 1, 0),
    (-1, -1, 0),
    (1, -1, 0),
    (-1, 1, 0),
    (1, 0, 1),
    (-1, 0, -1),
    (1, 0, -1),
    (-1, 0, 1),
    (0, 1, 1),
    (0, -1, -1),
    (0, 1, -1),
    (0, -1, 1),
]
OPP_F = [0, 2, 1, 4, 3, 6, 5, 8, 7, 10, 9, 12, 11, 14, 13, 16, 15, 18, 17]
NF = 19
NG = 7
NP = NF + NG
VEL = VEL_F + VEL_F[:NG]
OPP = OPP_F + [NF + other for other in OPP_F[:NG]]

HALO = 4
ROCK = 3.0e38

IN_F = [1, 7, 9, 11, 13]
IN_G = 1
NV = NP + 1
L_G2 = 0
L_F2 = L_G2 + NG
L_G3 = L_F2 + len(IN_F)
L_PH3 = L_G3 + 1
L_PH4 = L_PH3 + 1
L_MASK = L_PH4 + 1
N_FACE = L_MASK + 2


def pairing(sizes, axis, first):
    spare = "gy" if axis != "gy" else "gx"
    perm = []
    real = False

    def linear(at):
        return (at["gx"] * sizes["gy"] + at["gy"]) * sizes["gz"] + at["gz"]

    for gx in range(sizes["gx"]):
        for gy in range(sizes["gy"]):
            for gz in range(sizes["gz"]):
                at = {"gx": gx, "gy": gy, "gz": gz}
                other = at[axis] + (1 if at[axis] % 2 == first else -1)
                if 0 <= other < sizes[axis]:
                    real = True
                    perm.append((linear(at), linear({**at, axis: other})))
                elif at[spare] ^ 1 < sizes[spare]:
                    perm.append((linear(at), linear({**at, spare: at[spare] ^ 1})))
    return perm if real else None


def swap(sizes, axis, send_a, send_b):
    perm_a = pairing(sizes, axis, 0)
    perm_b = pairing(sizes, axis, 1)
    got_a = lax.ppermute(send_a, AXES, perm_a) if perm_a else send_a
    got_b = lax.ppermute(send_b, AXES, perm_b) if perm_b else got_a
    return got_a, got_b


def beside(sizes, cells):
    if sizes["gy"] <= 2:
        perm = pairing(sizes, "gy", 0)
        return lax.ppermute(cells, AXES, perm) if perm else cells
    got_a, got_b = swap(sizes, "gy", cells, cells)
    even = lax.axis_index("gy") % 2 == 0
    above = jnp.where(even, got_a, got_b)
    below = jnp.where(even, got_b, got_a)
    row = lax.broadcasted_iota(jnp.int32, cells.shape, cells.ndim - 2)
    return jnp.where(row < HALO, above, below)


def relax(rho, mom, phase, grads, pops):
    inv = 1.0 / rho
    vel = [m * inv for m in mom]
    if grads is not None:
        square = grads[0] * grads[0] + grads[1] * grads[1] + grads[2] * grads[2] + 0.01
        inv_mag = lax.rsqrt(square)
        mag = square * inv_mag
    out = {}
    if any(member < NF for member in pops):
        omega = 1.0 / (0.8 + 0.2 * phase)
        keep = 1.0 - omega
        scale = omega * rho
        base = scale * (1.0 - 1.5 * (vel[0] * vel[0] + vel[1] * vel[1] + vel[2] * vel[2]))
        quad_v = [4.5 * scale * v for v in vel]
        lin = [(3.0 * scale) * v for v in vel]
        diag = [quad_v[d] * vel[d] for d in range(3)]
        tail = {0: 0.0, 1: 0.0, 2: 0.0}
        if grads is not None:
            quad_g = [0.5 * inv_mag * g for g in grads]
            diag = [diag[d] + quad_g[d] * grads[d] for d in range(3)]
            tail = {
                0: (1.0 / 9.0) * mag,
                1: (-0.5 / 54.0) * mag,
                2: (-0.5 / 27.0) * mag,
            }

        def cross(a, b):
            total = quad_v[a] * vel[b]
            if grads is not None:
                total = total + quad_g[a] * grads[b]
            return 2.0 * total

        memo = {}

        def once(key, make):
            if key not in memo:
                memo[key] = make()
            return memo[key]

        for member in pops:
            if member >= NF:
                continue
            dims = [d for d in range(3) if VEL[member][d] != 0]
            signs = [VEL[member][d] for d in dims]
            if not dims:
                out[member] = keep * pops[member] + ((1.0 / 3.0) * base + tail[0])
                continue
            if len(dims) == 1:
                d = dims[0]
                even = once(("e", d), lambda: (1.0 / 18.0) * (base + diag[d]) + tail[1])
                odd = once(("o", d), lambda: (1.0 / 18.0) * lin[d])
                flip = signs[0]
            else:
                a, b = dims
                same = signs[0] * signs[1]
                both = once(("s", a, b), lambda: base + diag[a] + diag[b])
                mixed = once(("m", a, b), lambda: cross(a, b))
                even = once(
                    ("e", a, b, same),
                    lambda: (1.0 / 36.0) * (both + mixed if same > 0 else both - mixed) + tail[2],
                )
                odd = once(
                    ("o", a, b, same),
                    lambda: (1.0 / 36.0) * (lin[a] + lin[b] if same > 0 else lin[a] - lin[b]),
                )
                flip = signs[0]
            mid = keep * pops[member] + even
            out[member] = mid + odd if flip > 0 else mid - odd
    if any(member >= NF for member in pops):
        part = 1.25 * 0.125
        if grads is not None:
            sharpen = 0.7 * (1.0 - phase * phase) * inv_mag
        for member in pops:
            if member < NF:
                continue
            move = VEL[member]
            if move == (0, 0, 0):
                out[member] = (1.25 * 0.25) * phase - 0.25 * pops[member]
                continue
            d = [i for i in range(3) if move[i] != 0][0]
            drift = 4.0 * phase * vel[d]
            if grads is not None:
                drift = drift + sharpen * grads[d]
            still = part * phase - 0.25 * pops[member]
            out[member] = still + part * drift if move[d] > 0 else still - part * drift
    return out


def relax_rest(phase, grads, pops):
    square = grads[0] * grads[0] + grads[1] * grads[1] + grads[2] * grads[2] + 0.01
    inv_mag = lax.rsqrt(square)
    mag = square * inv_mag
    half = 0.5 * inv_mag
    sharpen = (1.25 * 0.125 * 0.7) * (1.0 - phase * phase) * inv_mag
    quad = [half * g for g in grads]
    diag = [quad[d] * grads[d] for d in range(3)]
    memo = {}
    out = {}
    for member in pops:
        move = VEL[member]
        dims = [d for d in range(3) if move[d] != 0]
        if member >= NF:
            if dims:
                d = dims[0]
                if d not in memo:
                    memo[d] = sharpen * grads[d]
                out[member] = pops[member] + memo[d] if move[d] > 0 else pops[member] - memo[d]
            else:
                out[member] = pops[member]
            continue
        key = tuple(abs(v) for v in move) + (
            (move[dims[0]] * move[dims[1]],) if len(dims) == 2 else ()
        )
        if key not in memo:
            if not dims:
                memo[key] = (1.0 / 9.0) * mag
            elif len(dims) == 1:
                memo[key] = (1.0 / 18.0) * diag[dims[0]] - (0.5 / 54.0) * mag
            else:
                a, b = dims
                mixed = 2.0 * (quad[a] * grads[b])
                both = diag[a] + diag[b]
                both = both + mixed if key[3] > 0 else both - mixed
                memo[key] = (1.0 / 36.0) * both - (0.5 / 27.0) * mag
        out[member] = pops[member] + memo[key]
    return out


def moments(pops):
    rho = pops[0]
    for member in range(1, NF):
        rho = rho + pops[member]
    mom = []
    for d in range(3):
        plus = [pops[m] for m in range(NF) if VEL[m][d] > 0]
        minus = [pops[m] for m in range(NF) if VEL[m][d] < 0]
        total = plus[0] - minus[0]
        for p, m in zip(plus[1:], minus[1:]):
            total = total + (p - m)
        mom.append(total)
    return rho, mom


def add_up(values):
    total = values[0]
    for value in values[1:]:
        total = total + value
    return total


def turn(value, shift, dim):
    size = value.shape[dim]
    shift = shift % size
    return pltpu.roll(value, shift, axis=dim) if shift else value


def load_kernel(flow, phase, mask, own, cells, ends, out_a, out_b, mask_in, sem):
    _, cx, cy, cz = own.shape
    copies = [
        pltpu.make_async_copy(flow, own.at[pl.ds(0, NF)], sem.at[0]),
        pltpu.make_async_copy(phase, own.at[pl.ds(NF, NG)], sem.at[1]),
        pltpu.make_async_copy(mask, mask_in, sem.at[2]),
    ]
    for one in copies:
        one.start()
    for one in copies:
        one.wait()
    cells[NP] = mask_in[...].astype(jnp.float32)
    for x in range(cx):
        values = [own[member, x] for member in range(NP)]
        rho, mom = moments(values)
        done = relax(rho, mom, add_up(values[NF:]), None, dict(enumerate(values)))
        for member in range(NP):
            cells[member, x] = done[member]
    even = lax.axis_index("gz") % 2 == 0
    lane = lax.broadcasted_iota(jnp.int32, (cy, cz), 1)
    group = lane // (2 * HALO)
    first_half = lane % (2 * HALO) < HALO
    per = cz // (2 * HALO * cx)
    for block in range(ends.shape[0]):
        total = jnp.zeros((cy, cz), jnp.float32)
        for field in range(block * per, min((block + 1) * per, NV)):
            for x in range(cx):
                slot = (field % per) * cx + x
                value = turn(cells[field, x], slot * 2 * HALO + HALO, 1)
                total = jnp.where(group == slot, value, total)
        ends[block] = total
    for pair in range(out_a.shape[0]):
        one = ends[2 * pair]
        two = ends[min(2 * pair + 1, ends.shape[0] - 1)]
        high = jnp.where(first_half, one, turn(two, HALO, 1))
        low = jnp.where(first_half, turn(one, -HALO, 1), two)
        out_a[pair] = jnp.where(even, high, low)
        out_b[pair] = jnp.where(even, low, high)


def pack_face(own, out, base, up):
    cx = own.shape[1]
    other = jnp.where(up, 0, 1)
    xs = [jnp.where(up, cx - 1 - d, d) for d in range(HALO)]
    for field in range(NV):
        out[base + field] = own[field, xs[0]]
    base = base + NV
    for member in range(NG):
        out[base + L_G2 + member] = own[NF + member, xs[1]]
    for slot, member in enumerate(IN_F):
        out[base + L_F2 + slot] = own[member + other, xs[1]]
    out[base + L_G3] = own[NF + IN_G + other, xs[2]]
    out[base + L_PH3] = add_up([own[NF + member, xs[2]] for member in range(NG)])
    far = add_up([own[NF + member, xs[3]] for member in range(NG)])
    out[base + L_PH4] = jnp.where(own[NP, xs[3]] == 1.0, far, 0.0)
    for d in range(2):
        out[base + L_MASK + d] = own[NP, xs[1 + d]]


def faces_kernel(own, out_a, out_b):
    even = lax.axis_index("gx") % 2 == 0
    pack_face(own, out_a, 0, even)
    pack_face(own, out_b, 0, jnp.logical_not(even))


def strips_kernel(ends, z_a, z_b, strips, *, sizes):
    blocks, cy, cz = ends.shape
    at_z = lax.axis_index("gz")
    even = at_z % 2 == 0
    lane = lax.broadcasted_iota(jnp.int32, (cy, cz), 1)
    first_half = lane % (2 * HALO) < HALO
    has_below = at_z > 0
    has_above = at_z < sizes["gz"] - 1
    for block in range(blocks):
        from_a, from_b = z_a[block // 2], z_b[block // 2]
        below = jnp.where(even, from_b, from_a)
        above = jnp.where(even, from_a, from_b)
        if block % 2 == 0:
            above = turn(above, HALO, 1)
        else:
            below = turn(below, -HALO, 1)
        if block == blocks - 1:
            below = jnp.where(has_below, below, 0.0)
            above = jnp.where(has_above, above, 0.0)
        own = ends[block]
        strips[block] = jnp.where(first_half, below, own)
        strips[blocks + block] = jnp.where(first_half, own, above)


def steps_kernel(
    own, cells, cells_y, strips, strips_y, far_a, far_b, far_a_y, far_b_y,
    x_a, x_b, x_a_y, x_b_y,
    flow_out, phase_out,
    face, fluid, potential,
    strip_pops, strip_fluid, fill_moved, fill_moved1, moved, stayed, strip_moved, strip_stayed,
    phase_pops, potential1, moved1, stayed1, result, sem,
    *, sizes,
):
    _, cx, cy, cz = own.shape
    rows = 2 * cy
    at_x = lax.axis_index("gx")
    at_y = lax.axis_index("gy")
    even_x = at_x % 2 == 0
    first, last = HALO, HALO + cx - 1
    own_rows = pl.ds(0, cy)

    def whole(cells, cells_y, *at):
        return jnp.concatenate([cells[at], cells_y[at]], axis=0)

    lane = lax.broadcasted_iota(jnp.int32, (rows, cz), 1)
    row = lax.broadcasted_iota(jnp.int32, (rows, cz), 0)
    has_left = at_x > 0
    has_right = at_x < sizes["gx"] - 1
    has_low = at_y > 0
    has_high = at_y < sizes["gy"] - 1
    high_row = jnp.where(has_high, cy + HALO, cy)
    low_row = jnp.where(has_low, cy + HALO, rows)
    row_ok = (row < high_row) | (row >= low_row)
    has = (has_left, has_right)

    def at_depth(side, depth):
        return first - depth if side == 0 else last + depth

    side_a = jnp.where(even_x, 1, 0)
    ends = ((x_a, x_a_y, side_a), (x_b, x_b_y, 1 - side_a))

    def whole_face(end, layer):
        return whole(end[0], end[1], layer)

    for x in range(cx):
        ok = (whole(cells, cells_y, NP, x) == 1.0) & row_ok
        fluid[first + x] = ok.astype(jnp.float32)
        total = add_up([whole(cells, cells_y, NF + member, x) for member in range(NG)])
        potential[first + x] = jnp.where(ok, total, 0.0)
    for end in ends:
        side = end[2]
        for layer in range(N_FACE):
            face[side, layer] = whole_face(end, NV + layer)
        at = jnp.where(side == 0, first - 1, last + 1)
        side_ok = row_ok & ((side == 0) & has_left | (side == 1) & has_right)
        ok = side_ok & (whole_face(end, NP) == 1.0)
        total = add_up([whole_face(end, NF + member) for member in range(NG)])
        fluid[at] = ok.astype(jnp.float32)
        potential[at] = jnp.where(ok, total, 0.0)
    for side in range(2):
        side_ok = row_ok & has[side]
        for depth in range(2, HALO + 1):
            at = at_depth(side, depth)
            ok = side_ok
            if depth == 2:
                total = add_up([face[side, L_G2 + m] for m in range(NG)])
            else:
                total = face[side, L_PH3 if depth == 3 else L_PH4]
            if depth < HALO:
                ok = ok & (face[side, L_MASK + depth - 2] == 1.0)
                fluid[at] = ok.astype(jnp.float32)
            potential[at] = jnp.where(ok, total, 0.0)

    cols = 2 * HALO
    wide = cols * cx
    per = cz // wide
    block_ok = row_ok & (
        ((lane < wide) & has_left)
        | ((lane >= wide) & (lane < 2 * wide))
        | ((lane >= 2 * wide) & (lane < 3 * wide) & has_right)
    )
    blocks = strips.shape[0] // 2
    group = lane // wide
    for side in range(2):
        for block in range(blocks):
            at = side * blocks + block
            from_a = whole(far_a, far_a_y, at)
            from_b = whole(far_b, far_b_y, at)
            left = jnp.where(even_x, from_b, from_a)
            mine = turn(whole(strips, strips_y, at), wide, 1)
            right = turn(jnp.where(even_x, from_a, from_b), 2 * wide, 1)
            for field in range(block * per, min((block + 1) * per, NV)):
                spot = field % per
                value = jnp.where(
                    group == spot, left, jnp.where(group == (spot + 1) % per, mine, right)
                )
                value = turn(value, -spot * wide, 1)
                if field < NP:
                    strip_pops[side, field] = value
                else:
                    strip_fluid[side] = jnp.where(block_ok, value, 0.0)

    def strip_grads(values):
        return (
            0.5 * (turn(values, -cols, 1) - turn(values, cols, 1)),
            0.5 * (turn(values, -1, 0) - turn(values, 1, 0)),
            0.5 * (turn(values, -1, 1) - turn(values, 1, 1)),
        )

    def push_strip(member, value, ok):
        move = VEL[member]
        value = jnp.where(ok, value, ROCK)
        value = turn(value, move[0] * cols + move[2], 1)
        return turn(value, move[1], 0)

    from_low = lane % cols == HALO
    fills = {}
    for member in range(NP):
        if VEL[member][2] > 0:
            base = 0 if member < NF else NF
            move = VEL[member]
            twin = base + VEL_F.index((move[0], move[1], -1))
            fills[member] = fills[twin] = (len(fills) // 2, member, twin)

    def to_ends(values, at):
        return pltpu.roll(values, (2 * cz - (at * cols + HALO)) % cz, axis=1)

    def main_grads(source, fill, at):
        here = source[at]
        fill = to_ends(fill, at)
        down = jnp.where(lane == 0, fill, turn(here, 1, 1))
        up = jnp.where(lane == cz - 1, fill, turn(here, -1, 1))
        return (
            0.5 * (source[at + 1] - source[at - 1]),
            0.5 * (turn(here, -1, 0) - turn(here, 1, 0)),
            0.5 * (up - down),
        )

    def push_z(member, value, source, at, part, memo):
        move = VEL[member]
        if move[2] == 0:
            return value
        size = value.shape[0]
        number = fills[member][0]
        if number not in memo:
            memo[number] = to_ends(source[number, part], at + move[0])
        edge = 0 if move[2] > 0 else cz - 1
        return jnp.where(lane[:size] == edge, memo[number], turn(value, move[2], 1))

    def push_main(member, value, ok, at, memo):
        value = turn(jnp.where(ok, value, ROCK), VEL[member][1], 0)
        return push_z(member, value, fill_moved, at, pl.ds(0, rows), memo)

    totals = []
    for side in range(2):
        ok = strip_fluid[side] == 1.0
        values = [strip_pops[side, member] for member in range(NP)]
        total = jnp.where(ok, add_up(values[NF:]), 0.0)
        totals.append(turn(total, 1 if side == 0 else -1, 1))
        done = relax_rest(total, strip_grads(total), dict(enumerate(values)))
        for member in range(NP):
            strip_stayed[side, member] = done[member]
            strip_moved[side, member] = push_strip(member, done[member], ok)

    fill_phase = jnp.where(from_low, totals[0], totals[1])
    for number, low, high in sorted(set(fills.values())):
        fill_moved[number] = jnp.where(from_low, strip_moved[0, low], strip_moved[1, high])

    def collide(at, values):
        ok = fluid[at] == 1.0
        grads = main_grads(potential, fill_phase, at)
        done = relax_rest(potential[at], grads, dict(enumerate(values)))
        memo = {}
        for member in range(NP):
            stayed[member, at] = done[member]
            moved[member, at] = push_main(member, done[member], ok, at, memo)

    def collide_own(x, carry):
        collide(first + x, [whole(cells, cells_y, member, x) for member in range(NP)])
        return carry

    lax.fori_loop(0, cx, collide_own, 0, unroll=True)
    for end in ends:
        collide(
            jnp.where(end[2] == 0, first - 1, last + 1),
            [whole_face(end, member) for member in range(NP)],
        )
    for side in range(2):
        at = at_depth(side, 2)
        members = {m + side: face[side, L_F2 + slot] for slot, m in enumerate(IN_F)}
        members.update({NF + m: face[side, L_G2 + m] for m in range(NG)})
        done = relax_rest(potential[at], main_grads(potential, fill_phase, at), members)
        ok = fluid[at] == 1.0
        memo = {}
        for member in done:
            stayed[member, at] = done[member]
            moved[member, at] = push_main(member, done[member], ok, at, memo)
        at = at_depth(side, 3)
        member = NF + IN_G + side
        done = relax_rest(
            potential[at], main_grads(potential, fill_phase, at), {member: face[side, L_G3]}
        )
        ok = fluid[at] == 1.0
        moved[member, at] = push_main(member, done[member], ok, at, {})

    def pull(member, at, part):
        if VEL[member] == (0, 0, 0):
            return stayed[member, at, part]
        value = moved[member, at - VEL[member][0], part]
        return jnp.where(value == ROCK, stayed[OPP[member], at, part], value)

    def stream(j, carry):
        at = first - 2 + j
        values = [pull(NF + member, at, pl.ds(0, rows)) for member in range(NG)]
        for member in range(NG):
            phase_pops[member, at] = values[member]
        potential1[at] = jnp.where(fluid[at] == 1.0, add_up(values), 0.0)
        return carry

    lax.fori_loop(0, cx + 4, stream, 0, unroll=True)

    totals = []
    crossed = {}
    for side in range(2):
        ok = strip_fluid[side] == 1.0
        values = []
        for member in range(NP):
            value = strip_moved[side, member]
            back = strip_stayed[side, OPP[member]]
            values.append(jnp.where(value == ROCK, back, value))
        total = jnp.where(ok, add_up(values[NF:]), 0.0)
        rho, mom = moments(values)
        sign = 1 if side == 0 else -1
        wanted = {m: values[m] for m in range(NP) if VEL[m][2] == sign}
        done = relax(rho, mom, total, strip_grads(total), wanted)
        for member in wanted:
            crossed[member] = push_strip(member, done[member], ok)
        totals.append(turn(total, sign, 1))
    fill_phase1 = jnp.where(from_low, totals[0], totals[1])
    for number, low, high in sorted(set(fills.values())):
        fill_moved1[number] = jnp.where(from_low, crossed[low], crossed[high])

    def collide1(at, wanted, keep):
        grads = main_grads(potential1, fill_phase1, at)
        halves = []
        for half in range(2):
            part = pl.ds(half * cy, cy)
            values = [pull(member, at, part) for member in range(NF)]
            values += [phase_pops[member, at, part] for member in range(NG)]
            rho, mom = moments(values)
            members = [m for m in wanted if half == 0 or VEL[m][1] != 0]
            done = relax(
                rho, mom, potential1[at, part],
                [g[half * cy : (half + 1) * cy] for g in grads],
                {m: values[m] for m in members},
            )
            halves.append((done, fluid[at, part] == 1.0))
        (done, ok), (done_y, ok_y) = halves
        memo = {}
        for member in wanted:
            if keep:
                stayed1[member, at] = done[member]
            step_y = VEL[member][1]
            value = turn(jnp.where(ok, done[member], ROCK), step_y, 0)
            if step_y:
                value_y = turn(jnp.where(ok_y, done_y[member], ROCK), step_y, 0)
                edge = 0 if step_y > 0 else cy - 1
                value = jnp.where(row[:cy] == edge, value_y, value)
            moved1[member, at] = push_z(member, value, fill_moved1, at, own_rows, memo)

    def outputs(x):
        return (
            pltpu.make_async_copy(
                result.at[pl.ds(0, NF), x], flow_out.at[:, x], sem.at[0, x]
            ),
            pltpu.make_async_copy(
                result.at[pl.ds(NF, NG), x], phase_out.at[:, x], sem.at[1, x]
            ),
        )

    def finish(x):
        at = first + x
        ok = fluid[at, own_rows] == 1.0
        for member in range(NP):
            if VEL[member] == (0, 0, 0):
                value = stayed1[member, at]
            else:
                value = moved1[member, at - VEL[member][0]]
                value = jnp.where(value == ROCK, stayed1[OPP[member], at], value)
            result[member, x] = jnp.where(ok, value, own[member, x])
        for one in outputs(x):
            one.start()

    collide1(first - 1, [m for m in range(NP) if VEL[m][0] == 1], False)
    for x in range(cx):
        collide1(first + x, range(NP), True)
        if x > 0:
            finish(x - 1)
    collide1(last + 1, [m for m in range(NP) if VEL[m][0] == -1], False)
    finish(cx - 1)
    for x in range(cx):
        for one in outputs(x):
            one.wait()


def shards(sizes, flow_pops, phase_pops, pore_mask):
    cx, cy, cz = pore_mask.shape
    rows = 2 * cy
    assert cx >= HALO and cy == 2 * HALO and 6 * cx * HALO <= cz
    f32 = jnp.float32
    vmem = pl.BlockSpec(memory_space=pltpu.VMEM)
    anywhere = pl.BlockSpec(memory_space=pl.ANY)

    def near(*arrays):
        return [pltpu.with_memory_space_constraint(a, pltpu.VMEM) for a in arrays]

    def call(kernel, out_shape, in_specs, args, scratch=(), out_specs=None):
        return pl.pallas_call(
            kernel,
            out_shape=out_shape,
            in_specs=in_specs,
            out_specs=out_specs or jax.tree.map(lambda _: vmem, out_shape),
            scratch_shapes=scratch,
        )(*args)

    end_blocks = pl.cdiv(NV, cz // (2 * HALO * cx))
    end_shape = pltpu.VMEM((end_blocks, cy, cz), f32)
    z_shape = pltpu.VMEM((pl.cdiv(end_blocks, 2), cy, cz), f32)
    own, cells, ends, z_a, z_b = call(
        load_kernel,
        (
            pltpu.VMEM((NP, cx, cy, cz), f32),
            pltpu.VMEM((NV, cx, cy, cz), f32),
            end_shape,
            z_shape,
            z_shape,
        ),
        [anywhere] * 3, (flow_pops, phase_pops, pore_mask),
        [
            pltpu.VMEM(pore_mask.shape, jnp.int32),
            pltpu.SemaphoreType.DMA((3,)),
        ],
    )
    cells_y = beside(sizes, cells)
    z_a, z_b = swap(sizes, "gz", z_a, z_b)

    x_shape = pltpu.VMEM((NV + N_FACE, cy, cz), f32)
    x_a, x_b = call(faces_kernel, (x_shape, x_shape), [vmem], near(cells))
    x_a, x_b = swap(sizes, "gx", x_a, x_b)
    x_a_y = beside(sizes, x_a)
    x_b_y = beside(sizes, x_b)

    strip_blocks = 2 * end_blocks
    strips = call(
        lambda *refs: strips_kernel(*refs, sizes=sizes),
        pltpu.VMEM((strip_blocks, cy, cz), f32), [vmem] * 3, near(ends, z_a, z_b),
    )
    strips_y = beside(sizes, strips)
    far_a, far_b = swap(sizes, "gx", strips, strips)
    far_a_y = beside(sizes, far_a)
    far_b_y = beside(sizes, far_b)

    deep = cx + 2 * HALO

    def block(*lead):
        return pltpu.VMEM((*lead, rows, cz), f32)

    return call(
        lambda *refs: steps_kernel(*refs, sizes=sizes),
        (
            jax.ShapeDtypeStruct(flow_pops.shape, f32),
            jax.ShapeDtypeStruct(phase_pops.shape, f32),
        ),
        [vmem] * 13,
        near(
            own, cells, cells_y, strips, strips_y, far_a, far_b, far_a_y, far_b_y,
            x_a, x_b, x_a_y, x_b_y,
        ),
        [
            block(2, N_FACE),
            block(deep),
            block(deep),
            block(2, NP),
            block(2),
            block(6),
            block(6),
            block(NP, deep),
            block(NP, deep),
            block(2, NP),
            block(2, NP),
            block(NG, deep),
            block(deep),
            pltpu.VMEM((NP, deep, cy, cz), f32),
            pltpu.VMEM((NP, deep, cy, cz), f32),
            pltpu.VMEM((NP, cx, cy, cz), f32),
            pltpu.SemaphoreType.DMA((2, cx)),
        ],
        (anywhere, anywhere),
    )


def solution(mesh):
    sizes = dict(mesh.shape)
    placed = (P(None, "gx", "gy", "gz"), P(None, "gx", "gy", "gz"), P("gx", "gy", "gz"))
    return jax.shard_map(
        lambda *args: shards(sizes, *args),
        mesh=mesh,
        in_specs=placed,
        out_specs=(P(None, "gx", "gy", "gz"), P(None, "gx", "gy", "gz")),
        check_vma=False,
    )
```

time: 28.5 us -> 22.2 us (0.78)
  the two profiles are of different devices: /device:TPU:21 before, /device:TPU:0 now
where the time goes in v5:
time: 22.2 us; the launch traced here: 22 us
  starting transfers between devices  10.1 us (45%)
  waiting for transfers between devices  6.67 us (30%)
  Pallas kernels  4.63 us (21%)
  between operations  0.66 us (3%)
    ppermute x3, starting transfers between devices, swap(): got_a = lax.ppermute(send_a, AXES, perm_a) if perm_a else send_a  8.24 us
    ppermute x3, waiting for transfers between devices, swap(): got_a = lax.ppermute(send_a, AXES, perm_a) if perm_a else send_a  5.76 us
    pallas_call x4, Pallas kernels, call(): pl.pallas_call(kernel, out_shape=out_shape, in_specs=in_specs, out_specs=...  4.63 us
    ppermute x6, starting transfers between devices, beside(): return lax.ppermute(cells, AXES, perm) if perm else cells  1.58 us
    ppermute x6, waiting for transfers between devices, beside(): return lax.ppermute(cells, AXES, perm) if perm else cells  0.9 us
  transfers between devices with their start and end apart: 12, of which 4 were waited for; matrix products, arithmetic and copies ran while one was open for 0% of the time, Pallas kernels for 1%

profile of v5, /device:TPU:0, one launch (start us, length us, event | category | flops | bytes accessed | tf_op | source)
XLA Modules:
  0.0 22.0 jit_solution(12282562115539926531)
XLA Ops:
  0.6 1.3 %shard_map.50 = (f32[26,4,8,128]{3,2,1,0:T(8,128)S(1)}, f32[27,4,8,128]{3,2,1,0:T(8,128)S(1)}, f32[7,8,128]{2,1,0:T(8,128)S(1)}, f32[4,8,128]{2,1,0:T(8,128)S(1)}, f32[4,8,128]{2,1,0:T(8,128)S(1)}) custom-call(f32[19,4,8,128]{3,2,1,0:T(8,128)} %flow.1, f32[7,4,8,128]{3,2,1,0:T(8,128)} %phase.1, s32[4,8,128]{2,1,0:T(8,128)} %mask.1), custom_call_target="tpu_custom_call" | custom-call | tf_op jit(solution)/shard_map/pallas_call | solution.py:653
  2.0 0.6 %collective-permute-start = (f32[27,4,8,128]{3,2,1,0:T(8,128)S(1)}, f32[27,4,8,128]{3,2,1,0:T(8,128)S(1)}, u32[]{:S(2)}, u32[]{:S(2)}) collective-permute-start(f32[27,4,8,128]{3,2,1,0:T(8,128)S(1)} %get-tuple-element.10.own.refs_1_), channel_id=1, source_target_pairs={{0,4},{1,5},{2,6},{3,7},{4,0},{5,1},{6,2},{7,3},{8,12},{9,13},{10,... | collective-permute-start | bytes 1327112 | tf_op jit(solution)/shard_map/ppermute | solution.py:86
  2.6 2.7 %collective-permute-start.8 = (f32[44,8,128]{2,1,0:T(8,128)S(1)}, f32[44,8,128]{2,1,0:T(8,128)S(1)}, u32[]{:S(2)}, u32[]{:S(2)}) collective-permute-start(f32[44,8,128]{2,1,0:T(8,128)S(1)} %get-tuple-element.14), channel_id=1, source_target_pairs={{0,8},{1,9},{2,10},{3,11},{4,12},{5,13},{6,14},{7,15},{8,0},{9,1},... | collective-permute-start | bytes 540680 | tf_op jit(solution)/shard_map/ppermute | solution.py:78
  5.2 0.2 collective-permute-start.9
  5.4 1.5 %collective-permute-start.1 = (f32[4,8,128]{2,1,0:T(8,128)S(1)}, f32[4,8,128]{2,1,0:T(8,128)S(1)}, u32[]{:S(2)}, u32[]{:S(2)}) collective-permute-start(f32[4,8,128]{2,1,0:T(8,128)S(1)} %get-tuple-element.12), channel_id=1, source_target_pairs={{0,1},{1,0},{2,3},{3,2},{4,5},{5,4},{6,7},{7,6},{8,9},{9,8},{10,11... | collective-permute-start | bytes 49160 | tf_op jit(solution)/shard_map/ppermute | solution.py:78
  6.9 0.0 collective-permute-start.2
  7.0 3.5 %collective-permute-done.8.refs_9_ = f32[44,8,128]{2,1,0:T(8,128)S(1)} collective-permute-done((f32[44,8,128]{2,1,0:T(8,128)S(1)}, f32[44,8,128]{2,1,0:T(8,128)S(1)}, u32[]{:S(2)}, u32[]{:S(2)}) %collective-permute-start.8) | collective-permute-done | bytes 180256 | tf_op jit(solution)/shard_map/ppermute | solution.py:78
  10.4 0.0 collective-permute-start.10
  10.4 0.0 collective-permute-done.9.refs_10_
  10.4 0.5 %collective-permute-start.11 = (f32[44,8,128]{2,1,0:T(8,128)S(1)}, f32[44,8,128]{2,1,0:T(8,128)S(1)}, u32[]{:S(2)}, u32[]{:S(2)}) collective-permute-start(f32[44,8,128]{2,1,0:T(8,128)S(1)} %collective-permute-done.9.refs_10_), channel_id=1, source_target_pairs={{0,4},{1,5},{2,6},{3,7},{4,0},{5,1},{6,2},{7,3},{8,12},{9,13},{10,... | collective-permute-start | bytes 540680 | tf_op jit(solution)/shard_map/ppermute | solution.py:86
  11.0 0.0 collective-permute-done.1.refs_1_
  11.0 0.0 collective-permute-done.2.refs_2_
  11.0 0.1 shard_map.51.refs_3_
  11.0 0.0 collective-permute-start.5
  11.1 4.1 %collective-permute-start.4 = (f32[14,8,128]{2,1,0:T(8,128)S(1)}, f32[14,8,128]{2,1,0:T(8,128)S(1)}, u32[]{:S(2)}, u32[]{:S(2)}) collective-permute-start(f32[14,8,128]{2,1,0:T(8,128)S(1)} %shard_map.51.refs_3_), channel_id=1, source_target_pairs={{0,8},{1,9},{2,10},{3,11},{4,12},{5,13},{6,14},{7,15},{8,0},{9,1},... | collective-permute-start | bytes 172040 | tf_op jit(solution)/shard_map/ppermute | solution.py:78
  15.2 0.0 collective-permute-done.5.refs_6_
  15.2 0.0 collective-permute-start.3
  15.2 2.3 %collective-permute-done.4.refs_5_ = f32[14,8,128]{2,1,0:T(8,128)S(1)} collective-permute-done((f32[14,8,128]{2,1,0:T(8,128)S(1)}, f32[14,8,128]{2,1,0:T(8,128)S(1)}, u32[]{:S(2)}, u32[]{:S(2)}) %collective-permute-start.4) | collective-permute-done | bytes 57376 | tf_op jit(solution)/shard_map/ppermute | solution.py:78
  17.5 0.0 collective-permute-start.7
  17.5 0.0 collective-permute-done.3.refs_4_
  17.5 0.5 %collective-permute-start.6 = (f32[14,8,128]{2,1,0:T(8,128)S(1)}, f32[14,8,128]{2,1,0:T(8,128)S(1)}, u32[]{:S(2)}, u32[]{:S(2)}) collective-permute-start(f32[14,8,128]{2,1,0:T(8,128)S(1)} %collective-permute-done.4.refs_5_), channel_id=1, source_target_pairs={{0,4},{1,5},{2,6},{3,7},{4,0},{5,1},{6,2},{7,3},{8,12},{9,13},{10,... | collective-permute-start | bytes 172040 | tf_op jit(solution)/shard_map/ppermute | solution.py:86
  18.0 0.7 %collective-permute-done.7.refs_8_ = f32[14,8,128]{2,1,0:T(8,128)S(1)} collective-permute-done((f32[14,8,128]{2,1,0:T(8,128)S(1)}, f32[14,8,128]{2,1,0:T(8,128)S(1)}, u32[]{:S(2)}, u32[]{:S(2)}) %collective-permute-start.7) | collective-permute-done | bytes 57376 | tf_op jit(solution)/shard_map/ppermute | solution.py:86
  18.7 0.2 collective-permute-done.6.refs_7_
  18.9 0.0 collective-permute-done.10.refs_11_
  18.9 0.0 collective-permute-done.11.refs_12_
  18.9 0.0 collective-permute-done.refs_2_
  18.9 3.2 %shard_map.53 = (f32[19,4,8,128]{3,2,1,0:T(8,128)}, f32[7,4,8,128]{3,2,1,0:T(8,128)}) custom-call(f32[26,4,8,128]{3,2,1,0:T(8,128)S(1)} %get-tuple-element.9.refs_0_, f32[27,4,8,128]{3,2,1,0:T(8,128)S(1)} %get-tuple-element.10.own.refs_1_, f32[27,4,8,128]{3,2,1,0:T(8,128)S(1)} %collective-permute-done.refs_2_, f32[14,8,128]{2,1,0:T(8,128)S(1)} %shard_map.51.refs_3_, ...), custom_call_target="tpu_custom_call" | custom-call | tf_op jit(solution)/shard_map/pallas_call | solution.py:653
  (1 shorter events, 0.0 us)
Async XLA Ops:
  2.0 16.9 %collective-permute-start = (f32[27,4,8,128]{3,2,1,0:T(8,128)S(1)}, f32[27,4,8,128]{3,2,1,0:T(8,128)S(1)}, u32[]{:S(2)}, u32[]{:S(2)}) collective-permute-start(f32[27,4,8,128]{3,2,1,0:T(8,128)S(1)} %get-tuple-element.10.own.refs_1_), channel_id=1, source_target_pairs={{0,4},{1,5},{2,6},{3,7},{4,0},{5,1},{6,2},{7,3},{8,12},{9,13},{10,... | collective-permute-start | bytes 1327112 | tf_op jit(solution)/shard_map/ppermute | solution.py:86
  2.6 7.9 %collective-permute-start.8 = (f32[44,8,128]{2,1,0:T(8,128)S(1)}, f32[44,8,128]{2,1,0:T(8,128)S(1)}, u32[]{:S(2)}, u32[]{:S(2)}) collective-permute-start(f32[44,8,128]{2,1,0:T(8,128)S(1)} %get-tuple-element.14), channel_id=1, source_target_pairs={{0,8},{1,9},{2,10},{3,11},{4,12},{5,13},{6,14},{7,15},{8,0},{9,1},... | collective-permute-start | bytes 540680 | tf_op jit(solution)/shard_map/ppermute | solution.py:78
  5.2 5.2 %collective-permute-start.9 = (f32[44,8,128]{2,1,0:T(8,128)S(1)}, f32[44,8,128]{2,1,0:T(8,128)S(1)}, u32[]{:S(2)}, u32[]{:S(2)}) collective-permute-start(f32[44,8,128]{2,1,0:T(8,128)S(1)} %get-tuple-element.15), channel_id=1, source_target_pairs={{0,4},{1,5},{2,6},{3,7},{4,0},{5,1},{6,2},{7,3},{8,16},{9,17},{10,... | collective-permute-start | bytes 540680 | tf_op jit(solution)/shard_map/ppermute | solution.py:79
  5.4 5.5 %collective-permute-start.1 = (f32[4,8,128]{2,1,0:T(8,128)S(1)}, f32[4,8,128]{2,1,0:T(8,128)S(1)}, u32[]{:S(2)}, u32[]{:S(2)}) collective-permute-start(f32[4,8,128]{2,1,0:T(8,128)S(1)} %get-tuple-element.12), channel_id=1, source_target_pairs={{0,1},{1,0},{2,3},{3,2},{4,5},{5,4},{6,7},{7,6},{8,9},{9,8},{10,11... | collective-permute-start | bytes 49160 | tf_op jit(solution)/shard_map/ppermute | solution.py:78
  6.9 4.0 %collective-permute-start.2 = (f32[4,8,128]{2,1,0:T(8,128)S(1)}, f32[4,8,128]{2,1,0:T(8,128)S(1)}, u32[]{:S(2)}, u32[]{:S(2)}) collective-permute-start(f32[4,8,128]{2,1,0:T(8,128)S(1)} %get-tuple-element.13), channel_id=1, source_target_pairs={{0,4},{1,2},{2,1},{3,7},{4,0},{5,6},{6,5},{7,3},{8,12},{9,10},{10,... | collective-permute-start | bytes 49160 | tf_op jit(solution)/shard_map/ppermute | solution.py:79
  10.4 8.4 %collective-permute-start.10 = (f32[44,8,128]{2,1,0:T(8,128)S(1)}, f32[44,8,128]{2,1,0:T(8,128)S(1)}, u32[]{:S(2)}, u32[]{:S(2)}) collective-permute-start(f32[44,8,128]{2,1,0:T(8,128)S(1)} %collective-permute-done.8.refs_9_), channel_id=1, source_target_pairs={{0,4},{1,5},{2,6},{3,7},{4,0},{5,1},{6,2},{7,3},{8,12},{9,13},{10,... | collective-permute-start | bytes 540680 | tf_op jit(solution)/shard_map/ppermute | solution.py:86
  10.4 8.4 %collective-permute-start.11 = (f32[44,8,128]{2,1,0:T(8,128)S(1)}, f32[44,8,128]{2,1,0:T(8,128)S(1)}, u32[]{:S(2)}, u32[]{:S(2)}) collective-permute-start(f32[44,8,128]{2,1,0:T(8,128)S(1)} %collective-permute-done.9.refs_10_), channel_id=1, source_target_pairs={{0,4},{1,5},{2,6},{3,7},{4,0},{5,1},{6,2},{7,3},{8,12},{9,13},{10,... | collective-permute-start | bytes 540680 | tf_op jit(solution)/shard_map/ppermute | solution.py:86
  11.0 4.1 %collective-permute-start.5 = (f32[14,8,128]{2,1,0:T(8,128)S(1)}, f32[14,8,128]{2,1,0:T(8,128)S(1)}, u32[]{:S(2)}, u32[]{:S(2)}) collective-permute-start(f32[14,8,128]{2,1,0:T(8,128)S(1)} %shard_map.51.refs_3_), channel_id=1, source_target_pairs={{0,4},{1,5},{2,6},{3,7},{4,0},{5,1},{6,2},{7,3},{8,16},{9,17},{10,... | collective-permute-start | bytes 172040 | tf_op jit(solution)/shard_map/ppermute | solution.py:79
  11.1 6.4 %collective-permute-start.4 = (f32[14,8,128]{2,1,0:T(8,128)S(1)}, f32[14,8,128]{2,1,0:T(8,128)S(1)}, u32[]{:S(2)}, u32[]{:S(2)}) collective-permute-start(f32[14,8,128]{2,1,0:T(8,128)S(1)} %shard_map.51.refs_3_), channel_id=1, source_target_pairs={{0,8},{1,9},{2,10},{3,11},{4,12},{5,13},{6,14},{7,15},{8,0},{9,1},... | collective-permute-start | bytes 172040 | tf_op jit(solution)/shard_map/ppermute | solution.py:78
  15.2 2.3 %collective-permute-start.3 = (f32[14,8,128]{2,1,0:T(8,128)S(1)}, f32[14,8,128]{2,1,0:T(8,128)S(1)}, u32[]{:S(2)}, u32[]{:S(2)}) collective-permute-start(f32[14,8,128]{2,1,0:T(8,128)S(1)} %shard_map.51.refs_3_), channel_id=1, source_target_pairs={{0,4},{1,5},{2,6},{3,7},{4,0},{5,1},{6,2},{7,3},{8,12},{9,13},{10,... | collective-permute-start | bytes 172040 | tf_op jit(solution)/shard_map/ppermute | solution.py:86
  17.5 1.2 %collective-permute-start.7 = (f32[14,8,128]{2,1,0:T(8,128)S(1)}, f32[14,8,128]{2,1,0:T(8,128)S(1)}, u32[]{:S(2)}, u32[]{:S(2)}) collective-permute-start(f32[14,8,128]{2,1,0:T(8,128)S(1)} %collective-permute-done.5.refs_6_), channel_id=1, source_target_pairs={{0,4},{1,5},{2,6},{3,7},{4,0},{5,1},{6,2},{7,3},{8,12},{9,13},{10,... | collective-permute-start | bytes 172040 | tf_op jit(solution)/shard_map/ppermute | solution.py:86
  17.5 1.4 %collective-permute-start.6 = (f32[14,8,128]{2,1,0:T(8,128)S(1)}, f32[14,8,128]{2,1,0:T(8,128)S(1)}, u32[]{:S(2)}, u32[]{:S(2)}) collective-permute-start(f32[14,8,128]{2,1,0:T(8,128)S(1)} %collective-permute-done.4.refs_5_), channel_id=1, source_target_pairs={{0,4},{1,5},{2,6},{3,7},{4,0},{5,1},{6,2},{7,3},{8,12},{9,13},{10,... | collective-permute-start | bytes 172040 | tf_op jit(solution)/shard_map/ppermute | solution.py:86

commit v6 on v5

--- a/solution.py
+++ b/solution.py
@@ -313,7 +313,11 @@
     pack_face(own, out_b, 0, jnp.logical_not(even))
 
 
-def strips_kernel(ends, z_a, z_b, strips, *, sizes):
+def merged(cx, cz):
+    return NF // (cz // (2 * HALO * cx)) // 2
+
+
+def strips_kernel(ends, z_a, z_b, strips, out_a, out_b, *, sizes, cx):
     blocks, cy, cz = ends.shape
     at_z = lax.axis_index("gz")
     even = at_z % 2 == 0
@@ -335,6 +339,22 @@
         own = ends[block]
         strips[block] = jnp.where(first_half, below, own)
         strips[blocks + block] = jnp.where(first_half, own, above)
+
+    wide = 2 * HALO * cx
+    pairs = merged(cx, cz)
+    even_x = lax.axis_index("gx") % 2 == 0
+    count = out_a.shape[0] // 2
+    upper = lane % wide >= wide // 2
+    for out, up in ((out_a, even_x), (out_b, jnp.logical_not(even_x))):
+        near = upper == up
+        shift = jnp.where(up, cz - wide // 2, wide // 2)
+        for side in range(2):
+            for pair in range(pairs):
+                one = strips[side * blocks + 2 * pair]
+                two = pltpu.roll(strips[side * blocks + 2 * pair + 1], shift, axis=1)
+                out[side * count + pair] = jnp.where(near, one, two)
+            for block in range(2 * pairs, blocks):
+                out[side * count + block - pairs] = strips[side * blocks + block]
 
 
 def steps_kernel(
@@ -415,15 +435,20 @@
         | ((lane >= 2 * wide) & (lane < 3 * wide) & has_right)
     )
     blocks = strips.shape[0] // 2
+    count = far_a.shape[0] // 2
+    pairs = merged(cx, cz)
     group = lane // wide
     for side in range(2):
         for block in range(blocks):
-            at = side * blocks + block
+            second = block < 2 * pairs and block % 2
+            at = side * count + (block // 2 if block < 2 * pairs else block - pairs)
             from_a = whole(far_a, far_a_y, at)
             from_b = whole(far_b, far_b_y, at)
             left = jnp.where(even_x, from_b, from_a)
-            mine = turn(whole(strips, strips_y, at), wide, 1)
-            right = turn(jnp.where(even_x, from_a, from_b), 2 * wide, 1)
+            right = jnp.where(even_x, from_a, from_b)
+            left = turn(left, wide // 2 if second else 0, 1)
+            right = turn(right, 2 * wide - (wide // 2 if second else 0), 1)
+            mine = turn(whole(strips, strips_y, side * blocks + block), wide, 1)
             for field in range(block * per, min((block + 1) * per, NV)):
                 spot = field % per
                 value = jnp.where(
@@ -514,7 +539,7 @@
         collide(first + x, [whole(cells, cells_y, member, x) for member in range(NP)])
         return carry
 
-    lax.fori_loop(0, cx, collide_own, 0, unroll=True)
+    lax.fori_loop(0, cx, collide_own, 0, unroll=2)
     for end in ends:
         collide(
             jnp.where(end[2] == 0, first - 1, last + 1),
@@ -552,7 +577,7 @@
         potential1[at] = jnp.where(fluid[at] == 1.0, add_up(values), 0.0)
         return carry
 
-    lax.fori_loop(0, cx + 4, stream, 0, unroll=True)
+    lax.fori_loop(0, cx + 4, stream, 0, unroll=2)
 
     totals = []
     crossed = {}
@@ -686,12 +711,14 @@
     x_b_y = beside(sizes, x_b)
 
     strip_blocks = 2 * end_blocks
-    strips = call(
-        lambda *refs: strips_kernel(*refs, sizes=sizes),
-        pltpu.VMEM((strip_blocks, cy, cz), f32), [vmem] * 3, near(ends, z_a, z_b),
+    far_shape = pltpu.VMEM((strip_blocks - 2 * merged(cx, cz), cy, cz), f32)
+    strips, far_a, far_b = call(
+        lambda *refs: strips_kernel(*refs, sizes=sizes, cx=cx),
+        (pltpu.VMEM((strip_blocks, cy, cz), f32), far_shape, far_shape),
+        [vmem] * 3, near(ends, z_a, z_b),
     )
     strips_y = beside(sizes, strips)
-    far_a, far_b = swap(sizes, "gx", strips, strips)
+    far_a, far_b = swap(sizes, "gx", far_a, far_b)
     far_a_y = beside(sizes, far_a)
     far_b_y = beside(sizes, far_b)
 

time: 22.2 us -> 29.7 us (1.34)
  the two profiles are of different devices: /device:TPU:0 before, /device:TPU:21 now
where the time goes in v6:
time: 29.7 us; the launch traced here: 29.6 us
  waiting for transfers between devices  12.9 us (43%)
  starting transfers between devices  11.5 us (39%)
  Pallas kernels  4.47 us (15%)
  between operations  0.66 us (2%)
    ppermute x6, starting transfers between devices, beside(): return lax.ppermute(cells, AXES, perm) if perm else cells  8.75 us
    ppermute x3, waiting for transfers between devices, swap(): got_a = lax.ppermute(send_a, AXES, perm_a) if perm_a else send_a  6.58 us
    ppermute x3, waiting for transfers between devices, swap(): got_b = lax.ppermute(send_b, AXES, perm_b) if perm_b else got_a  5.08 us
    pallas_call x4, Pallas kernels, call(): pl.pallas_call(kernel, out_shape=out_shape, in_specs=in_specs, out_specs=...  4.47 us
    ppermute x3, starting transfers between devices, swap(): got_a = lax.ppermute(send_a, AXES, perm_a) if perm_a else send_a  2.59 us
    ppermute x6, waiting for transfers between devices, beside(): return lax.ppermute(cells, AXES, perm) if perm else cells  1.23 us
  transfers between devices with their start and end apart: 12, of which 8 were waited for; matrix products, arithmetic and copies ran while one was open for 0% of the time, Pallas kernels for 1%

profile of v6, /device:TPU:21, one launch (start us, length us, event | category | flops | bytes accessed | tf_op | source)
XLA Modules:
  0.0 29.6 jit_solution(7125717988413747998)
XLA Ops:
  0.6 1.3 %shard_map.50 = (f32[26,4,8,128]{3,2,1,0:T(8,128)S(1)}, f32[27,4,8,128]{3,2,1,0:T(8,128)S(1)}, f32[7,8,128]{2,1,0:T(8,128)S(1)}, f32[4,8,128]{2,1,0:T(8,128)S(1)}, f32[4,8,128]{2,1,0:T(8,128)S(1)}) custom-call(f32[19,4,8,128]{3,2,1,0:T(8,128)} %flow.1, f32[7,4,8,128]{3,2,1,0:T(8,128)} %phase.1, s32[4,8,128]{2,1,0:T(8,128)} %mask.1), custom_call_target="tpu_custom_call" | custom-call | tf_op jit(solution)/shard_map/pallas_call | solution.py:678
  2.0 0.7 %collective-permute-start = (f32[27,4,8,128]{3,2,1,0:T(8,128)S(1)}, f32[27,4,8,128]{3,2,1,0:T(8,128)S(1)}, u32[]{:S(2)}, u32[]{:S(2)}) collective-permute-start(f32[27,4,8,128]{3,2,1,0:T(8,128)S(1)} %get-tuple-element.13.own.refs_1_), channel_id=1, source_target_pairs={{0,4},{1,5},{2,6},{3,7},{4,0},{5,1},{6,2},{7,3},{8,12},{9,13},{10,... | collective-permute-start | bytes 1327112 | tf_op jit(solution)/shard_map/ppermute | solution.py:86
  2.8 1.4 %collective-permute-start.8 = (f32[44,8,128]{2,1,0:T(8,128)S(1)}, f32[44,8,128]{2,1,0:T(8,128)S(1)}, u32[]{:S(2)}, u32[]{:S(2)}) collective-permute-start(f32[44,8,128]{2,1,0:T(8,128)S(1)} %get-tuple-element.20), channel_id=1, source_target_pairs={{0,8},{1,9},{2,10},{3,11},{4,12},{5,13},{6,14},{7,15},{8,0},{9,1},... | collective-permute-start | bytes 540680 | tf_op jit(solution)/shard_map/ppermute | solution.py:78
  4.1 0.0 collective-permute-start.9
  4.1 4.8 %collective-permute-done.8.refs_9_ = f32[44,8,128]{2,1,0:T(8,128)S(1)} collective-permute-done((f32[44,8,128]{2,1,0:T(8,128)S(1)}, f32[44,8,128]{2,1,0:T(8,128)S(1)}, u32[]{:S(2)}, u32[]{:S(2)}) %collective-permute-start.8) | collective-permute-done | bytes 180256 | tf_op jit(solution)/shard_map/ppermute | solution.py:78
  8.9 0.9 %collective-permute-start.10 = (f32[44,8,128]{2,1,0:T(8,128)S(1)}, f32[44,8,128]{2,1,0:T(8,128)S(1)}, u32[]{:S(2)}, u32[]{:S(2)}) collective-permute-start(f32[44,8,128]{2,1,0:T(8,128)S(1)} %collective-permute-done.8.refs_9_), channel_id=1, source_target_pairs={{0,4},{1,5},{2,6},{3,7},{4,0},{5,1},{6,2},{7,3},{8,12},{9,13},{10,... | collective-permute-start | bytes 540680 | tf_op jit(solution)/shard_map/ppermute | solution.py:86
  9.8 0.1 collective-permute-done.9.refs_10_
  9.9 1.2 %collective-permute-start.11 = (f32[44,8,128]{2,1,0:T(8,128)S(1)}, f32[44,8,128]{2,1,0:T(8,128)S(1)}, u32[]{:S(2)}, u32[]{:S(2)}) collective-permute-start(f32[44,8,128]{2,1,0:T(8,128)S(1)} %collective-permute-done.9.refs_10_), channel_id=1, source_target_pairs={{0,4},{1,5},{2,6},{3,7},{4,0},{5,1},{6,2},{7,3},{8,12},{9,13},{10,... | collective-permute-start | bytes 540680 | tf_op jit(solution)/shard_map/ppermute | solution.py:86
  11.1 1.2 %collective-permute-start.1 = (f32[4,8,128]{2,1,0:T(8,128)S(1)}, f32[4,8,128]{2,1,0:T(8,128)S(1)}, u32[]{:S(2)}, u32[]{:S(2)}) collective-permute-start(f32[4,8,128]{2,1,0:T(8,128)S(1)} %get-tuple-element.15), channel_id=1, source_target_pairs={{0,1},{1,0},{2,3},{3,2},{4,5},{5,4},{6,7},{7,6},{8,9},{9,8},{10,11... | collective-permute-start | bytes 49160 | tf_op jit(solution)/shard_map/ppermute | solution.py:78
  12.3 0.2 collective-permute-start.2
  12.5 1.2 %collective-permute-done.1.refs_1_ = f32[4,8,128]{2,1,0:T(8,128)S(1)} collective-permute-done((f32[4,8,128]{2,1,0:T(8,128)S(1)}, f32[4,8,128]{2,1,0:T(8,128)S(1)}, u32[]{:S(2)}, u32[]{:S(2)}) %collective-permute-start.1) | collective-permute-done | bytes 16416 | tf_op jit(solution)/shard_map/ppermute | solution.py:78
  13.7 2.1 %collective-permute-done.2.refs_2_ = f32[4,8,128]{2,1,0:T(8,128)S(1)} collective-permute-done((f32[4,8,128]{2,1,0:T(8,128)S(1)}, f32[4,8,128]{2,1,0:T(8,128)S(1)}, u32[]{:S(2)}, u32[]{:S(2)}) %collective-permute-start.2) | collective-permute-done | bytes 16416 | tf_op jit(solution)/shard_map/ppermute | solution.py:79
  15.8 0.1 shard_map.51
  15.9 0.0 collective-permute-start.4
  16.0 2.2 %collective-permute-start.3 = (f32[14,8,128]{2,1,0:T(8,128)S(1)}, f32[14,8,128]{2,1,0:T(8,128)S(1)}, u32[]{:S(2)}, u32[]{:S(2)}) collective-permute-start(f32[14,8,128]{2,1,0:T(8,128)S(1)} %get-tuple-element.17.refs_3_), channel_id=1, source_target_pairs={{0,4},{1,5},{2,6},{3,7},{4,0},{5,1},{6,2},{7,3},{8,12},{9,13},{10,... | collective-permute-start | bytes 172040 | tf_op jit(solution)/shard_map/ppermute | solution.py:86
  18.2 0.6 %collective-permute-done.4.refs_5_ = f32[10,8,128]{2,1,0:T(8,128)S(1)} collective-permute-done((f32[10,8,128]{2,1,0:T(8,128)S(1)}, f32[10,8,128]{2,1,0:T(8,128)S(1)}, u32[]{:S(2)}, u32[]{:S(2)}) %collective-permute-start.4) | collective-permute-done | bytes 40992 | tf_op jit(solution)/shard_map/ppermute | solution.py:78
  18.8 0.0 collective-permute-start.5
  18.8 2.8 %collective-permute-done.5.refs_6_ = f32[10,8,128]{2,1,0:T(8,128)S(1)} collective-permute-done((f32[10,8,128]{2,1,0:T(8,128)S(1)}, f32[10,8,128]{2,1,0:T(8,128)S(1)}, u32[]{:S(2)}, u32[]{:S(2)}) %collective-permute-start.5) | collective-permute-done | bytes 40992 | tf_op jit(solution)/shard_map/ppermute | solution.py:79
  21.7 3.7 %collective-permute-start.6 = (f32[10,8,128]{2,1,0:T(8,128)S(1)}, f32[10,8,128]{2,1,0:T(8,128)S(1)}, u32[]{:S(2)}, u32[]{:S(2)}) collective-permute-start(f32[10,8,128]{2,1,0:T(8,128)S(1)} %collective-permute-done.4.refs_5_), channel_id=1, source_target_pairs={{0,4},{1,5},{2,6},{3,7},{4,0},{5,1},{6,2},{7,3},{8,12},{9,13},{10,... | collective-permute-start | bytes 122888 | tf_op jit(solution)/shard_map/ppermute | solution.py:86
  25.4 0.0 collective-permute-done.3.refs_4_
  25.4 0.0 collective-permute-start.7
  25.4 0.9 %collective-permute-done.6.refs_7_ = f32[10,8,128]{2,1,0:T(8,128)S(1)} collective-permute-done((f32[10,8,128]{2,1,0:T(8,128)S(1)}, f32[10,8,128]{2,1,0:T(8,128)S(1)}, u32[]{:S(2)}, u32[]{:S(2)}) %collective-permute-start.6) | collective-permute-done | bytes 40992 | tf_op jit(solution)/shard_map/ppermute | solution.py:86
  26.3 0.4 %collective-permute-done.7.refs_8_ = f32[10,8,128]{2,1,0:T(8,128)S(1)} collective-permute-done((f32[10,8,128]{2,1,0:T(8,128)S(1)}, f32[10,8,128]{2,1,0:T(8,128)S(1)}, u32[]{:S(2)}, u32[]{:S(2)}) %collective-permute-start.7) | collective-permute-done | bytes 40992 | tf_op jit(solution)/shard_map/ppermute | solution.py:86
  26.6 0.0 collective-permute-done.10.refs_11_
  26.6 0.0 collective-permute-done.11.refs_12_
  26.6 0.0 collective-permute-done.refs_2_
  26.6 2.9 %shard_map.53 = (f32[19,4,8,128]{3,2,1,0:T(8,128)}, f32[7,4,8,128]{3,2,1,0:T(8,128)}) custom-call(f32[26,4,8,128]{3,2,1,0:T(8,128)S(1)} %get-tuple-element.12.refs_0_, f32[27,4,8,128]{3,2,1,0:T(8,128)S(1)} %get-tuple-element.13.own.refs_1_, f32[27,4,8,128]{3,2,1,0:T(8,128)S(1)} %collective-permute-done.refs_2_, f32[14,8,128]{2,1,0:T(8,128)S(1)} %get-tuple-element.17.refs_3_, ...), custom_call_target="tpu_custom_call" | custom-call | tf_op jit(solution)/shard_map/pallas_call | solution.py:678
  (1 shorter events, 0.0 us)
Async XLA Ops:
  2.0 24.6 %collective-permute-start = (f32[27,4,8,128]{3,2,1,0:T(8,128)S(1)}, f32[27,4,8,128]{3,2,1,0:T(8,128)S(1)}, u32[]{:S(2)}, u32[]{:S(2)}) collective-permute-start(f32[27,4,8,128]{3,2,1,0:T(8,128)S(1)} %get-tuple-element.13.own.refs_1_), channel_id=1, source_target_pairs={{0,4},{1,5},{2,6},{3,7},{4,0},{5,1},{6,2},{7,3},{8,12},{9,13},{10,... | collective-permute-start | bytes 1327112 | tf_op jit(solution)/shard_map/ppermute | solution.py:86
  2.8 6.1 %collective-permute-start.8 = (f32[44,8,128]{2,1,0:T(8,128)S(1)}, f32[44,8,128]{2,1,0:T(8,128)S(1)}, u32[]{:S(2)}, u32[]{:S(2)}) collective-permute-start(f32[44,8,128]{2,1,0:T(8,128)S(1)} %get-tuple-element.20), channel_id=1, source_target_pairs={{0,8},{1,9},{2,10},{3,11},{4,12},{5,13},{6,14},{7,15},{8,0},{9,1},... | collective-permute-start | bytes 540680 | tf_op jit(solution)/shard_map/ppermute | solution.py:78
  4.1 5.8 %collective-permute-start.9 = (f32[44,8,128]{2,1,0:T(8,128)S(1)}, f32[44,8,128]{2,1,0:T(8,128)S(1)}, u32[]{:S(2)}, u32[]{:S(2)}) collective-permute-start(f32[44,8,128]{2,1,0:T(8,128)S(1)} %get-tuple-element.21), channel_id=1, source_target_pairs={{0,4},{1,5},{2,6},{3,7},{4,0},{5,1},{6,2},{7,3},{8,16},{9,17},{10,... | collective-permute-start | bytes 540680 | tf_op jit(solution)/shard_map/ppermute | solution.py:79
  8.9 17.7 %collective-permute-start.10 = (f32[44,8,128]{2,1,0:T(8,128)S(1)}, f32[44,8,128]{2,1,0:T(8,128)S(1)}, u32[]{:S(2)}, u32[]{:S(2)}) collective-permute-start(f32[44,8,128]{2,1,0:T(8,128)S(1)} %collective-permute-done.8.refs_9_), channel_id=1, source_target_pairs={{0,4},{1,5},{2,6},{3,7},{4,0},{5,1},{6,2},{7,3},{8,12},{9,13},{10,... | collective-permute-start | bytes 540680 | tf_op jit(solution)/shard_map/ppermute | solution.py:86
  9.9 16.7 %collective-permute-start.11 = (f32[44,8,128]{2,1,0:T(8,128)S(1)}, f32[44,8,128]{2,1,0:T(8,128)S(1)}, u32[]{:S(2)}, u32[]{:S(2)}) collective-permute-start(f32[44,8,128]{2,1,0:T(8,128)S(1)} %collective-permute-done.9.refs_10_), channel_id=1, source_target_pairs={{0,4},{1,5},{2,6},{3,7},{4,0},{5,1},{6,2},{7,3},{8,12},{9,13},{10,... | collective-permute-start | bytes 540680 | tf_op jit(solution)/shard_map/ppermute | solution.py:86
  11.1 2.6 %collective-permute-start.1 = (f32[4,8,128]{2,1,0:T(8,128)S(1)}, f32[4,8,128]{2,1,0:T(8,128)S(1)}, u32[]{:S(2)}, u32[]{:S(2)}) collective-permute-start(f32[4,8,128]{2,1,0:T(8,128)S(1)} %get-tuple-element.15), channel_id=1, source_target_pairs={{0,1},{1,0},{2,3},{3,2},{4,5},{5,4},{6,7},{7,6},{8,9},{9,8},{10,11... | collective-permute-start | bytes 49160 | tf_op jit(solution)/shard_map/ppermute | solution.py:78
  12.3 3.5 %collective-permute-start.2 = (f32[4,8,128]{2,1,0:T(8,128)S(1)}, f32[4,8,128]{2,1,0:T(8,128)S(1)}, u32[]{:S(2)}, u32[]{:S(2)}) collective-permute-start(f32[4,8,128]{2,1,0:T(8,128)S(1)} %get-tuple-element.16), channel_id=1, source_target_pairs={{0,4},{1,2},{2,1},{3,7},{4,0},{5,6},{6,5},{7,3},{8,12},{9,10},{10,... | collective-permute-start | bytes 49160 | tf_op jit(solution)/shard_map/ppermute | solution.py:79
  15.9 2.9 %collective-permute-start.4 = (f32[10,8,128]{2,1,0:T(8,128)S(1)}, f32[10,8,128]{2,1,0:T(8,128)S(1)}, u32[]{:S(2)}, u32[]{:S(2)}) collective-permute-start(f32[10,8,128]{2,1,0:T(8,128)S(1)} %get-tuple-element.18), channel_id=1, source_target_pairs={{0,8},{1,9},{2,10},{3,11},{4,12},{5,13},{6,14},{7,15},{8,0},{9,1},... | collective-permute-start | bytes 122888 | tf_op jit(solution)/shard_map/ppermute | solution.py:78
  16.0 9.4 %collective-permute-start.3 = (f32[14,8,128]{2,1,0:T(8,128)S(1)}, f32[14,8,128]{2,1,0:T(8,128)S(1)}, u32[]{:S(2)}, u32[]{:S(2)}) collective-permute-start(f32[14,8,128]{2,1,0:T(8,128)S(1)} %get-tuple-element.17.refs_3_), channel_id=1, source_target_pairs={{0,4},{1,5},{2,6},{3,7},{4,0},{5,1},{6,2},{7,3},{8,12},{9,13},{10,... | collective-permute-start | bytes 172040 | tf_op jit(solution)/shard_map/ppermute | solution.py:86
  18.8 2.9 %collective-permute-start.5 = (f32[10,8,128]{2,1,0:T(8,128)S(1)}, f32[10,8,128]{2,1,0:T(8,128)S(1)}, u32[]{:S(2)}, u32[]{:S(2)}) collective-permute-start(f32[10,8,128]{2,1,0:T(8,128)S(1)} %get-tuple-element.19), channel_id=1, source_target_pairs={{0,4},{1,5},{2,6},{3,7},{4,0},{5,1},{6,2},{7,3},{8,16},{9,17},{10,... | collective-permute-start | bytes 122888 | tf_op jit(solution)/shard_map/ppermute | solution.py:79
  21.7 4.6 %collective-permute-start.6 = (f32[10,8,128]{2,1,0:T(8,128)S(1)}, f32[10,8,128]{2,1,0:T(8,128)S(1)}, u32[]{:S(2)}, u32[]{:S(2)}) collective-permute-start(f32[10,8,128]{2,1,0:T(8,128)S(1)} %collective-permute-done.4.refs_5_), channel_id=1, source_target_pairs={{0,4},{1,5},{2,6},{3,7},{4,0},{5,1},{6,2},{7,3},{8,12},{9,13},{10,... | collective-permute-start | bytes 122888 | tf_op jit(solution)/shard_map/ppermute | solution.py:86
  25.4 1.2 %collective-permute-start.7 = (f32[10,8,128]{2,1,0:T(8,128)S(1)}, f32[10,8,128]{2,1,0:T(8,128)S(1)}, u32[]{:S(2)}, u32[]{:S(2)}) collective-permute-start(f32[10,8,128]{2,1,0:T(8,128)S(1)} %collective-permute-done.5.refs_6_), channel_id=1, source_target_pairs={{0,4},{1,5},{2,6},{3,7},{4,0},{5,1},{6,2},{7,3},{8,12},{9,13},{10,... | collective-permute-start | bytes 122888 | tf_op jit(solution)/shard_map/ppermute | solution.py:86

commit v7 on v6

--- a/solution.py
+++ b/solution.py
@@ -377,6 +377,20 @@
     def whole(cells, cells_y, *at):
         return jnp.concatenate([cells[at], cells_y[at]], axis=0)
 
+    both = pl.ds(cy, rows)
+
+    def put(ref, at, value):
+        ref[(*at, both)] = value
+        ref[(*at, own_rows)] = value[cy:]
+
+    def rows_from(step, half):
+        if half == 0:
+            return pl.ds(cy - step, cy)
+        return pl.ds(1, cy) if step < 0 else pl.ds(rows - step, cy)
+
+    def take(ref, at, step):
+        return jnp.concatenate([ref[(*at, rows_from(step, half))] for half in (0, 1)], axis=0)
+
     lane = lax.broadcasted_iota(jnp.int32, (rows, cz), 1)
     row = lax.broadcasted_iota(jnp.int32, (rows, cz), 0)
     has_left = at_x > 0
@@ -401,7 +415,7 @@
         ok = (whole(cells, cells_y, NP, x) == 1.0) & row_ok
         fluid[first + x] = ok.astype(jnp.float32)
         total = add_up([whole(cells, cells_y, NF + member, x) for member in range(NG)])
-        potential[first + x] = jnp.where(ok, total, 0.0)
+        put(potential, (first + x,), jnp.where(ok, total, 0.0))
     for end in ends:
         side = end[2]
         for layer in range(N_FACE):
@@ -411,7 +425,7 @@
         ok = side_ok & (whole_face(end, NP) == 1.0)
         total = add_up([whole_face(end, NF + member) for member in range(NG)])
         fluid[at] = ok.astype(jnp.float32)
-        potential[at] = jnp.where(ok, total, 0.0)
+        put(potential, (at,), jnp.where(ok, total, 0.0))
     for side in range(2):
         side_ok = row_ok & has[side]
         for depth in range(2, HALO + 1):
@@ -424,7 +438,7 @@
             if depth < HALO:
                 ok = ok & (face[side, L_MASK + depth - 2] == 1.0)
                 fluid[at] = ok.astype(jnp.float32)
-            potential[at] = jnp.where(ok, total, 0.0)
+            put(potential, (at,), jnp.where(ok, total, 0.0))
 
     cols = 2 * HALO
     wide = cols * cx
@@ -470,8 +484,7 @@
     def push_strip(member, value, ok):
         move = VEL[member]
         value = jnp.where(ok, value, ROCK)
-        value = turn(value, move[0] * cols + move[2], 1)
-        return turn(value, move[1], 0)
+        return turn(value, move[0] * cols + move[2], 1)
 
     from_low = lane % cols == HALO
     fills = {}
@@ -486,13 +499,13 @@
         return pltpu.roll(values, (2 * cz - (at * cols + HALO)) % cz, axis=1)
 
     def main_grads(source, fill, at):
-        here = source[at]
+        here = source[at, both]
         fill = to_ends(fill, at)
         down = jnp.where(lane == 0, fill, turn(here, 1, 1))
         up = jnp.where(lane == cz - 1, fill, turn(here, -1, 1))
         return (
-            0.5 * (source[at + 1] - source[at - 1]),
-            0.5 * (turn(here, -1, 0) - turn(here, 1, 0)),
+            0.5 * (source[at + 1, both] - source[at - 1, both]),
+            0.5 * (take(source, (at,), -1) - take(source, (at,), 1)),
             0.5 * (up - down),
         )
 
@@ -508,8 +521,12 @@
         return jnp.where(lane[:size] == edge, memo[number], turn(value, move[2], 1))
 
     def push_main(member, value, ok, at, memo):
-        value = turn(jnp.where(ok, value, ROCK), VEL[member][1], 0)
-        return push_z(member, value, fill_moved, at, pl.ds(0, rows), memo)
+        value = jnp.where(ok, value, ROCK)
+        value = push_z(member, value, fill_moved, at, pl.ds(0, rows), memo)
+        if VEL[member][1]:
+            put(moved, (member, at), value)
+        else:
+            moved[member, at, both] = value
 
     totals = []
     for side in range(2):
@@ -520,20 +537,22 @@
         done = relax_rest(total, strip_grads(total), dict(enumerate(values)))
         for member in range(NP):
             strip_stayed[side, member] = done[member]
-            strip_moved[side, member] = push_strip(member, done[member], ok)
+            put(strip_moved, (side, member), push_strip(member, done[member], ok))
 
     fill_phase = jnp.where(from_low, totals[0], totals[1])
     for number, low, high in sorted(set(fills.values())):
-        fill_moved[number] = jnp.where(from_low, strip_moved[0, low], strip_moved[1, high])
+        fill_moved[number] = jnp.where(
+            from_low, strip_moved[0, low, both], strip_moved[1, high, both]
+        )
 
     def collide(at, values):
         ok = fluid[at] == 1.0
         grads = main_grads(potential, fill_phase, at)
-        done = relax_rest(potential[at], grads, dict(enumerate(values)))
+        done = relax_rest(potential[at, both], grads, dict(enumerate(values)))
         memo = {}
         for member in range(NP):
             stayed[member, at] = done[member]
-            moved[member, at] = push_main(member, done[member], ok, at, memo)
+            push_main(member, done[member], ok, at, memo)
 
     def collide_own(x, carry):
         collide(first + x, [whole(cells, cells_y, member, x) for member in range(NP)])
@@ -549,32 +568,38 @@
         at = at_depth(side, 2)
         members = {m + side: face[side, L_F2 + slot] for slot, m in enumerate(IN_F)}
         members.update({NF + m: face[side, L_G2 + m] for m in range(NG)})
-        done = relax_rest(potential[at], main_grads(potential, fill_phase, at), members)
+        done = relax_rest(potential[at, both], main_grads(potential, fill_phase, at), members)
         ok = fluid[at] == 1.0
         memo = {}
         for member in done:
             stayed[member, at] = done[member]
-            moved[member, at] = push_main(member, done[member], ok, at, memo)
+            push_main(member, done[member], ok, at, memo)
         at = at_depth(side, 3)
         member = NF + IN_G + side
         done = relax_rest(
-            potential[at], main_grads(potential, fill_phase, at), {member: face[side, L_G3]}
+            potential[at, both], main_grads(potential, fill_phase, at),
+            {member: face[side, L_G3]},
         )
         ok = fluid[at] == 1.0
-        moved[member, at] = push_main(member, done[member], ok, at, {})
-
-    def pull(member, at, part):
+        push_main(member, done[member], ok, at, {})
+
+    def pull(member, at, half):
+        part = pl.ds(half * cy, cy)
         if VEL[member] == (0, 0, 0):
             return stayed[member, at, part]
-        value = moved[member, at - VEL[member][0], part]
+        move = VEL[member]
+        value = moved[member, at - move[0], rows_from(move[1], half)]
         return jnp.where(value == ROCK, stayed[OPP[member], at, part], value)
 
     def stream(j, carry):
         at = first - 2 + j
-        values = [pull(NF + member, at, pl.ds(0, rows)) for member in range(NG)]
+        values = [
+            jnp.concatenate([pull(NF + member, at, half) for half in (0, 1)], axis=0)
+            for member in range(NG)
+        ]
         for member in range(NG):
             phase_pops[member, at] = values[member]
-        potential1[at] = jnp.where(fluid[at] == 1.0, add_up(values), 0.0)
+        put(potential1, (at,), jnp.where(fluid[at] == 1.0, add_up(values), 0.0))
         return carry
 
     lax.fori_loop(0, cx + 4, stream, 0, unroll=2)
@@ -585,7 +610,7 @@
         ok = strip_fluid[side] == 1.0
         values = []
         for member in range(NP):
-            value = strip_moved[side, member]
+            value = take(strip_moved, (side, member), VEL[member][1])
             back = strip_stayed[side, OPP[member]]
             values.append(jnp.where(value == ROCK, back, value))
         total = jnp.where(ok, add_up(values[NF:]), 0.0)
@@ -605,28 +630,30 @@
         halves = []
         for half in range(2):
             part = pl.ds(half * cy, cy)
-            values = [pull(member, at, part) for member in range(NF)]
+            values = [pull(member, at, half) for member in range(NF)]
             values += [phase_pops[member, at, part] for member in range(NG)]
             rho, mom = moments(values)
             members = [m for m in wanted if half == 0 or VEL[m][1] != 0]
             done = relax(
-                rho, mom, potential1[at, part],
+                rho, mom, potential1[at, pl.ds((1 + half) * cy, cy)],
                 [g[half * cy : (half + 1) * cy] for g in grads],
                 {m: values[m] for m in members},
             )
             halves.append((done, fluid[at, part] == 1.0))
         (done, ok), (done_y, ok_y) = halves
-        memo = {}
+        memo, memo_y = {}, {}
         for member in wanted:
             if keep:
                 stayed1[member, at] = done[member]
-            step_y = VEL[member][1]
-            value = turn(jnp.where(ok, done[member], ROCK), step_y, 0)
-            if step_y:
-                value_y = turn(jnp.where(ok_y, done_y[member], ROCK), step_y, 0)
-                edge = 0 if step_y > 0 else cy - 1
-                value = jnp.where(row[:cy] == edge, value_y, value)
-            moved1[member, at] = push_z(member, value, fill_moved1, at, own_rows, memo)
+            value = jnp.where(ok, done[member], ROCK)
+            middle = pl.ds(cy, cy)
+            moved1[member, at, middle] = push_z(member, value, fill_moved1, at, own_rows, memo)
+            if VEL[member][1]:
+                beyond = pl.ds(0, cy) if VEL[member][1] > 0 else pl.ds(rows, cy)
+                value = jnp.where(ok_y, done_y[member], ROCK)
+                moved1[member, at, beyond] = push_z(
+                    member, value, fill_moved1, at, pl.ds(cy, cy), memo_y
+                )
 
     def outputs(x):
         return (
@@ -645,7 +672,8 @@
             if VEL[member] == (0, 0, 0):
                 value = stayed1[member, at]
             else:
-                value = moved1[member, at - VEL[member][0]]
+                move = VEL[member]
+                value = moved1[member, at - move[0], pl.ds(cy - move[1], cy)]
                 value = jnp.where(value == ROCK, stayed1[OPP[member], at], value)
             result[member, x] = jnp.where(ok, value, own[member, x])
         for one in outputs(x):
@@ -727,6 +755,9 @@
     def block(*lead):
         return pltpu.VMEM((*lead, rows, cz), f32)
 
+    def tall(*lead):
+        return pltpu.VMEM((*lead, rows + cy, cz), f32)
+
     return call(
         lambda *refs: steps_kernel(*refs, sizes=sizes),
         (
@@ -741,18 +772,18 @@
         [
             block(2, N_FACE),
             block(deep),
-            block(deep),
+            tall(deep),
             block(2, NP),
             block(2),
             block(6),
             block(6),
+            tall(NP, deep),
             block(NP, deep),
-            block(NP, deep),
-            block(2, NP),
+            tall(2, NP),
             block(2, NP),
             block(NG, deep),
-            block(deep),
-            pltpu.VMEM((NP, deep, cy, cz), f32),
+            tall(deep),
+            tall(NP, deep),
             pltpu.VMEM((NP, deep, cy, cz), f32),
             pltpu.VMEM((NP, cx, cy, cz), f32),
             pltpu.SemaphoreType.DMA((2, cx)),

time: 29.7 us -> 29.7 us (level)
  no operation moved by 1% of the time
where the time goes in v7:
time: 29.7 us; the launch traced here: 29.6 us
  waiting for transfers between devices  12.9 us (43%)
  starting transfers between devices  11.5 us (39%)
  Pallas kernels  4.47 us (15%)
  between operations  0.66 us (2%)
    ppermute x6, starting transfers between devices, beside(): return lax.ppermute(cells, AXES, perm) if perm else cells  8.75 us
    ppermute x3, waiting for transfers between devices, swap(): got_a = lax.ppermute(send_a, AXES, perm_a) if perm_a else send_a  6.58 us
    ppermute x3, waiting for transfers between devices, swap(): got_b = lax.ppermute(send_b, AXES, perm_b) if perm_b else got_a  5.08 us
    pallas_call x4, Pallas kernels, call(): pl.pallas_call(kernel, out_shape=out_shape, in_specs=in_specs, out_specs=...  4.47 us
    ppermute x3, starting transfers between devices, swap(): got_a = lax.ppermute(send_a, AXES, perm_a) if perm_a else send_a  2.59 us
    ppermute x6, waiting for transfers between devices, beside(): return lax.ppermute(cells, AXES, perm) if perm else cells  1.23 us
  transfers between devices with their start and end apart: 12, of which 8 were waited for; matrix products, arithmetic and copies ran while one was open for 0% of the time, Pallas kernels for 1%

profile of v7, /device:TPU:21, one launch (start us, length us, event | category | flops | bytes accessed | tf_op | source)
XLA Modules:
  0.0 29.6 jit_solution(1099854833134671186)
XLA Ops:
  0.6 1.3 %shard_map.50 = (f32[26,4,8,128]{3,2,1,0:T(8,128)S(1)}, f32[27,4,8,128]{3,2,1,0:T(8,128)S(1)}, f32[7,8,128]{2,1,0:T(8,128)S(1)}, f32[4,8,128]{2,1,0:T(8,128)S(1)}, f32[4,8,128]{2,1,0:T(8,128)S(1)}) custom-call(f32[19,4,8,128]{3,2,1,0:T(8,128)} %flow.1, f32[7,4,8,128]{3,2,1,0:T(8,128)} %phase.1, s32[4,8,128]{2,1,0:T(8,128)} %mask.1), custom_call_target="tpu_custom_call" | custom-call | tf_op jit(solution)/shard_map/pallas_call | solution.py:706
  2.0 0.7 %collective-permute-start = (f32[27,4,8,128]{3,2,1,0:T(8,128)S(1)}, f32[27,4,8,128]{3,2,1,0:T(8,128)S(1)}, u32[]{:S(2)}, u32[]{:S(2)}) collective-permute-start(f32[27,4,8,128]{3,2,1,0:T(8,128)S(1)} %get-tuple-element.13.own.refs_1_), channel_id=1, source_target_pairs={{0,4},{1,5},{2,6},{3,7},{4,0},{5,1},{6,2},{7,3},{8,12},{9,13},{10,... | collective-permute-start | bytes 1327112 | tf_op jit(solution)/shard_map/ppermute | solution.py:86
  2.8 1.4 %collective-permute-start.8 = (f32[44,8,128]{2,1,0:T(8,128)S(1)}, f32[44,8,128]{2,1,0:T(8,128)S(1)}, u32[]{:S(2)}, u32[]{:S(2)}) collective-permute-start(f32[44,8,128]{2,1,0:T(8,128)S(1)} %get-tuple-element.20), channel_id=1, source_target_pairs={{0,8},{1,9},{2,10},{3,11},{4,12},{5,13},{6,14},{7,15},{8,0},{9,1},... | collective-permute-start | bytes 540680 | tf_op jit(solution)/shard_map/ppermute | solution.py:78
  4.1 0.0 collective-permute-start.9
  4.1 4.8 %collective-permute-done.8.refs_9_ = f32[44,8,128]{2,1,0:T(8,128)S(1)} collective-permute-done((f32[44,8,128]{2,1,0:T(8,128)S(1)}, f32[44,8,128]{2,1,0:T(8,128)S(1)}, u32[]{:S(2)}, u32[]{:S(2)}) %collective-permute-start.8) | collective-permute-done | bytes 180256 | tf_op jit(solution)/shard_map/ppermute | solution.py:78
  8.9 0.9 %collective-permute-start.10 = (f32[44,8,128]{2,1,0:T(8,128)S(1)}, f32[44,8,128]{2,1,0:T(8,128)S(1)}, u32[]{:S(2)}, u32[]{:S(2)}) collective-permute-start(f32[44,8,128]{2,1,0:T(8,128)S(1)} %collective-permute-done.8.refs_9_), channel_id=1, source_target_pairs={{0,4},{1,5},{2,6},{3,7},{4,0},{5,1},{6,2},{7,3},{8,12},{9,13},{10,... | collective-permute-start | bytes 540680 | tf_op jit(solution)/shard_map/ppermute | solution.py:86
  9.8 0.1 collective-permute-done.9.refs_10_
  9.9 1.2 %collective-permute-start.11 = (f32[44,8,128]{2,1,0:T(8,128)S(1)}, f32[44,8,128]{2,1,0:T(8,128)S(1)}, u32[]{:S(2)}, u32[]{:S(2)}) collective-permute-start(f32[44,8,128]{2,1,0:T(8,128)S(1)} %collective-permute-done.9.refs_10_), channel_id=1, source_target_pairs={{0,4},{1,5},{2,6},{3,7},{4,0},{5,1},{6,2},{7,3},{8,12},{9,13},{10,... | collective-permute-start | bytes 540680 | tf_op jit(solution)/shard_map/ppermute | solution.py:86
  11.1 1.2 %collective-permute-start.1 = (f32[4,8,128]{2,1,0:T(8,128)S(1)}, f32[4,8,128]{2,1,0:T(8,128)S(1)}, u32[]{:S(2)}, u32[]{:S(2)}) collective-permute-start(f32[4,8,128]{2,1,0:T(8,128)S(1)} %get-tuple-element.15), channel_id=1, source_target_pairs={{0,1},{1,0},{2,3},{3,2},{4,5},{5,4},{6,7},{7,6},{8,9},{9,8},{10,11... | collective-permute-start | bytes 49160 | tf_op jit(solution)/shard_map/ppermute | solution.py:78
  12.3 0.2 collective-permute-start.2
  12.5 1.2 %collective-permute-done.1.refs_1_ = f32[4,8,128]{2,1,0:T(8,128)S(1)} collective-permute-done((f32[4,8,128]{2,1,0:T(8,128)S(1)}, f32[4,8,128]{2,1,0:T(8,128)S(1)}, u32[]{:S(2)}, u32[]{:S(2)}) %collective-permute-start.1) | collective-permute-done | bytes 16416 | tf_op jit(solution)/shard_map/ppermute | solution.py:78
  13.7 2.1 %collective-permute-done.2.refs_2_ = f32[4,8,128]{2,1,0:T(8,128)S(1)} collective-permute-done((f32[4,8,128]{2,1,0:T(8,128)S(1)}, f32[4,8,128]{2,1,0:T(8,128)S(1)}, u32[]{:S(2)}, u32[]{:S(2)}) %collective-permute-start.2) | collective-permute-done | bytes 16416 | tf_op jit(solution)/shard_map/ppermute | solution.py:79
  15.8 0.1 shard_map.51
  15.9 0.0 collective-permute-start.4
  16.0 2.2 %collective-permute-start.3 = (f32[14,8,128]{2,1,0:T(8,128)S(1)}, f32[14,8,128]{2,1,0:T(8,128)S(1)}, u32[]{:S(2)}, u32[]{:S(2)}) collective-permute-start(f32[14,8,128]{2,1,0:T(8,128)S(1)} %get-tuple-element.17.refs_3_), channel_id=1, source_target_pairs={{0,4},{1,5},{2,6},{3,7},{4,0},{5,1},{6,2},{7,3},{8,12},{9,13},{10,... | collective-permute-start | bytes 172040 | tf_op jit(solution)/shard_map/ppermute | solution.py:86
  18.2 0.6 %collective-permute-done.4.refs_5_ = f32[10,8,128]{2,1,0:T(8,128)S(1)} collective-permute-done((f32[10,8,128]{2,1,0:T(8,128)S(1)}, f32[10,8,128]{2,1,0:T(8,128)S(1)}, u32[]{:S(2)}, u32[]{:S(2)}) %collective-permute-start.4) | collective-permute-done | bytes 40992 | tf_op jit(solution)/shard_map/ppermute | solution.py:78
  18.8 0.0 collective-permute-start.5
  18.8 2.8 %collective-permute-done.5.refs_6_ = f32[10,8,128]{2,1,0:T(8,128)S(1)} collective-permute-done((f32[10,8,128]{2,1,0:T(8,128)S(1)}, f32[10,8,128]{2,1,0:T(8,128)S(1)}, u32[]{:S(2)}, u32[]{:S(2)}) %collective-permute-start.5) | collective-permute-done | bytes 40992 | tf_op jit(solution)/shard_map/ppermute | solution.py:79
  21.7 3.7 %collective-permute-start.6 = (f32[10,8,128]{2,1,0:T(8,128)S(1)}, f32[10,8,128]{2,1,0:T(8,128)S(1)}, u32[]{:S(2)}, u32[]{:S(2)}) collective-permute-start(f32[10,8,128]{2,1,0:T(8,128)S(1)} %collective-permute-done.4.refs_5_), channel_id=1, source_target_pairs={{0,4},{1,5},{2,6},{3,7},{4,0},{5,1},{6,2},{7,3},{8,12},{9,13},{10,... | collective-permute-start | bytes 122888 | tf_op jit(solution)/shard_map/ppermute | solution.py:86
  25.4 0.0 collective-permute-done.3.refs_4_
  25.4 0.0 collective-permute-start.7
  25.4 0.9 %collective-permute-done.6.refs_7_ = f32[10,8,128]{2,1,0:T(8,128)S(1)} collective-permute-done((f32[10,8,128]{2,1,0:T(8,128)S(1)}, f32[10,8,128]{2,1,0:T(8,128)S(1)}, u32[]{:S(2)}, u32[]{:S(2)}) %collective-permute-start.6) | collective-permute-done | bytes 40992 | tf_op jit(solution)/shard_map/ppermute | solution.py:86
  26.3 0.4 %collective-permute-done.7.refs_8_ = f32[10,8,128]{2,1,0:T(8,128)S(1)} collective-permute-done((f32[10,8,128]{2,1,0:T(8,128)S(1)}, f32[10,8,128]{2,1,0:T(8,128)S(1)}, u32[]{:S(2)}, u32[]{:S(2)}) %collective-permute-start.7) | collective-permute-done | bytes 40992 | tf_op jit(solution)/shard_map/ppermute | solution.py:86
  26.6 0.0 collective-permute-done.10.refs_11_
  26.6 0.0 collective-permute-done.11.refs_12_
  26.6 0.0 collective-permute-done.refs_2_
  26.6 2.9 %shard_map.53 = (f32[19,4,8,128]{3,2,1,0:T(8,128)}, f32[7,4,8,128]{3,2,1,0:T(8,128)}) custom-call(f32[26,4,8,128]{3,2,1,0:T(8,128)S(1)} %get-tuple-element.12.refs_0_, f32[27,4,8,128]{3,2,1,0:T(8,128)S(1)} %get-tuple-element.13.own.refs_1_, f32[27,4,8,128]{3,2,1,0:T(8,128)S(1)} %collective-permute-done.refs_2_, f32[14,8,128]{2,1,0:T(8,128)S(1)} %get-tuple-element.17.refs_3_, ...), custom_call_target="tpu_custom_call" | custom-call | tf_op jit(solution)/shard_map/pallas_call | solution.py:706
  (1 shorter events, 0.0 us)
Async XLA Ops:
  2.0 24.6 %collective-permute-start = (f32[27,4,8,128]{3,2,1,0:T(8,128)S(1)}, f32[27,4,8,128]{3,2,1,0:T(8,128)S(1)}, u32[]{:S(2)}, u32[]{:S(2)}) collective-permute-start(f32[27,4,8,128]{3,2,1,0:T(8,128)S(1)} %get-tuple-element.13.own.refs_1_), channel_id=1, source_target_pairs={{0,4},{1,5},{2,6},{3,7},{4,0},{5,1},{6,2},{7,3},{8,12},{9,13},{10,... | collective-permute-start | bytes 1327112 | tf_op jit(solution)/shard_map/ppermute | solution.py:86
  2.8 6.1 %collective-permute-start.8 = (f32[44,8,128]{2,1,0:T(8,128)S(1)}, f32[44,8,128]{2,1,0:T(8,128)S(1)}, u32[]{:S(2)}, u32[]{:S(2)}) collective-permute-start(f32[44,8,128]{2,1,0:T(8,128)S(1)} %get-tuple-element.20), channel_id=1, source_target_pairs={{0,8},{1,9},{2,10},{3,11},{4,12},{5,13},{6,14},{7,15},{8,0},{9,1},... | collective-permute-start | bytes 540680 | tf_op jit(solution)/shard_map/ppermute | solution.py:78
  4.1 5.8 %collective-permute-start.9 = (f32[44,8,128]{2,1,0:T(8,128)S(1)}, f32[44,8,128]{2,1,0:T(8,128)S(1)}, u32[]{:S(2)}, u32[]{:S(2)}) collective-permute-start(f32[44,8,128]{2,1,0:T(8,128)S(1)} %get-tuple-element.21), channel_id=1, source_target_pairs={{0,4},{1,5},{2,6},{3,7},{4,0},{5,1},{6,2},{7,3},{8,16},{9,17},{10,... | collective-permute-start | bytes 540680 | tf_op jit(solution)/shard_map/ppermute | solution.py:79
  8.9 17.7 %collective-permute-start.10 = (f32[44,8,128]{2,1,0:T(8,128)S(1)}, f32[44,8,128]{2,1,0:T(8,128)S(1)}, u32[]{:S(2)}, u32[]{:S(2)}) collective-permute-start(f32[44,8,128]{2,1,0:T(8,128)S(1)} %collective-permute-done.8.refs_9_), channel_id=1, source_target_pairs={{0,4},{1,5},{2,6},{3,7},{4,0},{5,1},{6,2},{7,3},{8,12},{9,13},{10,... | collective-permute-start | bytes 540680 | tf_op jit(solution)/shard_map/ppermute | solution.py:86
  9.9 16.7 %collective-permute-start.11 = (f32[44,8,128]{2,1,0:T(8,128)S(1)}, f32[44,8,128]{2,1,0:T(8,128)S(1)}, u32[]{:S(2)}, u32[]{:S(2)}) collective-permute-start(f32[44,8,128]{2,1,0:T(8,128)S(1)} %collective-permute-done.9.refs_10_), channel_id=1, source_target_pairs={{0,4},{1,5},{2,6},{3,7},{4,0},{5,1},{6,2},{7,3},{8,12},{9,13},{10,... | collective-permute-start | bytes 540680 | tf_op jit(solution)/shard_map/ppermute | solution.py:86
  11.1 2.6 %collective-permute-start.1 = (f32[4,8,128]{2,1,0:T(8,128)S(1)}, f32[4,8,128]{2,1,0:T(8,128)S(1)}, u32[]{:S(2)}, u32[]{:S(2)}) collective-permute-start(f32[4,8,128]{2,1,0:T(8,128)S(1)} %get-tuple-element.15), channel_id=1, source_target_pairs={{0,1},{1,0},{2,3},{3,2},{4,5},{5,4},{6,7},{7,6},{8,9},{9,8},{10,11... | collective-permute-start | bytes 49160 | tf_op jit(solution)/shard_map/ppermute | solution.py:78
  12.3 3.5 %collective-permute-start.2 = (f32[4,8,128]{2,1,0:T(8,128)S(1)}, f32[4,8,128]{2,1,0:T(8,128)S(1)}, u32[]{:S(2)}, u32[]{:S(2)}) collective-permute-start(f32[4,8,128]{2,1,0:T(8,128)S(1)} %get-tuple-element.16), channel_id=1, source_target_pairs={{0,4},{1,2},{2,1},{3,7},{4,0},{5,6},{6,5},{7,3},{8,12},{9,10},{10,... | collective-permute-start | bytes 49160 | tf_op jit(solution)/shard_map/ppermute | solution.py:79
  15.9 2.9 %collective-permute-start.4 = (f32[10,8,128]{2,1,0:T(8,128)S(1)}, f32[10,8,128]{2,1,0:T(8,128)S(1)}, u32[]{:S(2)}, u32[]{:S(2)}) collective-permute-start(f32[10,8,128]{2,1,0:T(8,128)S(1)} %get-tuple-element.18), channel_id=1, source_target_pairs={{0,8},{1,9},{2,10},{3,11},{4,12},{5,13},{6,14},{7,15},{8,0},{9,1},... | collective-permute-start | bytes 122888 | tf_op jit(solution)/shard_map/ppermute | solution.py:78
  16.0 9.4 %collective-permute-start.3 = (f32[14,8,128]{2,1,0:T(8,128)S(1)}, f32[14,8,128]{2,1,0:T(8,128)S(1)}, u32[]{:S(2)}, u32[]{:S(2)}) collective-permute-start(f32[14,8,128]{2,1,0:T(8,128)S(1)} %get-tuple-element.17.refs_3_), channel_id=1, source_target_pairs={{0,4},{1,5},{2,6},{3,7},{4,0},{5,1},{6,2},{7,3},{8,12},{9,13},{10,... | collective-permute-start | bytes 172040 | tf_op jit(solution)/shard_map/ppermute | solution.py:86
  18.8 2.9 %collective-permute-start.5 = (f32[10,8,128]{2,1,0:T(8,128)S(1)}, f32[10,8,128]{2,1,0:T(8,128)S(1)}, u32[]{:S(2)}, u32[]{:S(2)}) collective-permute-start(f32[10,8,128]{2,1,0:T(8,128)S(1)} %get-tuple-element.19), channel_id=1, source_target_pairs={{0,4},{1,5},{2,6},{3,7},{4,0},{5,1},{6,2},{7,3},{8,16},{9,17},{10,... | collective-permute-start | bytes 122888 | tf_op jit(solution)/shard_map/ppermute | solution.py:79
  21.7 4.6 %collective-permute-start.6 = (f32[10,8,128]{2,1,0:T(8,128)S(1)}, f32[10,8,128]{2,1,0:T(8,128)S(1)}, u32[]{:S(2)}, u32[]{:S(2)}) collective-permute-start(f32[10,8,128]{2,1,0:T(8,128)S(1)} %collective-permute-done.4.refs_5_), channel_id=1, source_target_pairs={{0,4},{1,5},{2,6},{3,7},{4,0},{5,1},{6,2},{7,3},{8,12},{9,13},{10,... | collective-permute-start | bytes 122888 | tf_op jit(solution)/shard_map/ppermute | solution.py:86
  25.4 1.2 %collective-permute-start.7 = (f32[10,8,128]{2,1,0:T(8,128)S(1)}, f32[10,8,128]{2,1,0:T(8,128)S(1)}, u32[]{:S(2)}, u32[]{:S(2)}) collective-permute-start(f32[10,8,128]{2,1,0:T(8,128)S(1)} %collective-permute-done.5.refs_6_), channel_id=1, source_target_pairs={{0,4},{1,5},{2,6},{3,7},{4,0},{5,1},{6,2},{7,3},{8,12},{9,13},{10,... | collective-permute-start | bytes 122888 | tf_op jit(solution)/shard_map/ppermute | solution.py:86
